TPU v7x, 32 devices: a whole 2x2x4 slice. The times are simulated.
32 devices in a mesh: fsdp: 16 (over z, x, core), sp: 2 (over y).
Axes of the slice: x: 2, y: 2, z: 4, core: 2. Of those that a mesh axis runs over, the one named last changes fastest.
Arguments:
- patches: float32 [16, 1024, 6144], P('fsdp', 'sp'), may hold values from -6 to 6
- segments: int32 [16, 1024], P('fsdp'), may hold values from 0 to 7, never falling along the last dimension, each value on 1 to 512 neighbouring positions
- w_in: float32 [6144, 768], P('fsdp'), may hold values from -0.078125 to 0.078125
- norm1_gain: float32 [768], P('fsdp'), may hold values from 0.5 to 1.5
- norm1_bias: float32 [768], P('fsdp'), may hold values from -1 to 1
- w_qkv: float32 [768, 2304], P('fsdp'), may hold values from -0.21875 to 0.21875
- w_out: float32 [768, 768], P('fsdp'), may hold values from -0.625 to 0.625
- norm2_gain: float32 [768], P('fsdp'), may hold values from 0.5 to 1.5
- norm2_bias: float32 [768], P('fsdp'), may hold values from -1 to 1
- w_up: float32 [768, 3072], P('fsdp'), may hold values from -0.21875 to 0.21875
- w_down: float32 [3072, 768], P('fsdp'), may hold values from -0.109375 to 0.109375
- cotangent: float32 [16, 1024, 768], P('fsdp', 'sp'), may hold values from -6 to 6
Outputs:
- block_out: float32 [16, 1024, 768], P('fsdp', 'sp')
- grad_patches: float32 [16, 1024, 6144], P('fsdp', 'sp')
- grad_w_in: float32 [6144, 768], P('fsdp')
- grad_norm1_gain: float32 [768], P('fsdp')
- grad_norm1_bias: float32 [768], P('fsdp')
- grad_w_qkv: float32 [768, 2304], P('fsdp')
- grad_w_out: float32 [768, 768], P('fsdp')
- grad_norm2_gain: float32 [768], P('fsdp')
- grad_norm2_bias: float32 [768], P('fsdp')
- grad_w_up: float32 [768, 3072], P('fsdp')
- grad_w_down: float32 [3072, 768], P('fsdp')
Inputs may be any that keep to these rules, and one draw needn't show every extreme that they name: `segments`: along each sequence the document numbers never fall; each of the 8 documents has at least one row and at most 512 rows, and some document has exactly 512 rows.
All inputs are finite; a program needn't handle non-finite values.
Results may differ from a plain program's by a relative error of at most 0.0003.
Values sent between devices are 32-bit elements; how exact they have to be, the bound alone decides.
A program may use at most 256 MiB of HBM per device.

v0:
```python
import jax
import jax.numpy as jnp
from jax import lax
from jax.sharding import PartitionSpec as P

HEADS = 12


EPSILON = 1e-05


def matmul(left_side, right_side):
    return jnp.dot(
        left_side, right_side, precision=lax.Precision.HIGHEST, preferred_element_type=jnp.float32
    )


def matmul_tn(left_side, right_side):
    return lax.dot_general(
        left_side,
        right_side,
        (((0,), (0,)), ((), ())),
        precision=lax.Precision.HIGHEST,
        preferred_element_type=jnp.float32,
    )


def matmul_nt(left_side, right_side):
    return lax.dot_general(
        left_side,
        right_side,
        (((1,), (1,)), ((), ())),
        precision=lax.Precision.HIGHEST,
        preferred_element_type=jnp.float32,
    )


def layer_norm(values, scaling, offset):
    average = jnp.mean(values, axis=-1, keepdims=True)
    centred = values - average
    spread = jnp.mean(centred * centred, axis=-1, keepdims=True)
    return centred * lax.rsqrt(spread + EPSILON) * scaling + offset


def gelu_tanh(values):
    return jax.nn.gelu(values, approximate=True)


def scored(queries, key_rows, labels):
    length = labels.shape[0]
    factor = queries.shape[-1] ** (-0.5)
    raw_scores = matmul_nt(queries, key_rows) * factor
    places = jnp.arange(length, dtype=jnp.int32)
    allowed = (labels[:, None] == labels[None, :]) & (places[None, :] <= places[:, None])
    return (raw_scores, allowed, factor)


def attend_one(packed):
    queries, key_rows, value_rows, labels = packed
    raw_scores, allowed, factor = scored(queries, key_rows, labels)
    masked = jnp.where(allowed, raw_scores, -1e30)
    row_max = jnp.max(masked, axis=1, keepdims=True)
    exponent = jnp.exp(masked - row_max)
    summed = jnp.sum(exponent, axis=1, keepdims=True)
    attended = matmul(exponent / summed, value_rows)
    return (attended, (row_max + jnp.log(summed))[:, 0])


def attend_back(packed):
    queries, key_rows, value_rows, attended, log_total, grad_attended, labels = packed
    raw_scores, allowed, factor = scored(queries, key_rows, labels)
    weights = jnp.where(
        allowed, jnp.exp(jnp.where(allowed, raw_scores - log_total[:, None], -1e30)), 0.0
    )
    grad_values = matmul_tn(weights, grad_attended)
    grad_weights = matmul_nt(grad_attended, value_rows)
    row_dot = jnp.sum(grad_attended * attended, axis=1, keepdims=True)
    grad_scores = weights * (grad_weights - row_dot) * factor
    grad_queries = matmul(grad_scores, key_rows)
    grad_keys = matmul_tn(grad_scores, queries)
    return (grad_queries, grad_keys, grad_values)


def to_batch(blocked, heads_local):
    seq_count, length, columns = blocked.shape
    head_dim = columns // heads_local
    return (
        blocked.reshape(seq_count, length, heads_local, head_dim)
        .transpose(0, 2, 1, 3)
        .reshape(seq_count * heads_local, length, head_dim)
    )


def from_batch(blocked, seq_count):
    batch_size, length, head_dim = blocked.shape
    heads_local = batch_size // seq_count
    return (
        blocked.reshape(seq_count, heads_local, length, head_dim)
        .transpose(0, 2, 1, 3)
        .reshape(seq_count, length, heads_local * head_dim)
    )


def shards(
    patches,
    segments,
    w_in,
    norm1_gain,
    norm1_bias,
    w_qkv,
    w_out,
    norm2_gain,
    norm2_bias,
    w_up,
    w_down,
    cotangent,
):
    seq_count, local_len, patch_width = patches.shape
    model_width = w_out.shape[1]
    heads_local = HEADS // lax.axis_size("sp")
    row_count = seq_count * local_len
    norm_params = jnp.stack([norm1_gain, norm1_bias, norm2_gain, norm2_bias])
    gathered = (
        lax.all_gather(w_in, "fsdp", axis=0, tiled=True),
        lax.all_gather(w_qkv, "fsdp", axis=0, tiled=True),
        lax.all_gather(w_out, "fsdp", axis=0, tiled=True),
        lax.all_gather(w_up, "fsdp", axis=0, tiled=True),
        lax.all_gather(w_down, "fsdp", axis=0, tiled=True),
        lax.all_gather(norm_params, "fsdp", axis=1, tiled=True),
    )
    in_full, qkv_full, out_full, up_full, down_full, norm_full = gathered
    patch_rows = patches.reshape(row_count, patch_width)
    stream = matmul(patch_rows, in_full)
    normed, norm1_pull = jax.vjp(layer_norm, stream, norm_full[0], norm_full[1])
    projected = matmul(normed, qkv_full)
    query_tok = projected[:, :model_width].reshape(seq_count, local_len, model_width)
    key_tok = projected[:, model_width : 2 * model_width].reshape(seq_count, local_len, model_width)
    value_tok = projected[:, 2 * model_width :].reshape(seq_count, local_len, model_width)
    query_seq, key_seq, value_seq = (
        lax.all_to_all(query_tok, "sp", split_axis=2, concat_axis=1, tiled=True),
        lax.all_to_all(key_tok, "sp", split_axis=2, concat_axis=1, tiled=True),
        lax.all_to_all(value_tok, "sp", split_axis=2, concat_axis=1, tiled=True),
    )
    labels = jnp.repeat(segments, heads_local, axis=0)
    query_batch = to_batch(query_seq, heads_local)
    key_batch = to_batch(key_seq, heads_local)
    value_batch = to_batch(value_seq, heads_local)
    attended, log_total = lax.map(attend_one, (query_batch, key_batch, value_batch, labels))
    attended_tok = lax.all_to_all(
        from_batch(attended, seq_count), "sp", split_axis=1, concat_axis=2, tiled=True
    )
    attended_rows = attended_tok.reshape(row_count, model_width)
    residual = stream + matmul(attended_rows, out_full)
    normed_two, norm2_pull = jax.vjp(layer_norm, residual, norm_full[2], norm_full[3])
    hidden_pre = matmul(normed_two, up_full)
    hidden, gelu_pull = jax.vjp(gelu_tanh, hidden_pre)
    result = residual + matmul(hidden, down_full)
    block_out = result.reshape(seq_count, local_len, model_width)
    in_back, qkv_back, out_back, up_back, down_back = (
        lax.all_gather(w_in, "fsdp", axis=0, tiled=True),
        lax.all_gather(w_qkv, "fsdp", axis=0, tiled=True),
        lax.all_gather(w_out, "fsdp", axis=0, tiled=True),
        lax.all_gather(w_up, "fsdp", axis=0, tiled=True),
        lax.all_gather(w_down, "fsdp", axis=0, tiled=True),
    )
    grad_rows = cotangent.reshape(row_count, model_width)
    grad_down = matmul_tn(hidden, grad_rows)
    (grad_pre,) = gelu_pull(matmul_nt(grad_rows, down_back))
    grad_up = matmul_tn(normed_two, grad_pre)
    grad_resid_norm, grad_gain_two, grad_offset_two = norm2_pull(matmul_nt(grad_pre, up_back))
    grad_resid = grad_rows + grad_resid_norm
    grad_out = matmul_tn(attended_rows, grad_resid)
    grad_att = matmul_nt(grad_resid, out_back).reshape(seq_count, local_len, model_width)
    grad_att_seq = lax.all_to_all(grad_att, "sp", split_axis=2, concat_axis=1, tiled=True)
    grad_query, grad_key, grad_value = lax.map(
        attend_back,
        (
            query_batch,
            key_batch,
            value_batch,
            attended,
            log_total,
            to_batch(grad_att_seq, heads_local),
            labels,
        ),
    )
    back_query, back_key, back_value = (
        lax.all_to_all(
            from_batch(grad_query, seq_count), "sp", split_axis=1, concat_axis=2, tiled=True
        ),
        lax.all_to_all(
            from_batch(grad_key, seq_count), "sp", split_axis=1, concat_axis=2, tiled=True
        ),
        lax.all_to_all(
            from_batch(grad_value, seq_count), "sp", split_axis=1, concat_axis=2, tiled=True
        ),
    )
    grad_proj = jnp.concatenate([back_query, back_key, back_value], axis=2).reshape(
        row_count, 3 * model_width
    )
    grad_qkv = matmul_tn(normed, grad_proj)
    grad_stream_norm, grad_gain_one, grad_offset_one = norm1_pull(matmul_nt(grad_proj, qkv_back))
    grad_stream = grad_resid + grad_stream_norm
    grad_in = matmul_tn(patch_rows, grad_stream)
    grad_patch = matmul_nt(grad_stream, in_back).reshape(seq_count, local_len, patch_width)
    every_part = (
        lax.psum_scatter(grad_in, "fsdp", scatter_dimension=0, tiled=True),
        lax.psum_scatter(grad_qkv, "fsdp", scatter_dimension=0, tiled=True),
        lax.psum_scatter(grad_out, "fsdp", scatter_dimension=0, tiled=True),
        lax.psum_scatter(grad_up, "fsdp", scatter_dimension=0, tiled=True),
        lax.psum_scatter(grad_down, "fsdp", scatter_dimension=0, tiled=True),
        lax.psum_scatter(
            jnp.stack([grad_gain_one, grad_offset_one, grad_gain_two, grad_offset_two]),
            "fsdp",
            scatter_dimension=1,
            tiled=True,
        ),
    )
    total_in, total_qkv, total_out, total_up, total_down, norm_total = lax.psum(
        (every_part[0], every_part[1], every_part[2], every_part[3], every_part[4], every_part[5]),
        "sp",
    )
    norm_first = norm_total[0:2]
    norm_second = norm_total[2:4]
    return (
        block_out,
        grad_patch,
        total_in,
        norm_first[0],
        norm_first[1],
        total_qkv,
        total_out,
        norm_second[0],
        norm_second[1],
        total_up,
        total_down,
    )


def solution(mesh):
    placed = (
        P("fsdp", "sp", None),
        P("fsdp", None),
        P("fsdp", None),
        P("fsdp"),
        P("fsdp"),
        P("fsdp", None),
        P("fsdp", None),
        P("fsdp"),
        P("fsdp"),
        P("fsdp", None),
        P("fsdp", None),
        P("fsdp", "sp", None),
    )
    return jax.shard_map(
        shards,
        mesh=mesh,
        in_specs=placed,
        out_specs=(
            P("fsdp", "sp", None),
            P("fsdp", "sp", None),
            P("fsdp", None),
            P("fsdp"),
            P("fsdp"),
            P("fsdp", None),
            P("fsdp", None),
            P("fsdp"),
            P("fsdp"),
            P("fsdp", None),
            P("fsdp", None),
        ),
        check_vma=False,
    )
```

profile of v0, /device:TPU:0, one launch (start us, length us, event | category | flops | bytes accessed | tf_op | source)
XLA Modules:
  0.0 1493.7 jit_solution(15155381434222323224)
XLA Ops:
  10.7 23.5 %all-gather = f32[16,48,4]{1,2,0:T(4,128)S(1)} all-gather(f32[1,48,4]{1,2,0:T(4,128)S(1)} %maximum_bitcast_fusion.3), channel_id=1, replica_groups=mesh['fsdp'=16,'sp'=2] {'fsdp'}, dimensions={0}, use_global_device_ids=true | all-gather | bytes 13056 | tf_op jit(solution)/shard_map/all_gather | solution.py:129
  34.3 77.1 %all-gather.7.cloned.1.call-done = f32[6144,768]{1,0:T(8,128)} async-done(((f32[384,768]{1,0:T(8,128)}), f32[6144,768]{1,0:T(8,128)}) %all-gather.7.cloned.1.call-update) | async-done | bytes 18874384 | tf_op jit(solution)/shard_map/all_gather | solution.py:124
  111.4 34.8 %fusion.99 = (f32[512]{0:T(512)S(1)}, f32[512,768]{1,0:T(8,128)S(1)}) fusion(f32[6144,768]{1,0:T(8,128)} %all-gather.7.cloned.1.call-done, f32[1,512,6144]{2,1,0:T(8,128)} %param.16), kind=kOutput, calls=%fused_computation.156 | convolution fusion | flops 28991422464 | bytes 33032192 | tf_op jit(solution)/shard_map/dot_general | solution.py:13
  146.5 33.9 %all-gather.9.cloned.1.call-done = f32[768,2304]{1,0:T(8,128)} async-done(((f32[48,2304]{1,0:T(8,128)}), f32[768,2304]{1,0:T(8,128)}) %all-gather.9.cloned.1.call-update) | async-done | bytes 7077904 | tf_op jit(solution)/shard_map/all_gather | solution.py:125
  180.4 14.2 fusion.61
  208.5 14.6 all-to-all-done
  232.5 14.3 all-to-all-done.1
  278.2 114.5 %while.26 = (s32[]{:T(128)}, f32[6,1024,64]{2,1,0:T(8,128)}, f32[6,1024]{1,0:T(8,128)S(1)}, s32[6,1024]{1,0:T(8,128)S(1)}, f32[6,1024,64]{2,1,0:T(8,128)}, /*ind...) while((s32[]{:T(128)}, f32[6,1024,64]{2,1,0:T(8,128)}, f32[6,1024]{1,0:T(8,128)S(1)}, ...), condition=%wide.region_5.6_spmd, body=%wide.region_2.5_spmd.sunk | while | flops 813693952 | bytes 14992501 | solution.py:148
  399.9 20.2 %all_to_all.129 = f32[1,1024,384]{2,0,1:T(1,128)S(1)} all-to-all(f32[1,1024,384]{2,0,1:T(1,128)S(1)} %copy.129), channel_id=1, replica_groups=mesh['fsdp'=16,'sp'=2] {'sp'}, dimensions={1} | all-to-all | bytes 3145728 | tf_op jit(solution)/shard_map/all_to_all | solution.py:149
  428.4 19.5 %fusion.63 = f32[512,3072]{1,0:T(8,128)} fusion(f32[768,3072]{1,0:T(8,128)} %all-gather.13.cloned.1.call-done, f32[512,768]{1,0:T(8,128)S(1)} %get-tuple-element.343, f32[768]{0:T(1024)S(1)} %get-tuple-element.283, f32[768]{0:T(1024)S(1)} %get-tuple-element.282, f32[512]{0:T(512)S(1)} %fusion.85, f32[512]{0:T(512)S(1)} %broadcast_multiply_fusion), kind=kOutput, calls=%fused_computation.102 | convolution fusion | flops 14497087488 | bytes 17311744 | tf_op jit(solution)/shard_map/dot_general | solution.py:13
  447.9 22.0 %fusion.51 = f32[512,3072]{1,0:T(8,128)S(1)} fusion(f32[512,3072]{1,0:T(8,128)} %fusion.63, f32[3072,768]{1,0:T(8,128)} %all-gather.15.cloned.1.call-done, f32[1,512,768]{2,1,0:T(8,128)} %param.27), kind=kOutput, calls=%fused_computation.68 | convolution fusion | flops 14525399040 | bytes 23592960 | tf_op jit(solution)/shard_map/dot_general | solution.py:29
  469.9 17.7 %multiply_reduce_fusion = (f32[768]{0:T(1024)S(1)}, f32[512]{0:T(512)S(1)}, f32[768]{0:T(1024)S(1)}, f32[512,768]{1,0:T(8,128)S(1)}) fusion(f32[512,768]{1,0:T(8,128)S(1)} %get-tuple-element.343, f32[512]{0:T(512)S(1)} %fusion.85, f32[512]{0:T(512)S(1)} %broadcast_multiply_fusion, f32[768]{0:T(1024)S(1)} %get-tuple-element.282, ...), kind=kOutput, calls=%fused_computation.88 | convolution fusion | flops 14498658304 | bytes 18889728 | tf_op jit(solution)/shard_map/dot_general | solution.py:29
  513.3 9.3 all-to-all-done.4
  529.8 197.5 %while.27 = (s32[]{:T(128)}, f32[6,1024,64]{1,2,0:T(8,128)}, f32[6,1024,64]{1,2,0:T(8,128)}, f32[6,1024,64]{1,2,0:T(8,128)}, s32[6,1024]{1,0:T(8,128)S(1)}, /*in...) while((s32[]{:T(128)}, f32[6,1024,64]{1,2,0:T(8,128)}, ...), condition=%wide.region_12.13_spmd, body=%wide.region_10.12_spmd.sunk | while | flops 4044487680 | bytes 47502504 | solution.py:175
  540.5 7.7 multiply_multiply_fusion.11
  573.3 7.7 multiply_multiply_fusion.11
  606.2 7.7 multiply_multiply_fusion.11
  671.7 7.7 multiply_multiply_fusion.11
  704.5 7.7 multiply_multiply_fusion.11
  741.6 10.7 all-to-all-done.7
  761.9 9.7 all-to-all-done.6
  795.6 26.3 %fusion.52 = f32[768,2304]{1,0:T(8,128)} fusion(f32[1,512,768]{1,2,0:T(8,128)} %bitcast.248, f32[1,512,768]{1,2,0:T(8,128)} %bitcast.250, f32[1,512,768]{1,2,0:T(8,128)} %bitcast.252, f32[512,768]{1,0:T(8,128)S(1)} %get-tuple-element.341, f32[768]{0:T(1024)S(1)} %get-tuple-element.284, f32[768]{0:T(1024)S(1)} %get-tuple-element.285, f32[512]{0:T(512)S(1)} %fusion.84, ...), kind=kOutput, calls=%fused_computation.71 | convolution fusion | flops 10875568128 | bytes 13379584 | tf_op jit(solution)/shard_map/dot_general | solution.py:19
  821.9 19.8 %fusion.62 = f32[768,3072]{1,0:T(8,128)} fusion(f32[512,3072]{1,0:T(8,128)} %copy-done.5, f32[512,768]{1,0:T(8,128)S(1)} %get-tuple-element.343, f32[768]{0:T(1024)S(1)} %get-tuple-element.283, f32[768]{0:T(1024)S(1)} %get-tuple-element.282, f32[512]{0:T(512)S(1)} %fusion.85, f32[512]{0:T(512)S(1)} %broadcast_multiply_fusion), kind=kOutput, calls=%fused_computation.101 | convolution fusion | flops 14497087488 | bytes 17311744 | tf_op jit(solution)/shard_map/dot_general | solution.py:19
  841.8 21.2 %fusion.54 = f32[3072,768]{1,0:T(8,128)} fusion(f32[512,3072]{1,0:T(8,128)} %fusion.63, f32[1,512,768]{2,1,0:T(8,128)} %param.27), kind=kOutput, calls=%fused_computation.73 | convolution fusion | flops 14508097536 | bytes 17301504 | tf_op jit(solution)/shard_map/dot_general | solution.py:19
  863.1 27.4 %multiply_reduce_fusion.1 = (f32[768]{0:T(1024)S(1)}, f32[512]{0:T(512)S(1)}, f32[768]{0:T(1024)S(1)}, f32[512,768]{1,0:T(8,128)S(1)}) fusion(f32[512,768]{1,0:T(8,128)S(1)} %get-tuple-element.341, f32[512]{0:T(512)S(1)} %fusion.84, f32[512]{0:T(512)S(1)} %broadcast_multiply_fusion.1, f32[768]{0:T(1024)S(1)} %get-tuple-element.285, ...), kind=kOutput, calls=%fused_computation.89 | convolution fusion | flops 10877138944 | bytes 14957568 | tf_op jit(solution)/shard_map/dot_general | solution.py:29
  892.3 35.4 %fusion.43 = f32[6144,768]{0,1:T(8,128)} fusion(f32[1,512,6144]{2,1,0:T(8,128)} %param.16, f32[512,768]{1,0:T(8,128)S(1)} %copy-done.3, f32[512,768]{1,0:T(8,128)S(1)} %get-tuple-element.328, f32[512]{0:T(512)S(1)} %negate_multiply_fusion), kind=kOutput, calls=%fused_computation.59 | convolution fusion | flops 28991815680 | bytes 34605056 | tf_op jit(solution)/shard_map/dot_general | solution.py:19
  928.9 94.8 %reduce-scatter.15.cloned.1.call-done = f32[48,3072]{1,0:T(8,128)} async-done(((f32[768,3072]{1,0:T(8,128)}), f32[48,3072]{1,0:T(8,128)}) %reduce-scatter.15.cloned.1.call-update) | async-done | bytes 589840 | tf_op jit(solution)/shard_map/reduce_scatter | solution.py:210
  1023.7 115.8 %reduce-scatter.17.cloned.1.call-done = f32[192,768]{1,0:T(8,128)} async-done(((f32[3072,768]{1,0:T(8,128)}), f32[192,768]{1,0:T(8,128)}) %reduce-scatter.17.cloned.1.call-update) | async-done | bytes 589840 | tf_op jit(solution)/shard_map/reduce_scatter | solution.py:211
  1139.6 198.5 %reduce-scatter.9.cloned.1.call-done = f32[384,768]{0,1:T(8,128)} async-done(((f32[6144,768]{0,1:T(8,128)}), f32[384,768]{0,1:T(8,128)}) %reduce-scatter.9.cloned.1.call-update) | async-done | bytes 1179664 | tf_op jit(solution)/shard_map/reduce_scatter | solution.py:207
  1338.1 21.3 %add_bitcast_fusion = f32[1,512,768]{2,1,0:T(8,128)} fusion(f32[512,768]{1,0:T(8,128)S(1)} %get-tuple-element.343, f32[3072,768]{1,0:T(8,128)} %all-gather.15.cloned.1.call-done, f32[512,3072]{1,0:T(8,128)} %fusion.63), kind=kOutput, calls=%fused_computation.93 | convolution fusion | flops 14508490752 | bytes 18874368 | tf_op jit(solution)/shard_map/dot_general | solution.py:13
  1359.5 35.1 %convolution_bitcast_fusion.2 = f32[1,512,6144]{2,1,0:T(8,128)} fusion(f32[6144,768]{1,0:T(8,128)} %all-gather.7.cloned.1.call-done, f32[512,768]{1,0:T(8,128)S(1)} %copy-done.4, f32[512,768]{1,0:T(8,128)S(1)} %copy-done.8, f32[512]{0:T(512)S(1)} %negate_multiply_fusion), kind=kOutput, calls=%fused_computation.60 | convolution fusion | flops 28991815680 | bytes 34605056 | tf_op jit(solution)/shard_map/dot_general | solution.py:29
  1403.2 77.6 %all-reduce.3.cloned.1.call-done = (f32[384,768]{0,1:T(8,128)}, f32[48,2304]{1,0:T(8,128)}, f32[48,768]{1,0:T(8,128)}, f32[48,3072]{1,0:T(8,128)}, f32[192,768]{1,0:T(8,128)}) async-done(((f32[384,768]{0,1:T(8,128)}, f32[48,2304]{1,0:T(8,128)}, f32[48,768]{1,0:T(8,128)}, f32[48,3072]{1,0:T(8,128)}, f32[192,768]{1,0:T(8,128)}), (f32[384,768]{0,1:T(8,128)}, f32[48,2304]{1,0:T(8,128)}, f32[48,768]{1,0:T(8,128)}, ...) | async-done | bytes 2949136 | tf_op jit(solution)/shard_map/psum | solution.py:219
  (257 shorter events, 444.1 us)
Async XLA Ops:
  7.2 104.2 %all-gather.7.cloned.1.call-start = ((), (), s32[]{:S(2)}) async-start(), calls=%async_computation.14 | async-start | bytes 20054016 | tf_op jit(solution)/shard_map/all_gather | solution.py:124
  8.0 172.5 %all-gather.9.cloned.1.call-start = ((), (), s32[]{:S(2)}) async-start(), calls=%async_computation.15 | async-start | bytes 7520256 | tf_op jit(solution)/shard_map/all_gather | solution.py:125
  8.7 413.1 %all-gather.11.cloned.1.call-start = ((), (), s32[]{:S(2)}) async-start(), calls=%async_computation.16 | async-start | bytes 2506752 | tf_op jit(solution)/shard_map/all_gather | solution.py:126
  9.4 419.0 %all-gather.13.cloned.1.call-start = ((), (), s32[]{:S(2)}) async-start(), calls=%async_computation.17 | async-start | bytes 10027008 | tf_op jit(solution)/shard_map/all_gather | solution.py:127
  10.0 437.9 %all-gather.15.cloned.1.call-start = ((), (), s32[]{:S(2)}) async-start(), calls=%async_computation.18 | async-start | bytes 10027008 | tf_op jit(solution)/shard_map/all_gather | solution.py:128
  146.5 48.2 %copy-start.14 = (f32[512]{0:T(512)}, f32[512]{0:T(512)S(1)}, u32[]{:S(2)}) copy-start(f32[512]{0:T(512)S(1)} %multiply_reduce_fusion.5) | copy-start | bytes 6148
  199.5 23.6 %all-to-all-start = ((f32[1,512,768]{1,0,2:T(1,128)}), f32[1,512,768]{1,0,2:T(1,128)S(1)}, u32[]{:S(2)}, u32[]{:S(2)}) async-start(f32[1,512,768]{1,0,2:T(1,128)} %copy.118), calls=%async_computation | async-start | bytes 3145728 | tf_op jit(solution)/shard_map/all_to_all | solution.py:140
  223.1 23.8 %all-to-all-start.1 = ((f32[1,512,768]{1,0,2:T(1,128)}), f32[1,512,768]{1,0,2:T(1,128)}, u32[]{:S(2)}, u32[]{:S(2)}) async-start(f32[1,512,768]{1,0,2:T(1,128)} %copy.120), calls=%async_computation.1 | async-start | bytes 3145728 | tf_op jit(solution)/shard_map/all_to_all | solution.py:141
  246.9 22.9 %all-to-all-start.2 = ((f32[1,512,768]{1,0,2:T(1,128)}), f32[1,512,768]{1,0,2:T(1,128)}, u32[]{:S(2)}, u32[]{:S(2)}) async-start(f32[1,512,768]{1,0,2:T(1,128)} %copy.122), calls=%async_computation.2 | async-start | bytes 3145728 | tf_op jit(solution)/shard_map/all_to_all | solution.py:142
  447.9 22.0 %copy-start.1 = (f32[768,3072]{1,0:T(8,128)S(1)}, f32[768,3072]{1,0:T(8,128)}, u32[]{:S(2)}) copy-start(f32[768,3072]{1,0:T(8,128)} %all-gather.13.cloned.1.call-done) | copy-start | bytes 28311556
  469.9 17.8 %copy-start.5 = (f32[512,3072]{1,0:T(8,128)}, f32[512,3072]{1,0:T(8,128)S(1)}, u32[]{:S(2)}) copy-start(f32[512,3072]{1,0:T(8,128)S(1)} %fusion.51) | copy-start | bytes 18874372
  501.3 21.3 %all-to-all-start.4 = ((f32[1,512,768]{1,0,2:T(1,128)}), f32[1,512,768]{1,0,2:T(1,128)}, u32[]{:S(2)}, u32[]{:S(2)}) async-start(f32[1,512,768]{1,0,2:T(1,128)} %copy.131), calls=%async_computation.4 | async-start | bytes 3145728 | tf_op jit(solution)/shard_map/all_to_all | solution.py:174
  505.9 423.0 %reduce-scatter.13.cloned.1.call-start = ((), (), s32[]{:S(2)}) async-start(), calls=%async_computation.21 | async-start | bytes 2506752 | tf_op jit(solution)/shard_map/reduce_scatter | solution.py:209
  554.3 4.7 copy-start
  587.1 4.7 copy-start
  619.9 4.7 copy-start
  652.7 4.7 copy-start
  685.4 4.7 copy-start
  718.2 4.7 copy-start
  732.2 20.2 %all-to-all-start.7 = ((f32[1,1024,384]{2,0,1:T(1,128)}), f32[1,1024,384]{2,0,1:T(1,128)}, u32[]{:S(2)}, u32[]{:S(2)}) async-start(f32[1,1024,384]{2,0,1:T(1,128)} %copy.141), calls=%async_computation.7 | async-start | bytes 3145728 | tf_op jit(solution)/shard_map/all_to_all | solution.py:194
  752.3 19.2 %all-to-all-start.6 = ((f32[1,1024,384]{2,0,1:T(1,128)}), f32[1,1024,384]{2,0,1:T(1,128)}, u32[]{:S(2)}, u32[]{:S(2)}) async-start(f32[1,1024,384]{2,0,1:T(1,128)} %copy.139), calls=%async_computation.6 | async-start | bytes 3145728 | tf_op jit(solution)/shard_map/all_to_all | solution.py:191
  771.6 18.3 %all-to-all-start.5 = ((f32[1,1024,384]{2,0,1:T(1,128)}), f32[1,1024,384]{2,0,1:T(1,128)}, u32[]{:S(2)}, u32[]{:S(2)}) async-start(f32[1,1024,384]{2,0,1:T(1,128)} %copy.137), calls=%async_computation.5 | async-start | bytes 3145728 | tf_op jit(solution)/shard_map/all_to_all | solution.py:188
  776.2 152.7 %reduce-scatter.11.cloned.1.call-start = ((), (), s32[]{:S(2)}) async-start(), calls=%async_computation.20 | async-start | bytes 7520256 | tf_op jit(solution)/shard_map/reduce_scatter | solution.py:208
  821.9 201.8 %reduce-scatter.15.cloned.1.call-start = ((), (), s32[]{:S(2)}) async-start(), calls=%async_computation.22 | async-start | bytes 10027008 | tf_op jit(solution)/shard_map/reduce_scatter | solution.py:210
  841.7 297.8 %reduce-scatter.17.cloned.1.call-start = ((), (), s32[]{:S(2)}) async-start(), calls=%async_computation.23 | async-start | bytes 10027008 | tf_op jit(solution)/shard_map/reduce_scatter | solution.py:211
  863.0 27.5 %copy-start.15 = (f32[512]{0:T(512)S(1)}, f32[512]{0:T(512)}, u32[]{:S(2)}) copy-start(f32[512]{0:T(512)} %copy-done.14) | copy-start | bytes 6148
  863.0 475.0 %reduce-scatter.9.cloned.1.call-start = ((), (), s32[]{:S(2)}) async-start(), calls=%async_computation.19 | async-start | bytes 20054016 | tf_op jit(solution)/shard_map/reduce_scatter | solution.py:207
  927.7 469.2 %reduce-scatter.19.cloned.1.call-start = ((), (), s32[]{:S(2)}) async-start(), calls=%async_computation.24 | async-start | bytes 417792
  928.8 552.0 %all-reduce.3.cloned.1.call-start = ((), (), s32[]{:S(2)}) async-start(), calls=%async_computation.25 | async-start | bytes 5898240 | tf_op jit(solution)/shard_map/psum | solution.py:219
  1338.1 21.3 %copy-start.4 = (f32[512,768]{1,0:T(8,128)S(1)}, f32[512,768]{1,0:T(8,128)}, u32[]{:S(2)}) copy-start(f32[512,768]{1,0:T(8,128)} %copy-done.2) | copy-start | bytes 4718596
  1338.1 21.3 %copy-start.8 = (f32[512,768]{1,0:T(8,128)S(1)}, f32[512,768]{1,0:T(8,128)}, u32[]{:S(2)}) copy-start(f32[512,768]{1,0:T(8,128)} %copy-done.7) | copy-start | bytes 4718596
  1480.8 4.2 copy-start.11
  (13 other events, 33.3 us)
Sparse Core Ops, SparseCore 0:
  9.6 101.6 all-gather.6
  113.7 66.7 all-gather.8
  182.7 40.7 all-gather.10
  225.7 80.2 all-gather.12
  308.1 79.5 all-gather.14
  513.4 61.1 reduce-scatter.12
  822.0 86.1 reduce-scatter.10
  912.8 110.8 reduce-scatter.14
  1028.4 111.1 reduce-scatter.16
  1143.5 194.5 reduce-scatter.8
  1342.2 54.6 reduce-scatter.18
  1399.5 81.2 all-reduce.2
where the time goes:
time: 1510 us; the launch traced here: 1490 us
  waiting for transfers between devices  667 us (44%)
  matrix products  532 us (35%)
  local copies, waits for them, and re-layouts  168 us (11%)
  blocking collectives  48.6 us (3%)
  starting transfers between devices  31.9 us (2%)
  other arithmetic  29.9 us (2%)
    dot_general x23, matrix products, matmul_nt(): lax.dot_general(left_side, right_side, (((1,), (1,)), ((), ())), precisio...  236 us
    reduce_scatter x1, waiting for transfers between devices, shards(): lax.psum_scatter(grad_in, 'fsdp', scatter_dimension=0, tiled=True)  199 us
    dot_general x17, matrix products, matmul_tn(): lax.dot_general(left_side, right_side, (((0,), (0,)), ((), ())), precisio...  164 us
    dot_general x11, matrix products, matmul(): jnp.dot(left_side, right_side, precision=lax.Precision.HIGHEST, preferred...  132 us
    reduce_scatter x1, waiting for transfers between devices, shards(): lax.psum_scatter(grad_down, 'fsdp', scatter_dimension=0, tiled=True)  116 us
    reduce_scatter x1, waiting for transfers between devices, shards(): lax.psum_scatter(grad_up, 'fsdp', scatter_dimension=0, tiled=True)  94.8 us
    psum x1, waiting for transfers between devices, shards(): lax.psum((every_part[0], every_part[1], every_part[2], every_part[3], eve...  77.6 us
    all_gather x1, waiting for transfers between devices, shards(): lax.all_gather(w_in, 'fsdp', axis=0, tiled=True)  77.1 us
  transfers between devices with their start and end apart: 19, of which 14 were waited for; matrix products, arithmetic and copies ran while one was open for 45% of the time, Pallas kernels for 0%

commit v1 on v0

--- a/solution.py
+++ b/solution.py
@@ -1,6 +1,8 @@
 import jax
 import jax.numpy as jnp
 from jax import lax
+from jax.experimental import pallas as pl
+from jax.experimental.pallas import tpu as pltpu
 from jax.sharding import PartitionSpec as P
 
 HEADS = 12
@@ -11,7 +13,7 @@
 
 def matmul(left_side, right_side):
     return jnp.dot(
-        left_side, right_side, precision=lax.Precision.HIGHEST, preferred_element_type=jnp.float32
+        left_side, right_side, precision=lax.Precision.HIGH, preferred_element_type=jnp.float32
     )
 
 
@@ -20,7 +22,7 @@
         left_side,
         right_side,
         (((0,), (0,)), ((), ())),
-        precision=lax.Precision.HIGHEST,
+        precision=lax.Precision.HIGH,
         preferred_element_type=jnp.float32,
     )
 
@@ -30,7 +32,7 @@
         left_side,
         right_side,
         (((1,), (1,)), ((), ())),
-        precision=lax.Precision.HIGHEST,
+        precision=lax.Precision.HIGH,
         preferred_element_type=jnp.float32,
     )
 
@@ -237,37 +239,384 @@
     )
 
 
+LANES = 128
+BLOCK = 256
+BF = jnp.bfloat16
+F32 = jnp.float32
+
+
+def halves(values):
+    high = values.astype(BF).astype(F32)
+    return high, values - high
+
+
+def roll_half(values):
+    return pltpu.roll(values, LANES // 2, 1)
+
+
+def low_lanes(rows):
+    return lax.broadcasted_iota(jnp.int32, (rows, LANES), 1) < LANES // 2
+
+
+def pair_tiles(values):
+    high, low = halves(values)
+    first = low_lanes(values.shape[0])
+    return (
+        jnp.where(first, high, roll_half(low)).astype(BF),
+        jnp.where(first, roll_half(high), low).astype(BF),
+    )
+
+
+def spread_tiles(values):
+    high, low = halves(values)
+    first = low_lanes(values.shape[0])
+    high_r, low_r = roll_half(high), roll_half(low)
+    return (
+        jnp.concatenate([jnp.where(first, high, high_r), jnp.where(first, low, low_r)], axis=1).astype(BF),
+        jnp.concatenate([jnp.where(first, high_r, high), jnp.where(first, low_r, low)], axis=1).astype(BF),
+    )
+
+
+def nt(left, right):
+    return lax.dot_general(left, right, (((1,), (1,)), ((), ())), preferred_element_type=F32)
+
+
+def nn(left, right):
+    return lax.dot_general(left, right, (((1,), (0,)), ((), ())), preferred_element_type=F32)
+
+
+def tn(left, right):
+    return lax.dot_general(left, right, (((0,), (0,)), ((), ())), preferred_element_type=F32)
+
+
+def split_bf(values):
+    high = values.astype(BF)
+    return high, (values - high.astype(F32)).astype(BF)
+
+
+def forward_kernel(pos_ref, seg_ref, *refs):
+    (q_own, k_own, v_own, q_in, k_in, v_in, seg_col, seg_row,
+     o_own, o_out, lse_ref, tq, hk, tv, out_s) = refs
+    rows = q_own.shape[0]
+    own = pl.multiple_of(pos_ref[0] * rows, rows)
+    other = pl.multiple_of((1 - pos_ref[0]) * rows, rows)
+    for place, q, k, v in ((own, q_own, k_own, v_own), (other, q_in, k_in, v_in)):
+        span = pl.ds(place, rows)
+        for head, tile in enumerate(pair_tiles(q[...] * 0.125)):
+            tq[head, span, :] = jnp.concatenate([tile, tile], axis=1)
+        for head, tile in enumerate(spread_tiles(k[...])):
+            hk[head, span, :] = tile
+        for head, tile in enumerate(pair_tiles(v[...])):
+            tv[head, span, :] = tile
+    blocks = 2 * rows // BLOCK
+    first = low_lanes(BLOCK)
+
+    def query_block(i, carry):
+        q_span = pl.ds(pl.multiple_of(i * BLOCK, BLOCK), BLOCK)
+        first_label = seg_ref[i * BLOCK]
+        start = jnp.int32(0)
+        for j in range(blocks):
+            start = start + jnp.where((j < i) & (seg_ref[j * BLOCK + BLOCK - 1] < first_label), 1, 0)
+        label = seg_col[q_span, :1]
+        q_place = i * BLOCK + lax.broadcasted_iota(jnp.int32, (BLOCK, BLOCK), 0)
+
+        def key_block(step, state):
+            j = i - step
+            k_span = pl.ds(pl.multiple_of(j * BLOCK, BLOCK), BLOCK)
+            k_place = j * BLOCK + lax.broadcasted_iota(jnp.int32, (BLOCK, BLOCK), 1)
+            allowed = (label == seg_row[j]) & (k_place <= q_place)
+            new_state = []
+            for head in range(2):
+                top, total, acc = state[head]
+                scores = nt(tq[head, q_span, :], hk[head, k_span, :])
+                scores = jnp.where(allowed, scores, -1e30)
+                new_top = jnp.maximum(top, jnp.max(scores, axis=1, keepdims=True))
+                weight = jnp.exp(scores - new_top)
+                keep = jnp.exp(top - new_top)
+                high, low = split_bf(weight)
+                values = tv[head, k_span, :]
+                new_state.append((
+                    new_top,
+                    total * keep + jnp.sum(weight, axis=1, keepdims=True),
+                    acc * keep + nn(high, values) + nn(low, values),
+                ))
+            return tuple(new_state)
+
+        init = (
+            jnp.full((BLOCK, 1), -1e30, F32),
+            jnp.zeros((BLOCK, 1), F32),
+            jnp.zeros((BLOCK, LANES), F32),
+        )
+        state = lax.fori_loop(0, i - start + 1, key_block, (init, init))
+        outs, logs = [], []
+        for top, total, acc in state:
+            outs.append((acc + roll_half(acc)) / total)
+            logs.append(jnp.broadcast_to(top + jnp.log(total), (BLOCK, LANES)))
+        out_s[q_span, :] = jnp.where(first, outs[0], outs[1])
+        lse_ref[q_span, :] = jnp.where(first, logs[0], logs[1])
+        return carry
+
+    lax.fori_loop(0, blocks, query_block, 0)
+    o_own[...] = out_s[pl.ds(own, rows), :]
+    o_out[...] = out_s[pl.ds(other, rows), :]
+
+
+def attend_forward(own, received, position, labels):
+    rows, columns = own.shape
+    width = columns // 3
+    pairs = width // LANES
+    length = 2 * rows
+
+    def part(which):
+        return pl.BlockSpec((rows, LANES), lambda g, *_: (0, which * pairs + g))
+
+    whole = pl.BlockSpec((rows, LANES), lambda g, *_: (0, g))
+    return pl.pallas_call(
+        forward_kernel,
+        grid_spec=pltpu.PrefetchScalarGridSpec(
+            num_scalar_prefetch=2,
+            grid=(pairs,),
+            in_specs=[part(0), part(1), part(2), part(0), part(1), part(2),
+                      pl.BlockSpec((length, LANES), lambda g, *_: (0, 0)),
+                      pl.BlockSpec((length // BLOCK, 1, BLOCK), lambda g, *_: (0, 0, 0))],
+            out_specs=[whole, whole, pl.BlockSpec((length, LANES), lambda g, *_: (0, g))],
+            scratch_shapes=[
+                pltpu.VMEM((2, length, 2 * LANES), BF),
+                pltpu.VMEM((2, length, 2 * LANES), BF),
+                pltpu.VMEM((2, length, LANES), BF),
+                pltpu.VMEM((length, LANES), F32),
+            ],
+        ),
+        out_shape=[
+            jax.ShapeDtypeStruct((rows, width), F32),
+            jax.ShapeDtypeStruct((rows, width), F32),
+            jax.ShapeDtypeStruct((length, width), F32),
+        ],
+        cost_estimate=pl.CostEstimate(flops=20 * 10**9, bytes_accessed=8 * rows * columns * 3, transcendentals=length * width * 8),
+        compiler_params=pltpu.CompilerParams(vmem_limit_bytes=48 * 1024 * 1024),
+        name="attend_forward",
+    )(position, labels, own, own, own, received, received, received,
+      jnp.broadcast_to(labels[:, None], (length, LANES)), labels.reshape(length // BLOCK, 1, BLOCK))
+
+
+def backward_kernel(pos_ref, seg_ref, *refs):
+    (q_own, k_own, v_own, q_in, k_in, v_in, o_own, o_in, g_own, g_in, lse_ref, seg_col, seg_row,
+     gq_own, gk_own, gv_own, gq_out, gk_out, gv_out,
+     tq, hk, tk, hv, tg, lse_t, delta_t, gq_s, gk_s, gv_s) = refs
+    rows = q_own.shape[0]
+    length = 2 * rows
+    own = pl.multiple_of(pos_ref[0] * rows, rows)
+    other = pl.multiple_of((1 - pos_ref[0]) * rows, rows)
+    half = LANES // 2
+    for place, q, k, v, o, g in ((own, q_own, k_own, v_own, o_own, g_own), (other, q_in, k_in, v_in, o_in, g_in)):
+        span = pl.ds(place, rows)
+        for head, tile in enumerate(pair_tiles(q[...] * 0.125)):
+            tq[head, span, :] = jnp.concatenate([tile, tile], axis=1)
+        for head, tile in enumerate(pair_tiles(g[...])):
+            tg[head, span, :] = jnp.concatenate([tile, tile], axis=1)
+        for head, tile in enumerate(spread_tiles(k[...])):
+            hk[head, span, :] = tile
+        for head, tile in enumerate(spread_tiles(v[...])):
+            hv[head, span, :] = tile
+        for head, tile in enumerate(pair_tiles(k[...])):
+            tk[head, span, :] = tile
+        turned = jnp.transpose(o[...] * g[...])
+        for head in range(2):
+            delta_t[head, 0:1, span] = jnp.sum(turned[head * half:(head + 1) * half], axis=0, keepdims=True)
+    turned = jnp.transpose(lse_ref[...])
+    for head in range(2):
+        lse_t[head, 0:1, :] = turned[head * half:head * half + 1]
+    blocks = length // BLOCK
+    first = low_lanes(BLOCK)
+    gq_s[...] = jnp.zeros_like(gq_s)
+
+    def key_block(j, carry):
+        k_span = pl.ds(pl.multiple_of(j * BLOCK, BLOCK), BLOCK)
+        last_label = seg_ref[j * BLOCK + BLOCK - 1]
+        count = jnp.int32(1)
+        for i in range(blocks):
+            count = count + jnp.where((i > j) & (seg_ref[i * BLOCK] <= last_label), 1, 0)
+        label = seg_col[k_span, :1]
+        k_place = j * BLOCK + lax.broadcasted_iota(jnp.int32, (BLOCK, BLOCK), 0)
+
+        def query_block(step, state):
+            i = j + step
+            q_span = pl.ds(pl.multiple_of(i * BLOCK, BLOCK), BLOCK)
+            q_place = i * BLOCK + lax.broadcasted_iota(jnp.int32, (BLOCK, BLOCK), 1)
+            allowed = (label == seg_row[i]) & (k_place <= q_place)
+            new_state = []
+            for head in range(2):
+                grad_k, grad_v = state[head]
+                query = tq[head, q_span, :]
+                grad = tg[head, q_span, :]
+                scores = nt(hk[head, k_span, :], query)
+                weight = jnp.exp(jnp.where(allowed, scores - lse_t[head, 0:1, q_span], -1e30))
+                grad_weight = nt(hv[head, k_span, :], grad)
+                grad_score = weight * (grad_weight - delta_t[head, 0:1, q_span])
+                w_high, w_low = split_bf(weight)
+                s_high, s_low = split_bf(grad_score)
+                grad_v = grad_v + nn(w_high, grad[:, :LANES]) + nn(w_low, grad[:, :LANES])
+                grad_k = grad_k + nn(s_high, query[:, :LANES]) + nn(s_low, query[:, :LANES])
+                keys = tk[head, k_span, :]
+                gq_s[head, q_span, :] += tn(s_high, keys) + tn(s_low, keys)
+                new_state.append((grad_k, grad_v))
+            return tuple(new_state)
+
+        zero = jnp.zeros((BLOCK, LANES), F32)
+        state = lax.fori_loop(0, count, query_block, ((zero, zero), (zero, zero)))
+        for slot, store in ((0, gk_s), (1, gv_s)):
+            left, right = state[0][slot], state[1][slot]
+            store[k_span, :] = jnp.where(first, left + roll_half(left), right + roll_half(right))
+        return carry
+
+    lax.fori_loop(0, blocks, key_block, 0)
+    wide = low_lanes(rows)
+    for place, gq, gk, gv in ((own, gq_own, gk_own, gv_own), (other, gq_out, gk_out, gv_out)):
+        span = pl.ds(place, rows)
+        left, right = gq_s[0, span, :], gq_s[1, span, :]
+        gq[...] = jnp.where(wide, left + roll_half(left), right + roll_half(right)) * 0.125
+        gk[...] = gk_s[span, :]
+        gv[...] = gv_s[span, :]
+
+
+def attend_backward(own, received, out_own, out_in, grad_own, grad_in, logs, position, labels):
+    rows, columns = own.shape
+    width = columns // 3
+    pairs = width // LANES
+    length = 2 * rows
+
+    def part(which):
+        return pl.BlockSpec((rows, LANES), lambda g, *_: (0, which * pairs + g))
+
+    whole = pl.BlockSpec((rows, LANES), lambda g, *_: (0, g))
+    outs = pl.pallas_call(
+        backward_kernel,
+        grid_spec=pltpu.PrefetchScalarGridSpec(
+            num_scalar_prefetch=2,
+            grid=(pairs,),
+            in_specs=[part(0), part(1), part(2), part(0), part(1), part(2), whole, whole, whole, whole,
+                      pl.BlockSpec((length, LANES), lambda g, *_: (0, g)),
+                      pl.BlockSpec((length, LANES), lambda g, *_: (0, 0)),
+                      pl.BlockSpec((length // BLOCK, 1, BLOCK), lambda g, *_: (0, 0, 0))],
+            out_specs=[whole] * 6,
+            scratch_shapes=[
+                pltpu.VMEM((2, length, 2 * LANES), BF),
+                pltpu.VMEM((2, length, 2 * LANES), BF),
+                pltpu.VMEM((2, length, LANES), BF),
+                pltpu.VMEM((2, length, 2 * LANES), BF),
+                pltpu.VMEM((2, length, 2 * LANES), BF),
+                pltpu.VMEM((2, 8, length), F32),
+                pltpu.VMEM((2, 8, length), F32),
+                pltpu.VMEM((2, length, LANES), F32),
+                pltpu.VMEM((length, LANES), F32),
+                pltpu.VMEM((length, LANES), F32),
+            ],
+        ),
+        out_shape=[jax.ShapeDtypeStruct((rows, width), F32)] * 6,
+        cost_estimate=pl.CostEstimate(flops=40 * 10**9, bytes_accessed=8 * rows * columns * 5, transcendentals=length * width * 8),
+        compiler_params=pltpu.CompilerParams(vmem_limit_bytes=56 * 1024 * 1024),
+        name="attend_backward",
+    )(position, labels, own, own, own, received, received, received, out_own, out_in, grad_own, grad_in, logs,
+      jnp.broadcast_to(labels[:, None], (length, LANES)), labels.reshape(length // BLOCK, 1, BLOCK))
+    return outs
+
+
+def fast_shards(
+    patches, segments, w_in, norm1_gain, norm1_bias, w_qkv, w_out, norm2_gain, norm2_bias, w_up, w_down, cotangent
+):
+    _, rows, patch_width = patches.shape
+    width = w_out.shape[1]
+    position = lax.axis_index("sp")
+    places = position[None].astype(jnp.int32)
+    labels = segments[0]
+    norm_params = jnp.stack([norm1_gain, norm1_bias, norm2_gain, norm2_bias])
+    in_full = lax.all_gather(w_in, "fsdp", axis=0, tiled=True)
+    norm_full = lax.all_gather(norm_params, "fsdp", axis=1, tiled=True)
+    qkv_full = lax.all_gather(w_qkv, "fsdp", axis=0, tiled=True)
+    out_full = lax.all_gather(w_out, "fsdp", axis=0, tiled=True)
+    up_full = lax.all_gather(w_up, "fsdp", axis=0, tiled=True)
+    down_full = lax.all_gather(w_down, "fsdp", axis=0, tiled=True)
+    patch_rows = patches[0]
+    stream = matmul(patch_rows, in_full)
+    normed, norm1_pull = jax.vjp(layer_norm, stream, norm_full[0], norm_full[1])
+    half = width // 2
+    by_half = qkv_full.reshape(width, 3, 2, half)
+    swap = [(0, 1), (1, 0)]
+
+    def columns_of(which):
+        return lax.dynamic_index_in_dim(by_half, which, 2, keepdims=False).reshape(width, 3 * half)
+
+    own_columns = columns_of(position)
+    sent_columns = columns_of(1 - position)
+    received = lax.ppermute(matmul(normed, sent_columns), "sp", swap)
+    own = matmul(normed, own_columns)
+    out_own, out_sent, logs = attend_forward(own, received, places, labels)
+    out_in = lax.ppermute(out_sent, "sp", swap)
+
+    def whole_rows(mine, theirs):
+        return jnp.where(position == 0, jnp.concatenate([mine, theirs], 1), jnp.concatenate([theirs, mine], 1))
+
+    attended_rows = whole_rows(out_own, out_in)
+    residual = stream + matmul(attended_rows, out_full)
+    normed_two, norm2_pull = jax.vjp(layer_norm, residual, norm_full[2], norm_full[3])
+    hidden_pre = matmul(normed_two, up_full)
+    hidden, gelu_pull = jax.vjp(gelu_tanh, hidden_pre)
+    block_out = residual + matmul(hidden, down_full)
+    grad_rows = cotangent[0]
+    grad_down = matmul_tn(hidden, grad_rows)
+    (grad_pre,) = gelu_pull(matmul_nt(grad_rows, down_full))
+    grad_up = matmul_tn(normed_two, grad_pre)
+    grad_resid_norm, grad_gain_two, grad_offset_two = norm2_pull(matmul_nt(grad_pre, up_full))
+    grad_resid = grad_rows + grad_resid_norm
+    grad_out = matmul_tn(attended_rows, grad_resid)
+    out_by_half = out_full.reshape(2, half, width)
+    grad_sent = matmul_nt(grad_resid, lax.dynamic_index_in_dim(out_by_half, 1 - position, 0, keepdims=False))
+    grad_in = lax.ppermute(grad_sent, "sp", swap)
+    grad_own = matmul_nt(grad_resid, lax.dynamic_index_in_dim(out_by_half, position, 0, keepdims=False))
+    parts = attend_backward(own, received, out_own, out_sent, grad_own, grad_in, logs, places, labels)
+    mine = jnp.concatenate(parts[:3], axis=1)
+    theirs = lax.ppermute(jnp.concatenate(parts[3:], axis=1), "sp", swap)
+    grad_normed = matmul_nt(mine, own_columns) + matmul_nt(theirs, sent_columns)
+    grad_proj = whole_rows(mine.reshape(rows, 3, half), theirs.reshape(rows, 3, half))
+    low = jnp.where(position == 0, mine, theirs).reshape(rows, 3, 1, half)
+    high = jnp.where(position == 0, theirs, mine).reshape(rows, 3, 1, half)
+    grad_proj = jnp.concatenate([low, high], axis=2).reshape(rows, 3 * width)
+    grad_qkv = matmul_tn(normed, grad_proj)
+    grad_stream_norm, grad_gain_one, grad_offset_one = norm1_pull(grad_normed)
+    grad_stream = grad_resid + grad_stream_norm
+    grad_w_in = matmul_tn(patch_rows, grad_stream)
+    grad_patch = matmul_nt(grad_stream, in_full)
+
+    def scattered(value, dimension=0):
+        return lax.psum_scatter(value, "fsdp", scatter_dimension=dimension, tiled=True)
+
+    totals = lax.psum(
+        (
+            scattered(grad_w_in),
+            scattered(grad_qkv),
+            scattered(grad_out),
+            scattered(grad_up),
+            scattered(grad_down),
+            scattered(jnp.stack([grad_gain_one, grad_offset_one, grad_gain_two, grad_offset_two]), 1),
+        ),
+        "sp",
+    )
+    norms = totals[5]
+    return (
+        block_out[None], grad_patch[None], totals[0], norms[0], norms[1], totals[1], totals[2], norms[2], norms[3],
+        totals[3], totals[4],
+    )
+
+
 def solution(mesh):
-    placed = (
-        P("fsdp", "sp", None),
-        P("fsdp", None),
-        P("fsdp", None),
-        P("fsdp"),
-        P("fsdp"),
-        P("fsdp", None),
-        P("fsdp", None),
-        P("fsdp"),
-        P("fsdp"),
-        P("fsdp", None),
-        P("fsdp", None),
-        P("fsdp", "sp", None),
-    )
+    sharded = P("fsdp", "sp", None)
+    matrix = P("fsdp", None)
+    vector = P("fsdp")
+    fast = mesh.shape["fsdp"] == 16 and mesh.shape["sp"] == 2
     return jax.shard_map(
-        shards,
+        fast_shards if fast else shards,
         mesh=mesh,
-        in_specs=placed,
-        out_specs=(
-            P("fsdp", "sp", None),
-            P("fsdp", "sp", None),
-            P("fsdp", None),
-            P("fsdp"),
-            P("fsdp"),
-            P("fsdp", None),
-            P("fsdp", None),
-            P("fsdp"),
-            P("fsdp"),
-            P("fsdp", None),
-            P("fsdp", None),
-        ),
+        in_specs=(sharded, matrix, matrix, vector, vector, matrix, matrix, vector, vector, matrix, matrix, sharded),
+        out_specs=(sharded, sharded, matrix, vector, vector, matrix, matrix, vector, vector, matrix, matrix),
         check_vma=False,
     )

time: 1510 us -> 1240 us (0.82)
  matrix products: 532 us -> 184 us
  waiting for transfers between devices: 667 us -> 854 us
  local copies, waits for them, and re-layouts: 168 us -> 64.8 us
  Pallas kernels: 0 us -> 67.1 us
  starting transfers between devices: 31.9 us -> 6.44 us
  blocking collectives: 48.6 us -> 28.4 us
  other arithmetic: 29.9 us -> 12.6 us
    dot_general x23 -> x7, matrix products: 236 us -> 57.6 us  [matmul_nt(): lax.dot_general(left_side, right_side, (((1,), (1,)), ((), ())), precisio...]
    ppermute x0 -> x4, waiting for transfers between devices: none -> 116 us  [the longest x1 48.1 us: fast_shards(): received = lax.ppermute(matmul(normed, sent_columns), 'sp', swap)]
    dot_general x17 -> x5, matrix products: 164 us -> 65.4 us  [matmul_tn(): lax.dot_general(left_side, right_side, (((0,), (0,)), ((), ())), precisio...]
    dot_general x11 -> x6, matrix products: 132 us -> 61 us  [matmul(): jnp.dot(left_side, right_side, precision=lax.Precision.HIGH, preferred_el...]
    pallas_call x0 -> x2, Pallas kernels: none -> 67.1 us  [the longest x1 36.9 us: attend_backward(): pl.pallas_call(backward_kernel, grid_spec=pltpu.PrefetchScalarGridSpec(nu...]
    all_to_all x7 -> x0, waiting for transfers between devices: 63.5 us -> none  [the longest x1 14.6 us: shards(): lax.all_to_all(query_tok, 'sp', split_axis=2, concat_axis=1, tiled=True)]
    all_gather x5, waiting for transfers between devices: 111 us -> 171 us  [the longest x1 65.5 us: fast_shards(): down_full = lax.all_gather(w_down, 'fsdp', axis=0, tiled=True)]
    reduce_scatter x5, waiting for transfers between devices: 409 us -> 464 us  [scattered(): lax.psum_scatter(value, 'fsdp', scatter_dimension=dimension, tiled=True)]
  transfers between devices with their start and end apart: 19 -> 16, of which waited for: 14 -> 13; matrix products, arithmetic and copies ran while one was open for 45% -> 18% of each run, Pallas kernels for 0% -> 2%
where the time goes in v1:
time: 1240 us; the launch traced here: 1230 us
  waiting for transfers between devices  854 us (69%)
  matrix products  184 us (15%)
  Pallas kernels  67.1 us (5%)
  local copies, waits for them, and re-layouts  64.8 us (5%)
  blocking collectives  28.4 us (2%)
  between operations  15.2 us (1%)
  other arithmetic  12.6 us (1%)
    reduce_scatter x5, waiting for transfers between devices, scattered(): lax.psum_scatter(value, 'fsdp', scatter_dimension=dimension, tiled=True)  464 us
    psum x1, waiting for transfers between devices, fast_shards(): lax.psum((scattered(grad_w_in), scattered(grad_qkv), scattered(grad_out),...  77.6 us
    all_gather x1, waiting for transfers between devices, fast_shards(): down_full = lax.all_gather(w_down, 'fsdp', axis=0, tiled=True)  65.5 us
    dot_general x5, matrix products, matmul_tn(): lax.dot_general(left_side, right_side, (((0,), (0,)), ((), ())), precisio...  65.4 us
    dot_general x6, matrix products, matmul(): jnp.dot(left_side, right_side, precision=lax.Precision.HIGH, preferred_el...  61 us
    all_gather x1, waiting for transfers between devices, fast_shards(): in_full = lax.all_gather(w_in, 'fsdp', axis=0, tiled=True)  60.1 us
    dot_general x7, matrix products, matmul_nt(): lax.dot_general(left_side, right_side, (((1,), (1,)), ((), ())), precisio...  57.6 us
    ppermute x1, waiting for transfers between devices, fast_shards(): received = lax.ppermute(matmul(normed, sent_columns), 'sp', swap)  48.1 us
  transfers between devices with their start and end apart: 16, of which 13 were waited for; matrix products, arithmetic and copies ran while one was open for 18% of the time, Pallas kernels for 2%

profile of v1, /device:TPU:0, one launch (start us, length us, event | category | flops | bytes accessed | tf_op | source)
XLA Modules:
  0.0 1232.1 jit_solution(12913938644675041480)
XLA Ops:
  10.7 23.5 %all-gather = f32[16,48,4]{1,2,0:T(4,128)S(1)} all-gather(f32[1,48,4]{1,2,0:T(4,128)S(1)} %maximum_bitcast_fusion), channel_id=1, replica_groups=mesh['fsdp'=16,'sp'=2] {'fsdp'}, dimensions={0}, use_global_device_ids=true | all-gather | bytes 13056 | tf_op jit(solution)/shard_map/all_gather | solution.py:534
  34.3 45.4 %all-gather.9.cloned.1.call-done = f32[768,2304]{1,0:T(8,128)} async-done(((f32[48,2304]{1,0:T(8,128)}), f32[768,2304]{1,0:T(8,128)}) %all-gather.9.cloned.1.call-update) | async-done | bytes 7077904 | tf_op jit(solution)/shard_map/all_gather | solution.py:535
  79.7 9.3 reshape.114
  89.0 27.6 %dynamic-slice_reduce_fusion = (f32[768,3,384]{2,1,0:T(4,128)S(1)}, f32[768,3,384]{2,1,0:T(4,128)}) fusion(f32[768,3,2,384]{3,2,1,0:T(2,128)} %reshape.114, s32[]{:T(128)S(6)} %select_n.32, s32[]{:T(128)S(6)} %select_n.31), kind=kLoop, calls=%fused_computation.16 | loop fusion | bytes 14155784 | tf_op jit(solution)/shard_map/jit(dynamic_index_in_dim)/dynamic_slice | solution.py:547
  118.7 60.1 %all-gather.7.cloned.1.call-done = f32[6144,768]{1,0:T(8,128)} async-done(((f32[384,768]{1,0:T(8,128)}), f32[6144,768]{1,0:T(8,128)}) %all-gather.7.cloned.1.call-update) | async-done | bytes 18874384 | tf_op jit(solution)/shard_map/all_gather | solution.py:533
  178.8 20.8 %fusion.72 = (f32[512]{0:T(512)S(1)}, f32[512,768]{1,0:T(8,128)S(1)}) fusion(f32[6144,768]{1,0:T(8,128)} %all-gather.7.cloned.1.call-done, f32[1,512,6144]{2,1,0:T(8,128)} %param.12), kind=kOutput, calls=%fused_computation.115 | convolution fusion | flops 14495907840 | bytes 33032192 | tf_op jit(solution)/shard_map/dot_general | solution.py:15
  209.1 48.1 %collective-permute-done.refs_3_.refs_4_.refs_5_ = f32[512,1152]{1,0:T(8,128)S(1)} collective-permute-done((f32[512,1152]{1,0:T(8,128)S(1)}, f32[512,1152]{1,0:T(8,128)S(1)}, u32[]{:S(2)}, u32[]{:S(2)}) %collective-permute-start) | collective-permute-done | bytes 2359328 | tf_op jit(solution)/shard_map/ppermute | solution.py:551
  258.5 30.2 %attend_forward.1 = (f32[512,384]{1,0:T(8,128)S(1)}, f32[512,384]{1,0:T(8,128)}, f32[1024,384]{1,0:T(8,128)S(1)}) custom-call(s32[1]{0:T(128)} %bitcast.1.pos_ref, s32[1024]{0:T(1024)S(1)} %bitcast.83, f32[512,1152]{1,0:T(8,128)S(1)} %fusion.33.refs_0_.refs_1_.refs_2_, f32[512,1152]{1,0:T(8,128)S(1)} %fusion.33.refs_0_.refs_1_.refs_2_, ...), custom_call_target="tpu_custom_call" | custom-call | flops 20000000000 | bytes 14155776 | tf_op jit(solution)/shard_map/attend_forward/pallas_call | solution.py:374
  291.3 12.3 collective-permute-done.1
  303.6 4.3 fusion.73
  309.4 12.7 %fusion.21 = f32[512,3072]{1,0:T(8,128)} fusion(f32[768,3072]{1,0:T(8,128)} %all-gather.13.cloned.1.call-done, f32[512,768]{1,0:T(8,128)} %copy-done.9, f32[768]{0:T(1024)S(1)} %get-tuple-element.71, f32[768]{0:T(1024)S(1)} %get-tuple-element.70, f32[512]{0:T(512)S(1)} %fusion.57, f32[512]{0:T(512)S(1)} %broadcast_multiply_fusion), kind=kOutput, calls=%fused_computation.41 | convolution fusion | flops 7249330176 | bytes 17311744 | tf_op jit(solution)/shard_map/dot_general | solution.py:15
  322.1 65.5 %all-gather.15.cloned.1.call-done = f32[3072,768]{1,0:T(8,128)} async-done(((f32[192,768]{1,0:T(8,128)}), f32[3072,768]{1,0:T(8,128)}) %all-gather.15.cloned.1.call-update) | async-done | bytes 9437200 | tf_op jit(solution)/shard_map/all_gather | solution.py:538
  387.6 14.6 %fusion.12 = f32[512,3072]{1,0:T(8,128)S(1)} fusion(f32[512,3072]{1,0:T(8,128)} %fusion.21, f32[3072,768]{1,0:T(8,128)} %all-gather.15.cloned.1.call-done, f32[1,512,768]{2,1,0:T(8,128)} %param.23), kind=kOutput, calls=%fused_computation.13 | convolution fusion | flops 7277641728 | bytes 23592960 | tf_op jit(solution)/shard_map/dot_general | solution.py:31
  402.2 8.6 multiply_reduce_fusion
  420.1 15.5 %collective-permute-done.2.refs_9_ = f32[512,384]{1,0:T(8,128)S(1)} collective-permute-done((f32[512,384]{1,0:T(8,128)S(1)}, f32[512,384]{1,0:T(8,128)S(1)}, u32[]{:S(2)}, u32[]{:S(2)}) %collective-permute-start.2) | collective-permute-done | bytes 786464 | tf_op jit(solution)/shard_map/ppermute | solution.py:574
  436.6 36.9 %attend_backward.1 = (f32[512,384]{1,0:T(8,128)}, f32[512,384]{1,0:T(8,128)}, f32[512,384]{1,0:T(8,128)}, f32[512,384]{1,0:T(8,128)}, f32[512,384]{1,0:T(8,128)}, /*index=5*/f32[512,384]{1,0:T(8,128)}) custom-call(s32[1]{0:T(128)} %bitcast.1.pos_ref, s32[1024]{0:T(1024)} %bitcast.80, f32[512,1152]{1,0:T(8,128)} %copy-done.2, f32[512,1152]{1,0:T(8,128)} %copy-done.2, ...), custom_call_target="tpu_custom_call" | custom-call | flops 40000000000 | bytes 23592960 | tf_op jit(solution)/shard_map/attend_backward/pallas_call | solution.py:492
  483.7 39.9 %collective-permute-done.3 = f32[512,1152]{1,0:T(8,128)} collective-permute-done((f32[512,1152]{1,0:T(8,128)}, f32[512,1152]{1,0:T(8,128)}, u32[]{:S(2)}, u32[]{:S(2)}) %collective-permute-start.3) | collective-permute-done | bytes 2359328 | tf_op jit(solution)/shard_map/ppermute | solution.py:578
  523.6 4.2 broadcast_select_fusion.1
  537.9 14.0 %fusion.31 = f32[768,2304]{1,0:T(8,128)} fusion(f32[512,2304]{0,1:T(8,128)S(1)} %bitcast.89, f32[512,768]{1,0:T(8,128)S(1)} %get-tuple-element.90, f32[768]{0:T(1024)S(1)} %get-tuple-element.72, f32[768]{0:T(1024)S(1)} %get-tuple-element.73, f32[512]{0:T(512)S(1)} %fusion.56, f32[512]{0:T(512)S(1)} %broadcast_multiply_fusion.1), kind=kOutput, calls=%fused_computation.53 | convolution fusion | flops 5437390848 | bytes 13379584 | tf_op jit(solution)/shard_map/dot_general | solution.py:21
  552.0 12.2 fusion.20
  564.3 14.4 %fusion.13 = f32[3072,768]{1,0:T(8,128)} fusion(f32[512,3072]{1,0:T(8,128)} %fusion.21, f32[1,512,768]{2,1,0:T(8,128)} %param.23), kind=kOutput, calls=%fused_computation.18 | convolution fusion | flops 7260340224 | bytes 17301504 | tf_op jit(solution)/shard_map/dot_general | solution.py:21
  578.8 6.2 fusion.74
  590.5 21.0 %fusion.4 = f32[6144,768]{0,1:T(8,128)} fusion(f32[1,512,6144]{2,1,0:T(8,128)} %param.12, f32[512,768]{1,0:T(8,128)S(1)} %copy-done.7, f32[512,768]{1,0:T(8,128)S(1)} %get-tuple-element.80, f32[512]{0:T(512)S(1)} %negate_multiply_fusion), kind=kOutput, calls=%fused_computation.4 | convolution fusion | flops 14496301056 | bytes 34605056 | tf_op jit(solution)/shard_map/dot_general | solution.py:21
  612.7 33.7 %reduce-scatter.11.cloned.1.call-done = f32[48,2304]{1,0:T(8,128)} async-done(((f32[768,2304]{1,0:T(8,128)}), f32[48,2304]{1,0:T(8,128)}) %reduce-scatter.11.cloned.1.call-update) | async-done | bytes 442384 | tf_op jit(solution)/shard_map/reduce_scatter | solution.py:591
  646.5 115.6 %reduce-scatter.15.cloned.1.call-done = f32[48,3072]{1,0:T(8,128)} async-done(((f32[768,3072]{1,0:T(8,128)}), f32[48,3072]{1,0:T(8,128)}) %reduce-scatter.15.cloned.1.call-update) | async-done | bytes 589840 | tf_op jit(solution)/shard_map/reduce_scatter | solution.py:591
  762.0 115.8 %reduce-scatter.17.cloned.1.call-done = f32[192,768]{1,0:T(8,128)} async-done(((f32[3072,768]{1,0:T(8,128)}), f32[192,768]{1,0:T(8,128)}) %reduce-scatter.17.cloned.1.call-update) | async-done | bytes 589840 | tf_op jit(solution)/shard_map/reduce_scatter | solution.py:591
  877.8 198.5 %reduce-scatter.9.cloned.1.call-done = f32[384,768]{0,1:T(8,128)} async-done(((f32[6144,768]{0,1:T(8,128)}), f32[384,768]{0,1:T(8,128)}) %reduce-scatter.9.cloned.1.call-update) | async-done | bytes 1179664 | tf_op jit(solution)/shard_map/reduce_scatter | solution.py:591
  1076.4 16.0 %add_bitcast_fusion = f32[1,512,768]{2,1,0:T(8,128)} fusion(f32[512,768]{1,0:T(8,128)S(1)} %copy-done.10, f32[3072,768]{1,0:T(8,128)} %all-gather.15.cloned.1.call-done, f32[512,3072]{1,0:T(8,128)} %fusion.21), kind=kOutput, calls=%fused_computation.33 | convolution fusion | flops 7260733440 | bytes 18874368 | tf_op jit(solution)/shard_map/dot_general | solution.py:15
  1092.4 20.5 %convolution_bitcast_fusion = f32[1,512,6144]{2,1,0:T(8,128)} fusion(f32[6144,768]{1,0:T(8,128)} %all-gather.7.cloned.1.call-done, f32[512,768]{1,0:T(8,128)S(1)} %copy-done.8, f32[512,768]{1,0:T(8,128)S(1)} %copy-done.20, f32[512]{0:T(512)S(1)} %negate_multiply_fusion), kind=kOutput, calls=%fused_computation.5 | convolution fusion | flops 14496301056 | bytes 34605056 | tf_op jit(solution)/shard_map/dot_general | solution.py:31
  1112.9 22.3 %reduce-scatter.19.cloned.1.call-done = f32[48,4]{1,0:T(8,128)} async-done(((f32[768,4]{1,0:T(8,128)}), f32[48,4]{1,0:T(8,128)}) %reduce-scatter.19.cloned.1.call-update) | async-done | bytes 784
  1136.0 4.9 psum.43
  1141.4 77.6 %all-reduce.3.cloned.1.call-done = (f32[384,768]{0,1:T(8,128)}, f32[48,2304]{1,0:T(8,128)}, f32[48,768]{1,0:T(8,128)}, f32[48,3072]{1,0:T(8,128)}, f32[192,768]{1,0:T(8,128)}) async-done(((f32[384,768]{0,1:T(8,128)}, f32[48,2304]{1,0:T(8,128)}, f32[48,768]{1,0:T(8,128)}, f32[48,3072]{1,0:T(8,128)}, f32[192,768]{1,0:T(8,128)}), (f32[384,768]{0,1:T(8,128)}, f32[48,2304]{1,0:T(8,128)}, f32[48,768]{1,0:T(8,128)}, ...) | async-done | bytes 2949136 | tf_op jit(solution)/shard_map/psum | solution.py:593
  (152 shorter events, 64.7 us)
Async XLA Ops:
  7.2 72.5 %all-gather.9.cloned.1.call-start = ((), (), s32[]{:S(2)}) async-start(), calls=%async_computation.7 | async-start | bytes 7520256 | tf_op jit(solution)/shard_map/all_gather | solution.py:535
  8.0 170.9 %all-gather.7.cloned.1.call-start = ((), (), s32[]{:S(2)}) async-start(), calls=%async_computation.6 | async-start | bytes 20054016 | tf_op jit(solution)/shard_map/all_gather | solution.py:533
  8.7 282.6 %all-gather.11.cloned.1.call-start = ((), (), s32[]{:S(2)}) async-start(), calls=%async_computation.8 | async-start | bytes 2506752 | tf_op jit(solution)/shard_map/all_gather | solution.py:536
  9.4 300.0 %all-gather.13.cloned.1.call-start = ((), (), s32[]{:S(2)}) async-start(), calls=%async_computation.9 | async-start | bytes 10027008 | tf_op jit(solution)/shard_map/all_gather | solution.py:537
  10.0 377.6 %all-gather.15.cloned.1.call-start = ((), (), s32[]{:S(2)}) async-start(), calls=%async_computation.10 | async-start | bytes 10027008 | tf_op jit(solution)/shard_map/all_gather | solution.py:538
  10.6 602.1 %reduce-scatter.13.cloned.1.call-start = ((), (), s32[]{:S(2)}) async-start(), calls=%async_computation.13 | async-start | bytes 2506752 | tf_op jit(solution)/shard_map/reduce_scatter | solution.py:591
  178.8 21.1 %copy-start.11 = (f32[96,8,3,384]{3,1,2,0:T(8,128)S(1)}, f32[96,8,3,384]{3,1,2,0:T(8,128)}, u32[]{:S(2)}) copy-start(f32[96,8,3,384]{3,1,2,0:T(8,128)} %copy.37) | copy-start | bytes 10616836
  199.9 5.3 copy-start.14
  203.7 53.5 %collective-permute-start = (f32[512,1152]{1,0:T(8,128)S(1)}, f32[512,1152]{1,0:T(8,128)S(1)}, u32[]{:S(2)}, u32[]{:S(2)}) collective-permute-start(f32[512,1152]{1,0:T(8,128)S(1)} %fusion.32), channel_id=1, source_target_pairs={{0,1},{1,0},{2,3},{3,2},{4,5},{5,4},{6,7},{7,6},{8,9},{9,8},{10,11... | collective-permute-start | bytes 7077896 | tf_op jit(solution)/shard_map/ppermute | solution.py:551
  205.5 51.7 %copy-start.4 = (s32[1,1024]{1,0:T(1,128)S(1)}, s32[1,1024]{1,0:T(1,128)}, u32[]{:S(2)}) copy-start(s32[1,1024]{1,0:T(1,128)} %param.13) | copy-start | bytes 12292
  209.1 79.7 %copy-start.2 = (f32[512,1152]{1,0:T(8,128)}, f32[512,1152]{1,0:T(8,128)S(1)}, u32[]{:S(2)}) copy-start(f32[512,1152]{1,0:T(8,128)S(1)} %fusion.33.refs_0_.refs_1_.refs_2_) | copy-start | bytes 7077892
  258.5 30.2 %copy-start.3 = (s32[1024,128]{1,0:T(8,128)}, s32[1024,128]{1,0:T(8,128)S(1)}, u32[]{:S(2)}) copy-start(s32[1024,128]{1,0:T(8,128)S(1)} %broadcast_in_dim.34.refs_6_.refs_11_) | copy-start | bytes 1572868
  289.9 18.0 %copy-start = (f32[512,384]{1,0:T(8,128)}, f32[512,384]{1,0:T(8,128)S(1)}, u32[]{:S(2)}) copy-start(f32[512,384]{1,0:T(8,128)S(1)} %get-tuple-element.20.refs_6_) | copy-start | bytes 2359300
  289.9 13.7 %collective-permute-start.1 = (f32[512,384]{1,0:T(8,128)}, f32[512,384]{1,0:T(8,128)S(1)}, u32[]{:S(2)}, u32[]{:S(2)}) collective-permute-start(f32[512,384]{1,0:T(8,128)} %get-tuple-element.21.refs_7_), channel_id=1, source_target_pairs={{0,1},{1,0},{2,3},{3,2},{4,5},{5,4},{6,7},{7,6},{8,9},{9,8},{10,11... | collective-permute-start | bytes 2359304 | tf_op jit(solution)/shard_map/ppermute | solution.py:554
  322.1 80.1 %copy-start.10 = (f32[512,768]{1,0:T(8,128)S(1)}, f32[512,768]{1,0:T(8,128)}, u32[]{:S(2)}) copy-start(f32[512,768]{1,0:T(8,128)} %copy-done.9) | copy-start | bytes 4718596
  387.6 14.6 %copy-start.17 = (f32[768,3072]{1,0:T(8,128)S(1)}, f32[768,3072]{1,0:T(8,128)}, u32[]{:S(2)}) copy-start(f32[768,3072]{1,0:T(8,128)} %all-gather.13.cloned.1.call-done) | copy-start | bytes 28311556
  402.2 8.6 copy-start.21
  412.5 65.8 %copy-start.6 = (f32[512,768]{1,0:T(8,128)}, f32[512,768]{1,0:T(8,128)S(1)}, u32[]{:S(2)}) copy-start(f32[512,768]{1,0:T(8,128)S(1)} %bitcast_add_fusion) | copy-start | bytes 4718596
  415.9 19.8 %collective-permute-start.2 = (f32[512,384]{1,0:T(8,128)S(1)}, f32[512,384]{1,0:T(8,128)S(1)}, u32[]{:S(2)}, u32[]{:S(2)}) collective-permute-start(f32[512,384]{1,0:T(8,128)S(1)} %fusion.22), channel_id=1, source_target_pairs={{0,1},{1,0},{2,3},{3,2},{4,5},{5,4},{6,7},{7,6},{8,9},{9,8},{10,11... | collective-permute-start | bytes 2359304 | tf_op jit(solution)/shard_map/ppermute | solution.py:574
  473.5 4.8 copy-start.1
  476.8 46.9 %collective-permute-start.3 = (f32[512,1152]{1,0:T(8,128)}, f32[512,1152]{1,0:T(8,128)}, u32[]{:S(2)}, u32[]{:S(2)}) collective-permute-start(f32[512,1152]{1,0:T(8,128)} %pad_maximum_fusion.1), channel_id=1, source_target_pairs={{0,1},{1,0},{2,3},{3,2},{4,5},{5,4},{6,7},{7,6},{8,9},{9,8},{10,11... | collective-permute-start | bytes 7077896 | tf_op jit(solution)/shard_map/ppermute | solution.py:578
  482.0 164.5 %reduce-scatter.11.cloned.1.call-start = ((), (), s32[]{:S(2)}) async-start(), calls=%async_computation.12 | async-start | bytes 7520256 | tf_op jit(solution)/shard_map/reduce_scatter | solution.py:591
  483.7 44.2 %copy-start.15 = (f32[512,1152]{1,0:T(8,128)}, f32[512,1152]{1,0:T(8,128)S(1)}, u32[]{:S(2)}) copy-start(f32[512,1152]{1,0:T(8,128)S(1)} %constant_dynamic-update-slice_fusion) | copy-start | bytes 7077892
  552.0 210.1 %reduce-scatter.15.cloned.1.call-start = ((), (), s32[]{:S(2)}) async-start(), calls=%async_computation.14 | async-start | bytes 10027008 | tf_op jit(solution)/shard_map/reduce_scatter | solution.py:591
  564.3 313.6 %reduce-scatter.17.cloned.1.call-start = ((), (), s32[]{:S(2)}) async-start(), calls=%async_computation.15 | async-start | bytes 10027008 | tf_op jit(solution)/shard_map/reduce_scatter | solution.py:591
  578.8 497.6 %reduce-scatter.9.cloned.1.call-start = ((), (), s32[]{:S(2)}) async-start(), calls=%async_computation.11 | async-start | bytes 20054016 | tf_op jit(solution)/shard_map/reduce_scatter | solution.py:591
  578.8 6.2 copy-start.13
  578.8 6.2 copy-start.16
  611.6 523.6 %reduce-scatter.19.cloned.1.call-start = ((), (), s32[]{:S(2)}) async-start(), calls=%async_computation.16 | async-start | bytes 417792
  612.7 606.4 %all-reduce.3.cloned.1.call-start = ((), (), s32[]{:S(2)}) async-start(), calls=%async_computation.17 | async-start | bytes 5898240 | tf_op jit(solution)/shard_map/psum | solution.py:593
  1076.4 16.0 %copy-start.8 = (f32[512,768]{1,0:T(8,128)S(1)}, f32[512,768]{1,0:T(8,128)}, u32[]{:S(2)}) copy-start(f32[512,768]{1,0:T(8,128)} %copy-done.6) | copy-start | bytes 4718596
  1076.4 16.0 %copy-start.20 = (f32[512,768]{1,0:T(8,128)S(1)}, f32[512,768]{1,0:T(8,128)}, u32[]{:S(2)}) copy-start(f32[512,768]{1,0:T(8,128)} %copy-done.19) | copy-start | bytes 4718596
  (21 other events, 53.5 us)
Sparse Core Ops, SparseCore 0:
  10.3 69.3 all-gather.8
  81.3 97.4 all-gather.6
  181.1 42.2 all-gather.10
  225.6 80.2 all-gather.12
  308.0 79.5 all-gather.14
  482.1 60.1 reduce-scatter.12
  552.1 94.3 reduce-scatter.10
  651.1 110.8 reduce-scatter.14
  766.7 111.0 reduce-scatter.16
  881.8 194.5 reduce-scatter.8
  1080.4 54.6 reduce-scatter.18
  1137.8 81.1 all-reduce.2

commit v2 on v1

--- a/solution.py
+++ b/solution.py
@@ -1,3 +1,5 @@
+import functools
+
 import jax
 import jax.numpy as jnp
 from jax import lax
@@ -521,6 +523,362 @@
     return outs
 
 
+MESH = pl.DeviceIdType.MESH
+PIECE = 48
+
+
+def scatter_kernel(plan, *refs):
+    count = len(plan)
+    units = sum(plan)
+    pairs = units // 2
+    turned, grads = refs[:count], refs[count:2 * count]
+    stream_ref, weight_ref, norms_ref, extra_ref = refs[2 * count:2 * count + 4]
+    total_ref, patch_ref, norm_total_ref, extra_total_ref = refs[2 * count + 4:2 * count + 8]
+    (t_buf, g_buf, g_high, g_low, part, s_high, s_low, w_buf, p_buf, land_a, n_x, n_z, n_y, y_y, y_x, y_z, done,
+     v_c, v_x, v_y, v_z, extra_in,
+     load_sem, w_sem, p_sem, a_sem, nx_sem, nz_sem, ny_sem, yy_sem, yx_sem, yz_sem, ye_sem, v_sem, o_sem) = refs[2 * count + 8:]
+    fsdp = lax.axis_index("fsdp")
+    row = lax.axis_index("sp")
+    z, x, core = fsdp // 4, (fsdp // 2) % 2, fsdp % 2
+    half = PIECE // 2
+
+    def device(z_at, x_at, core_at, row_at):
+        return ((z_at * 2 + x_at) * 2 + core_at, row_at)
+
+    sibling = device(z, x, 1 - core, row)
+    beside = device(z, 1 - x, core, row)
+    across = device(z, x, core, 1 - row)
+    along = [device((z + step) % 4, x, core, row) for step in (1, 2, 3)]
+
+    barrier = pltpu.get_barrier_semaphore()
+    for peer in [sibling, beside, across] + along:
+        pl.semaphore_signal(barrier, inc=1, device_id=peer, device_id_type=MESH)
+
+    def remote(source, target, sems, index, peer):
+        return pltpu.make_async_remote_copy(
+            src_ref=source, dst_ref=target, send_sem=sems.at[(0,) + index], recv_sem=sems.at[(1,) + index],
+            device_id=peer, device_id_type=MESH,
+        )
+
+    def loads(unit, slot, act):
+        base = 0
+        for which in range(count):
+            first, last = base, base + plan[which]
+            base = last
+
+            @pl.when((unit >= first) & (unit < last))
+            def _(which=which, first=first):
+                j = unit - first
+                for side in range(2):
+                    rows_ref = turned[which]
+                    source = rows_ref.at[:, side, j] if rows_ref.shape[2] > 1 else rows_ref.at[:, side, 0]
+                    act(pltpu.make_async_copy(source, t_buf.at[slot, side], load_sem.at[slot, side]))
+                grad = grads[which]
+                width = g_buf.shape[2]
+                if grad.shape[1] > width:
+                    grad = grad.at[:, pl.ds(pl.multiple_of(j * width, width), width)]
+                act(pltpu.make_async_copy(grad, g_buf.at[slot], load_sem.at[slot, 2]))
+
+    def start(copy):
+        copy.start()
+
+    def wait(copy):
+        copy.wait()
+
+    def weight_copy(block, slot):
+        return pltpu.make_async_copy(weight_ref.at[block], w_buf.at[slot], w_sem.at[slot])
+
+    def patch_copy(block, slot):
+        columns = w_buf.shape[1]
+        return pltpu.make_async_copy(
+            p_buf.at[slot], patch_ref.at[:, pl.ds(pl.multiple_of(block * columns, columns), columns)], p_sem.at[slot]
+        )
+
+    def core_copy(unit, slot):
+        return remote(part.at[slot, 1 - core], land_a.at[unit], a_sem, (unit,), sibling)
+
+    def nx_copy(p):
+        return remote(land_a.at[2 * p, :, 1 - x], n_x.at[p], nx_sem, (p,), beside)
+
+    def nz_copy(p, step):
+        return remote(n_x.at[p, (z + step + 1) % 4], n_z.at[p, step], nz_sem, (p, step), along[step])
+
+    def ny_copy(p):
+        return remote(n_x.at[p, z], n_y.at[p], ny_sem, (p,), across)
+
+    def yy_copy(p):
+        return remote(
+            land_a.at[2 * p + 1, :, :, pl.ds(pl.multiple_of((1 - row) * half, half), half)], y_y.at[p], yy_sem, (p,), across
+        )
+
+    def yx_copy(p):
+        return remote(y_y.at[p, :, 1 - x], y_x.at[p], yx_sem, (p,), beside)
+
+    def yz_copy(p, step):
+        return remote(y_x.at[p, (z + step + 1) % 4], y_z.at[p, step], yz_sem, (p, step), along[step])
+
+    def ye_copy(p):
+        place = pl.ds(pl.multiple_of(row * half, half), half)
+        return remote(y_x.at[p, z], done.at[2 * p + 1, place], ye_sem, (p,), across)
+
+    loads(0, 0, start)
+    weight_copy(0, 0).start()
+    s_high[...] = stream_ref[...].astype(BF)
+    s_low[...] = (stream_ref[...] - s_high[...].astype(F32)).astype(BF)
+    pl.semaphore_wait(barrier, 6)
+
+    v_copies = [
+        remote(norms_ref, v_c, v_sem, (0,), sibling),
+        remote(v_c, v_x, v_sem, (1,), beside),
+        remote(v_x, v_y, v_sem, (2,), across),
+    ] + [remote(v_y, v_z.at[step], v_sem, (3 + step,), along[step]) for step in range(3)]
+    v_copies[0].start()
+    extra_copy = remote(extra_ref, extra_in, v_sem, (6,), across)
+    extra_copy.start()
+
+    def compute(unit, slot):
+        loads(unit, slot, wait)
+
+        @pl.when(unit + 1 < units)
+        def _():
+            loads(unit + 1, 1 - slot, start)
+
+        @pl.when(unit >= 2)
+        def _():
+            core_copy(unit - 2, slot).wait_send()
+
+        grad = g_buf[slot]
+        g_high[...] = grad.astype(BF)
+        g_low[...] = (grad - g_high[...].astype(F32)).astype(BF)
+
+        def side_of(turn, carry):
+            side = jnp.where(turn == 0, 1 - core, core)
+            high, low = split_bf(t_buf[slot, side].reshape(8 * PIECE, t_buf.shape[4]))
+            product = nn(high, g_high[...]) + nn(high, g_low[...]) + nn(low, g_high[...])
+            part[slot, side] = product.reshape(4, 2, PIECE, product.shape[1])
+
+            @pl.when(turn == 0)
+            def _():
+                core_copy(unit, slot).start()
+
+            return carry
+
+        lax.fori_loop(0, 2, side_of, 0)
+
+    def patch_block(block, slot):
+        weight_copy(block, slot).wait()
+
+        @pl.when(block + 1 < weight_ref.shape[0])
+        def _():
+            weight_copy(block + 1, 1 - slot).start()
+
+        @pl.when(block >= 2)
+        def _():
+            patch_copy(block - 2, slot).wait()
+
+        high, low = split_bf(w_buf[slot])
+        p_buf[slot] = nt(s_high[...], high) + nt(s_high[...], low) + nt(s_low[...], high)
+        patch_copy(block, slot).start()
+
+    def loop(number, body):
+        def step(i, carry):
+            body(i)
+            return carry
+
+        lax.fori_loop(0, number, step, 0)
+
+    def after_core(unit, slot):
+        core_copy(unit, slot).wait_recv()
+
+        def add(i):
+            for b in range(2):
+                land_a[unit, i, b] = land_a[unit, i, b] + part[slot, core, i, b]
+
+        loop(4, add)
+
+    def iteration(p, carry):
+        @pl.when(p < pairs)
+        def _():
+            compute(2 * p, 0)
+            compute(2 * p + 1, 1)
+            after_core(2 * p, 0)
+            nx_copy(p).start()
+            after_core(2 * p + 1, 1)
+            yy_copy(p).start()
+
+        q = p - 1
+
+        @pl.when((q >= 0) & (q < pairs))
+        def _():
+            nx_copy(q).wait_recv()
+
+            def add_n(i):
+                n_x[q, i] = n_x[q, i] + land_a[2 * q, i, x]
+
+            loop(4, add_n)
+            for step in range(3):
+                nz_copy(q, step).start()
+            yy_copy(q).wait_recv()
+            own = pl.ds(pl.multiple_of(row * half, half), half)
+
+            def add_y(i):
+                for b in range(2):
+                    y_y[q, i, b] = y_y[q, i, b] + land_a[2 * q + 1, i, b, own]
+
+            loop(4, add_y)
+            yx_copy(q).start()
+
+        @pl.when(p < pairs)
+        def _():
+            patch_block(2 * p, 0)
+            patch_block(2 * p + 1, 1)
+
+        r = p - 2
+
+        @pl.when((r >= 0) & (r < pairs))
+        def _():
+            for step in range(3):
+                nz_copy(r, step).wait_recv()
+            n_x[r, z] = n_x[r, z] + n_z[r, 0] + n_z[r, 1] + n_z[r, 2]
+            ny_copy(r).start()
+            yx_copy(r).wait_recv()
+
+            def add_x(i):
+                y_x[r, i] = y_x[r, i] + y_y[r, i, x]
+
+            loop(4, add_x)
+            for step in range(3):
+                yz_copy(r, step).start()
+
+        s = p - 3
+
+        @pl.when((s >= 0) & (s < pairs))
+        def _():
+            ny_copy(s).wait_recv()
+            done[2 * s] = n_x[s, z] + n_y[s]
+            for step in range(3):
+                yz_copy(s, step).wait_recv()
+            total = y_x[s, z] + y_z[s, 0] + y_z[s, 1] + y_z[s, 2]
+            y_x[s, z] = total
+            done[2 * s + 1, pl.ds(pl.multiple_of(row * half, half), half)] = total
+            ye_copy(s).start()
+
+        @pl.when(p == 0)
+        def _():
+            v_copies[0].wait_recv()
+            v_c[...] = v_c[...] + norms_ref[...]
+            v_copies[1].start()
+
+        @pl.when(p == 1)
+        def _():
+            v_copies[1].wait_recv()
+            v_x[...] = v_x[...] + v_c[...]
+            v_copies[2].start()
+
+        @pl.when(p == 2)
+        def _():
+            v_copies[2].wait_recv()
+            v_y[...] = v_y[...] + v_x[...]
+            for step in range(3):
+                v_copies[3 + step].start()
+
+        @pl.when(p == 3)
+        def _():
+            for step in range(3):
+                v_copies[3 + step].wait_recv()
+            norm_total_ref[...] = v_y[...] + v_z[0] + v_z[1] + v_z[2]
+            extra_copy.wait_recv()
+            extra_total_ref[...] = extra_ref[...] + extra_in[...]
+
+        return carry
+
+    lax.fori_loop(0, pairs + 3, iteration, 0)
+
+    def finish(p):
+        ye_copy(p).wait()
+        nx_copy(p).wait_send()
+        ny_copy(p).wait_send()
+        yy_copy(p).wait_send()
+        yx_copy(p).wait_send()
+        for step in range(3):
+            nz_copy(p, step).wait_send()
+            yz_copy(p, step).wait_send()
+
+    loop(pairs, finish)
+    out = pltpu.make_async_copy(done, total_ref, o_sem)
+    out.start()
+    for copy in v_copies + [extra_copy]:
+        copy.wait_send()
+    core_copy(units - 2, 0).wait_send()
+    core_copy(units - 1, 1).wait_send()
+    blocks = weight_ref.shape[0]
+    patch_copy(blocks - 2, 0).wait()
+    patch_copy(blocks - 1, 1).wait()
+    out.wait()
+
+
+def reduce_gradients(turned, grads, grad_stream, weight, norms, extra):
+    rows, width = grad_stream.shape
+    plan, views = [], []
+    for left, right in zip(turned, grads):
+        tall = left.shape[0] // (16 * PIECE)
+        plan.append(tall * (right.shape[1] // width))
+        views.append(left.reshape(8, 2, tall, PIECE, rows))
+    units = sum(plan)
+    pairs = units // 2
+    owners = 16
+    block = weight.shape[0] // owners
+    half = PIECE // 2
+    dma = pltpu.SemaphoreType.DMA
+    any_space = pl.BlockSpec(memory_space=pl.ANY)
+    vmem = pl.BlockSpec(memory_space=pltpu.VMEM)
+    flops = 6 * rows * width * (units * 16 * PIECE + weight.shape[0])
+    return pl.pallas_call(
+        functools.partial(scatter_kernel, tuple(plan)),
+        out_shape=[
+            jax.ShapeDtypeStruct((units, PIECE, width), F32),
+            jax.ShapeDtypeStruct((rows, weight.shape[0]), F32),
+            jax.ShapeDtypeStruct(norms.shape, F32),
+            jax.ShapeDtypeStruct(extra.shape, F32),
+        ],
+        in_specs=[any_space] * (2 * len(plan)) + [vmem, any_space, vmem, vmem],
+        out_specs=[any_space, any_space, vmem, vmem],
+        scratch_shapes=[
+            pltpu.VMEM((2, 2, 8, PIECE, rows), F32),
+            pltpu.VMEM((2, rows, width), F32),
+            pltpu.VMEM((rows, width), BF),
+            pltpu.VMEM((rows, width), BF),
+            pltpu.VMEM((2, 2, 4, 2, PIECE, width), F32),
+            pltpu.VMEM((rows, width), BF),
+            pltpu.VMEM((rows, width), BF),
+            pltpu.VMEM((2, block, width), F32),
+            pltpu.VMEM((2, rows, block), F32),
+            pltpu.VMEM((units, 4, 2, PIECE, width), F32),
+            pltpu.VMEM((pairs, 4, PIECE, width), F32),
+            pltpu.VMEM((pairs, 3, PIECE, width), F32),
+            pltpu.VMEM((pairs, PIECE, width), F32),
+            pltpu.VMEM((pairs, 4, 2, half, width), F32),
+            pltpu.VMEM((pairs, 4, half, width), F32),
+            pltpu.VMEM((pairs, 3, half, width), F32),
+            pltpu.VMEM((units, PIECE, width), F32),
+            pltpu.VMEM(norms.shape, F32),
+            pltpu.VMEM(norms.shape, F32),
+            pltpu.VMEM(norms.shape, F32),
+            pltpu.VMEM((3,) + norms.shape, F32),
+            pltpu.VMEM(extra.shape, F32),
+            dma((2, 3)), dma((2,)), dma((2,)),
+            dma((2, units)), dma((2, pairs)), dma((2, pairs, 3)), dma((2, pairs)),
+            dma((2, pairs)), dma((2, pairs)), dma((2, pairs, 3)), dma((2, pairs)),
+            dma((2, 7)), dma,
+        ],
+        cost_estimate=pl.CostEstimate(flops=flops, bytes_accessed=120 * 10**6, transcendentals=0),
+        compiler_params=pltpu.CompilerParams(
+            collective_id=0, has_side_effects=True, vmem_limit_bytes=67043328
+        ),
+        name="reduce_gradients",
+    )(*views, *grads, grad_stream, weight.reshape(owners, block, width), norms, extra)
+
+
 def fast_shards(
     patches, segments, w_in, norm1_gain, norm1_bias, w_qkv, w_out, norm2_gain, norm2_bias, w_up, w_down, cotangent
 ):
@@ -564,11 +922,11 @@
     block_out = residual + matmul(hidden, down_full)
     grad_rows = cotangent[0]
     grad_down = matmul_tn(hidden, grad_rows)
-    (grad_pre,) = gelu_pull(matmul_nt(grad_rows, down_full))
-    grad_up = matmul_tn(normed_two, grad_pre)
+    down_part = lax.psum_scatter(grad_down, "fsdp", scatter_dimension=0, tiled=True)
+    later_rows, _ = lax.optimization_barrier((grad_rows, grad_down))
+    (grad_pre,) = gelu_pull(matmul_nt(later_rows, down_full))
     grad_resid_norm, grad_gain_two, grad_offset_two = norm2_pull(matmul_nt(grad_pre, up_full))
     grad_resid = grad_rows + grad_resid_norm
-    grad_out = matmul_tn(attended_rows, grad_resid)
     out_by_half = out_full.reshape(2, half, width)
     grad_sent = matmul_nt(grad_resid, lax.dynamic_index_in_dim(out_by_half, 1 - position, 0, keepdims=False))
     grad_in = lax.ppermute(grad_sent, "sp", swap)
@@ -577,34 +935,26 @@
     mine = jnp.concatenate(parts[:3], axis=1)
     theirs = lax.ppermute(jnp.concatenate(parts[3:], axis=1), "sp", swap)
     grad_normed = matmul_nt(mine, own_columns) + matmul_nt(theirs, sent_columns)
-    grad_proj = whole_rows(mine.reshape(rows, 3, half), theirs.reshape(rows, 3, half))
     low = jnp.where(position == 0, mine, theirs).reshape(rows, 3, 1, half)
     high = jnp.where(position == 0, theirs, mine).reshape(rows, 3, 1, half)
     grad_proj = jnp.concatenate([low, high], axis=2).reshape(rows, 3 * width)
-    grad_qkv = matmul_tn(normed, grad_proj)
     grad_stream_norm, grad_gain_one, grad_offset_one = norm1_pull(grad_normed)
     grad_stream = grad_resid + grad_stream_norm
-    grad_w_in = matmul_tn(patch_rows, grad_stream)
-    grad_patch = matmul_nt(grad_stream, in_full)
-
-    def scattered(value, dimension=0):
-        return lax.psum_scatter(value, "fsdp", scatter_dimension=dimension, tiled=True)
-
-    totals = lax.psum(
-        (
-            scattered(grad_w_in),
-            scattered(grad_qkv),
-            scattered(grad_out),
-            scattered(grad_up),
-            scattered(grad_down),
-            scattered(jnp.stack([grad_gain_one, grad_offset_one, grad_gain_two, grad_offset_two]), 1),
-        ),
-        "sp",
-    )
-    norms = totals[5]
+    vectors = jnp.stack([grad_gain_one, grad_offset_one, grad_gain_two, grad_offset_two] + [jnp.zeros_like(grad_gain_one)] * 4)
+    pieces, grad_patch, vector_sums, total_down = reduce_gradients(
+        [normed_two.T, attended_rows.T, normed.T, patch_rows.T],
+        [grad_pre, grad_resid, grad_proj, grad_stream],
+        grad_stream, in_full, vectors, down_part,
+    )
+    own_part = w_out.shape[0]
+    vector_sums = lax.dynamic_slice(vector_sums, (0, lax.axis_index("fsdp") * own_part), (4, own_part))
+
+    def across(first, last):
+        return jnp.concatenate([pieces[i] for i in range(first, last)], axis=1)
+
     return (
-        block_out[None], grad_patch[None], totals[0], norms[0], norms[1], totals[1], totals[2], norms[2], norms[3],
-        totals[3], totals[4],
+        block_out[None], grad_patch[None], pieces[8:16].reshape(8 * PIECE, width), vector_sums[0], vector_sums[1],
+        across(5, 8), pieces[4], vector_sums[2], vector_sums[3], across(0, 4), total_down,
     )
 
 

time: 1240 us -> 807 us (0.65)
  waiting for transfers between devices: 854 us -> 251 us
  Pallas kernels: 67.1 us -> 256 us
  matrix products: 184 us -> 113 us
  local copies, waits for them, and re-layouts: 64.8 us -> 110 us
    reduce_scatter x5 -> x1, waiting for transfers between devices: 464 us -> 0.01 us  [fast_shards(): lax.psum_scatter(grad_down, 'fsdp', scatter_dimension=0, tiled=True)]
    pallas_call x0 -> x1, Pallas kernels: none -> 189 us  [reduce_gradients(): pl.pallas_call(functools.partial(scatter_kernel, tuple(plan)), out_shape=...]
    psum x1 -> x0, waiting for transfers between devices: 77.6 us -> none  [fast_shards(): lax.psum((scattered(grad_w_in), scattered(grad_qkv), scattered(grad_out),...]
    dot_general x5 -> x1, matrix products: 65.4 us -> 11.6 us  [matmul_tn(): lax.dot_general(left_side, right_side, (((0,), (0,)), ((), ())), precisio...]
    ppermute x1, waiting for transfers between devices: 39.9 us -> 14 us  [fast_shards(): theirs = lax.ppermute(jnp.concatenate(parts[3:], axis=1), 'sp', swap)]
    unnamed x13 -> x6, waiting for transfers between devices: 25.5 us -> 3.13 us
    all_gather x1, waiting for transfers between devices: 65.5 us -> 47.4 us  [fast_shards(): down_full = lax.all_gather(w_down, 'fsdp', axis=0, tiled=True)]
    dot_general x7 -> x6, matrix products: 57.6 us -> 41.3 us  [matmul_nt(): lax.dot_general(left_side, right_side, (((1,), (1,)), ((), ())), precisio...]
  transfers between devices with their start and end apart: 16 -> 10, of which waited for: 13 -> 7; matrix products, arithmetic and copies ran while one was open for 18% -> 27% of each run, Pallas kernels for 2% -> 8%
where the time goes in v2:
time: 807 us; the launch traced here: 797 us
  Pallas kernels  256 us (32%)
  waiting for transfers between devices  251 us (31%)
  matrix products  113 us (14%)
  local copies, waits for them, and re-layouts  110 us (14%)
  blocking collectives  23.5 us (3%)
  other arithmetic  22.4 us (3%)
  between operations  15.1 us (2%)
    pallas_call x1, Pallas kernels, reduce_gradients(): pl.pallas_call(functools.partial(scatter_kernel, tuple(plan)), out_shape=...  189 us
    all_gather x1, waiting for transfers between devices, fast_shards(): in_full = lax.all_gather(w_in, 'fsdp', axis=0, tiled=True)  59.9 us
    dot_general x6, matrix products, matmul(): jnp.dot(left_side, right_side, precision=lax.Precision.HIGH, preferred_el...  59.7 us
    ppermute x1, waiting for transfers between devices, fast_shards(): received = lax.ppermute(matmul(normed, sent_columns), 'sp', swap)  47.9 us
    all_gather x1, waiting for transfers between devices, fast_shards(): down_full = lax.all_gather(w_down, 'fsdp', axis=0, tiled=True)  47.4 us
    all_gather x1, waiting for transfers between devices, fast_shards(): qkv_full = lax.all_gather(w_qkv, 'fsdp', axis=0, tiled=True)  45.4 us
    dot_general x6, matrix products, matmul_nt(): lax.dot_general(left_side, right_side, (((1,), (1,)), ((), ())), precisio...  41.3 us
    pallas_call x1, Pallas kernels, attend_backward(): pl.pallas_call(backward_kernel, grid_spec=pltpu.PrefetchScalarGridSpec(nu...  36.9 us
  transfers between devices with their start and end apart: 10, of which 7 were waited for; matrix products, arithmetic and copies ran while one was open for 27% of the time, Pallas kernels for 8%

profile of v2, /device:TPU:0, one launch (start us, length us, event | category | flops | bytes accessed | tf_op | source)
XLA Modules:
  0.0 797.3 jit_solution(17691956909169049367)
XLA Ops:
  10.7 23.5 %all-gather = f32[16,48,4]{1,2,0:T(4,128)S(1)} all-gather(f32[1,48,4]{1,2,0:T(4,128)S(1)} %maximum_bitcast_fusion), channel_id=1, replica_groups=mesh['fsdp'=16,'sp'=2] {'fsdp'}, dimensions={0}, use_global_device_ids=true | all-gather | bytes 13056 | tf_op jit(solution)/shard_map/all_gather | solution.py:892
  34.3 45.4 %all-gather.9.cloned.1.call-done = f32[768,2304]{1,0:T(8,128)} async-done(((f32[48,2304]{1,0:T(8,128)}), f32[768,2304]{1,0:T(8,128)}) %all-gather.9.cloned.1.call-update) | async-done | bytes 7077904 | tf_op jit(solution)/shard_map/all_gather | solution.py:893
  79.7 9.3 %reshape.132 = f32[768,3,2,384]{3,2,1,0:T(2,128)} reshape(f32[768,2304]{1,0:T(8,128)} %all-gather.9.cloned.1.call-done) | data formatting | bytes 14155776 | tf_op jit(solution)/shard_map/reshape | solution.py:901
  89.0 27.8 %dynamic-slice_reduce_fusion = (f32[768,3,384]{2,1,0:T(4,128)S(1)}, f32[768,3,384]{2,1,0:T(4,128)}) fusion(f32[768,3,2,384]{3,2,1,0:T(2,128)} %reshape.132, s32[]{:T(128)S(6)} %select_n.35, s32[]{:T(128)S(6)} %select_n.34), kind=kLoop, calls=%fused_computation.12 | loop fusion | bytes 14155784 | tf_op jit(solution)/shard_map/jit(dynamic_index_in_dim)/dynamic_slice | solution.py:905
  118.9 59.9 %all-gather.7.cloned.1.call-done = f32[6144,768]{1,0:T(8,128)} async-done(((f32[384,768]{1,0:T(8,128)}), f32[6144,768]{1,0:T(8,128)}) %all-gather.7.cloned.1.call-update) | async-done | bytes 18874384 | tf_op jit(solution)/shard_map/all_gather | solution.py:891
  178.8 20.7 %fusion.52 = (f32[512]{0:T(512)S(1)}, f32[512,768]{1,0:T(8,128)S(1)}) fusion(f32[6144,768]{1,0:T(8,128)} %all-gather.7.cloned.1.call-done, f32[1,512,6144]{2,1,0:T(8,128)} %param.12), kind=kOutput, calls=%fused_computation.108 | convolution fusion | flops 14495907840 | bytes 33032192 | tf_op jit(solution)/shard_map/dot_general | solution.py:17
  199.9 3.8 fusion.21
  205.5 3.7 fusion.22.refs_0_.refs_1_.refs_2_
  209.2 47.9 %collective-permute-done.refs_3_.refs_4_.refs_5_ = f32[512,1152]{1,0:T(8,128)S(1)} collective-permute-done((f32[512,1152]{1,0:T(8,128)S(1)}, f32[512,1152]{1,0:T(8,128)S(1)}, u32[]{:S(2)}, u32[]{:S(2)}) %collective-permute-start) | collective-permute-done | bytes 2359328 | tf_op jit(solution)/shard_map/ppermute | solution.py:909
  258.5 30.0 %attend_forward.1 = (f32[512,384]{1,0:T(8,128)S(1)}, f32[512,384]{1,0:T(8,128)}, f32[1024,384]{1,0:T(8,128)S(1)}) custom-call(s32[1]{0:T(128)} %bitcast.1.pos_ref, s32[1024]{0:T(1024)S(1)} %bitcast.100, f32[512,1152]{1,0:T(8,128)S(1)} %fusion.22.refs_0_.refs_1_.refs_2_, f32[512,1152]{1,0:T(8,128)S(1)} %fusion.22.refs_0_.refs_1_.refs_2_, ...), custom_call_target="tpu_custom_call" | custom-call | flops 20000000000 | bytes 14155776 | tf_op jit(solution)/shard_map/attend_forward/pallas_call | solution.py:376
  291.1 17.6 %collective-permute-done.1 = f32[512,384]{1,0:T(8,128)S(1)} collective-permute-done((f32[512,384]{1,0:T(8,128)}, f32[512,384]{1,0:T(8,128)S(1)}, u32[]{:S(2)}, u32[]{:S(2)}) %collective-permute-start.1) | collective-permute-done | bytes 786464 | tf_op jit(solution)/shard_map/ppermute | solution.py:912
  308.8 4.2 fusion.53
  314.5 11.4 %fusion.11 = f32[512,3072]{1,0:T(8,128)S(1)} fusion(f32[768,3072]{1,0:T(8,128)} %all-gather.13.cloned.1.call-done, f32[512,768]{1,0:T(8,128)} %copy-done.10, f32[768]{0:T(1024)S(1)} %get-tuple-element.48, f32[768]{0:T(1024)S(1)} %get-tuple-element.47, f32[512]{0:T(512)S(1)} %fusion.37, f32[512]{0:T(512)S(1)} %broadcast_multiply_fusion), kind=kOutput, calls=%fused_computation.34 | convolution fusion | flops 7249330176 | bytes 17311744 | tf_op jit(solution)/shard_map/dot_general | solution.py:17
  328.5 11.6 %fusion.8 = f32[3072,768]{1,0:T(8,128)} fusion(f32[512,3072]{1,0:T(8,128)S(1)} %fusion.11, f32[1,512,768]{2,1,0:T(8,128)S(1)} %copy-done.25), kind=kOutput, calls=%fused_computation.14 | convolution fusion | flops 7260340224 | bytes 17301504 | tf_op jit(solution)/shard_map/dot_general | solution.py:23
  340.1 47.4 %all-gather.15.cloned.1.call-done = f32[3072,768]{1,0:T(8,128)} async-done(((f32[192,768]{1,0:T(8,128)}), f32[3072,768]{1,0:T(8,128)}) %all-gather.15.cloned.1.call-update) | async-done | bytes 9437200 | tf_op jit(solution)/shard_map/all_gather | solution.py:896
  387.6 14.5 %fusion.7.refs_4_ = f32[512,3072]{1,0:T(8,128)S(1)} fusion(f32[512,3072]{1,0:T(8,128)} %copy-done.20, f32[512,768]{1,0:T(8,128)} %bitcast.118, f32[3072,768]{1,0:T(8,128)} %all-gather.15.cloned.1.call-done), kind=kOutput, calls=%fused_computation.9 | convolution fusion | flops 7277641728 | bytes 23592960 | tf_op jit(solution)/shard_map/dot_general | solution.py:33
  402.1 14.1 %multiply_reduce_fusion = (f32[768]{0:T(1024)S(1)}, f32[512]{0:T(512)S(1)}, f32[768]{0:T(1024)S(1)}, f32[512,768]{1,0:T(8,128)S(1)}) fusion(f32[512,768]{1,0:T(8,128)S(1)} %copy-done.11, f32[512]{0:T(512)S(1)} %fusion.37, f32[512]{0:T(512)S(1)} %broadcast_multiply_fusion, f32[768]{0:T(1024)S(1)} %get-tuple-element.47, f32[512,3072]{1,0:T(8,128)S(1)} %fusion.7.refs_4_, ...), kind=kOutput, calls=%fused_computation.20 | convolution fusion | flops 7250900992 | bytes 18889728 | tf_op jit(solution)/shard_map/dot_general | solution.py:33
  425.6 15.9 %collective-permute-done.2.refs_9_ = f32[512,384]{1,0:T(8,128)S(1)} collective-permute-done((f32[512,384]{1,0:T(8,128)S(1)}, f32[512,384]{1,0:T(8,128)S(1)}, u32[]{:S(2)}, u32[]{:S(2)}) %collective-permute-start.2) | collective-permute-done | bytes 786464 | tf_op jit(solution)/shard_map/ppermute | solution.py:932
  442.4 36.9 %attend_backward.1 = (f32[512,384]{1,0:T(8,128)}, f32[512,384]{1,0:T(8,128)}, f32[512,384]{1,0:T(8,128)}, f32[512,384]{1,0:T(8,128)}, f32[512,384]{1,0:T(8,128)}, /*index=5*/f32[512,384]{1,0:T(8,128)}) custom-call(s32[1]{0:T(128)} %bitcast.1.pos_ref, s32[1024]{0:T(1024)} %bitcast.97, f32[512,1152]{1,0:T(8,128)} %copy-done.2, f32[512,1152]{1,0:T(8,128)} %copy-done.2, ...), custom_call_target="tpu_custom_call" | custom-call | flops 40000000000 | bytes 23592960 | tf_op jit(solution)/shard_map/attend_backward/pallas_call | solution.py:494
  484.0 12.7 %copy.43 = f32[6144,512]{1,0:T(8,128)} copy(f32[6144,512]{0,1:T(8,128)} %bitcast.108) | data formatting | bytes 25165824 | tf_op jit(solution)/shard_map/transpose | solution.py:945
  504.5 15.9 %add_bitcast_fusion = f32[1,512,768]{2,1,0:T(8,128)} fusion(f32[512,768]{1,0:T(8,128)S(1)} %copy-done.12, f32[3072,768]{1,0:T(8,128)} %all-gather.15.cloned.1.call-done, f32[512,3072]{1,0:T(8,128)} %copy-done.20), kind=kOutput, calls=%fused_computation.26 | convolution fusion | flops 7260733440 | bytes 18874368 | tf_op jit(solution)/shard_map/dot_general | solution.py:17
  521.5 14.0 %collective-permute-done.3 = f32[512,1152]{1,0:T(8,128)} collective-permute-done((f32[512,1152]{1,0:T(8,128)}, f32[512,1152]{1,0:T(8,128)}, u32[]{:S(2)}, u32[]{:S(2)}) %collective-permute-start.3) | collective-permute-done | bytes 2359328 | tf_op jit(solution)/shard_map/ppermute | solution.py:936
  535.6 5.1 fusion.54
  540.7 3.9 multiply_reduce_fusion.1
  547.1 3.2 copy.42
  550.3 4.2 broadcast_select_fusion.1
  554.5 3.3 copy.45
  559.8 5.5 pad_maximum_fusion
  565.3 8.2 %copy.46 = f32[512,3,2,384]{3,2,1,0:T(2,128)} copy(f32[512,3,2,384]{0,3,1,2:T(8,128)} %pad_maximum_fusion) | data formatting | bytes 9437184 | tf_op jit(solution)/shard_map/concatenate | solution.py:940
  573.5 7.2 reshape.142.refs_6_
  582.8 189.3 %reduce_gradients.1 = (f32[16,48,768]{2,1,0:T(8,128)}, f32[512,6144]{1,0:T(8,128)}, f32[8,768]{1,0:T(8,128)}, f32[192,768]{1,0:T(8,128)}) custom-call(f32[8,2,1,48,512]{4,3,2,1,0:T(8,128)} %bitcast.115, f32[8,2,1,48,512]{4,3,2,1,0:T(8,128)} %bitcast.116, f32[8,2,1,48,512]{4,3,2,1,0:T(8,128)} %bitcast.117, f32[8,2,8,48,512]{4,3,2,1,0:T(8,128)} %bitcast.109, ...), custom_call_target="tpu_custom_call" | custom-call | flops 43486543872 | bytes 120000000 | tf_op jit(solution)/shard_map/reduce_gradients/pallas_call | solution.py:836
  778.3 10.9 %copy.55 = f32[1,512,6144]{2,1,0:T(8,128)} copy(f32[1,512,6144]{2,1,0:T(8,128)} %bitcast.110) | data formatting | bytes 25165824
  (139 shorter events, 53.3 us)
Async XLA Ops:
  7.2 3.5 copy-start.31
  7.2 3.5 copy-start.32
  7.2 72.5 %all-gather.9.cloned.1.call-start = ((), (), s32[]{:S(2)}) async-start(), calls=%async_computation.2 | async-start | bytes 7520256 | tf_op jit(solution)/shard_map/all_gather | solution.py:893
  8.0 170.9 %all-gather.7.cloned.1.call-start = ((), (), s32[]{:S(2)}) async-start(), calls=%async_computation.1 | async-start | bytes 20054016 | tf_op jit(solution)/shard_map/all_gather | solution.py:891
  8.7 282.4 %all-gather.11.cloned.1.call-start = ((), (), s32[]{:S(2)}) async-start(), calls=%async_computation.3 | async-start | bytes 2506752 | tf_op jit(solution)/shard_map/all_gather | solution.py:894
  9.4 305.0 %all-gather.13.cloned.1.call-start = ((), (), s32[]{:S(2)}) async-start(), calls=%async_computation.4 | async-start | bytes 10027008 | tf_op jit(solution)/shard_map/all_gather | solution.py:895
  10.0 377.6 %all-gather.15.cloned.1.call-start = ((), (), s32[]{:S(2)}) async-start(), calls=%async_computation.5 | async-start | bytes 10027008 | tf_op jit(solution)/shard_map/all_gather | solution.py:896
  10.6 572.2 %reduce-scatter.2.cloned.1.call-start = ((), (), s32[]{:S(2)}) async-start(), calls=%async_computation.6 | async-start | bytes 10027008 | tf_op jit(solution)/shard_map/reduce_scatter | solution.py:925
  178.8 21.0 %copy-start.6 = (f32[96,8,3,384]{3,1,2,0:T(8,128)S(1)}, f32[96,8,3,384]{3,1,2,0:T(8,128)}, u32[]{:S(2)}) copy-start(f32[96,8,3,384]{3,1,2,0:T(8,128)} %copy.50) | copy-start | bytes 10616836
  199.9 5.3 copy-start.15
  203.7 53.5 %collective-permute-start = (f32[512,1152]{1,0:T(8,128)S(1)}, f32[512,1152]{1,0:T(8,128)S(1)}, u32[]{:S(2)}, u32[]{:S(2)}) collective-permute-start(f32[512,1152]{1,0:T(8,128)S(1)} %fusion.21), channel_id=1, source_target_pairs={{0,1},{1,0},{2,3},{3,2},{4,5},{5,4},{6,7},{7,6},{8,9},{9,8},{10,11... | collective-permute-start | bytes 7077896 | tf_op jit(solution)/shard_map/ppermute | solution.py:909
  205.4 3.8 copy-start.8
  205.5 51.7 %copy-start.4 = (s32[1,1024]{1,0:T(1,128)S(1)}, s32[1,1024]{1,0:T(1,128)}, u32[]{:S(2)}) copy-start(s32[1,1024]{1,0:T(1,128)} %param.13) | copy-start | bytes 12292
  209.2 79.3 %copy-start.2 = (f32[512,1152]{1,0:T(8,128)}, f32[512,1152]{1,0:T(8,128)S(1)}, u32[]{:S(2)}) copy-start(f32[512,1152]{1,0:T(8,128)S(1)} %fusion.22.refs_0_.refs_1_.refs_2_) | copy-start | bytes 7077892
  257.3 31.2 %copy-start.3 = (s32[1024,128]{1,0:T(8,128)}, s32[1024,128]{1,0:T(8,128)S(1)}, u32[]{:S(2)}) copy-start(s32[1024,128]{1,0:T(8,128)S(1)} %broadcast_in_dim.34.refs_6_.refs_11_) | copy-start | bytes 1572868
  289.7 23.2 %copy-start = (f32[512,384]{1,0:T(8,128)}, f32[512,384]{1,0:T(8,128)S(1)}, u32[]{:S(2)}) copy-start(f32[512,384]{1,0:T(8,128)S(1)} %get-tuple-element.25.refs_6_) | copy-start | bytes 2359300
  289.7 19.0 %collective-permute-start.1 = (f32[512,384]{1,0:T(8,128)}, f32[512,384]{1,0:T(8,128)S(1)}, u32[]{:S(2)}, u32[]{:S(2)}) collective-permute-start(f32[512,384]{1,0:T(8,128)} %get-tuple-element.26.refs_7_), channel_id=1, source_target_pairs={{0,1},{1,0},{2,3},{3,2},{4,5},{5,4},{6,7},{7,6},{8,9},{9,8},{10,11... | collective-permute-start | bytes 2359304 | tf_op jit(solution)/shard_map/ppermute | solution.py:912
  308.8 4.2 copy-start.22
  314.5 14.1 %copy-start.25 = (f32[1,512,768]{2,1,0:T(8,128)S(1)}, f32[1,512,768]{2,1,0:T(8,128)}, u32[]{:S(2)}) copy-start(f32[1,512,768]{2,1,0:T(8,128)} %param.23) | copy-start | bytes 4718596
  340.1 62.0 %copy-start.11 = (f32[512,768]{1,0:T(8,128)S(1)}, f32[512,768]{1,0:T(8,128)}, u32[]{:S(2)}) copy-start(f32[512,768]{1,0:T(8,128)} %copy-done.10) | copy-start | bytes 4718596
  402.1 14.1 %copy-start.37 = (f32[512,3072]{1,0:T(8,128)}, f32[512,3072]{1,0:T(8,128)S(1)}, u32[]{:S(2)}) copy-start(f32[512,3072]{1,0:T(8,128)S(1)} %fusion.7.refs_4_) | copy-start | bytes 18874372
  418.4 7.3 copy-start.13
  421.8 19.8 %collective-permute-start.2 = (f32[512,384]{1,0:T(8,128)S(1)}, f32[512,384]{1,0:T(8,128)S(1)}, u32[]{:S(2)}, u32[]{:S(2)}) collective-permute-start(f32[512,384]{1,0:T(8,128)S(1)} %fusion.12), channel_id=1, source_target_pairs={{0,1},{1,0},{2,3},{3,2},{4,5},{5,4},{6,7},{7,6},{8,9},{9,8},{10,11... | collective-permute-start | bytes 2359304 | tf_op jit(solution)/shard_map/ppermute | solution.py:932
  482.5 53.1 %collective-permute-start.3 = (f32[512,1152]{1,0:T(8,128)}, f32[512,1152]{1,0:T(8,128)}, u32[]{:S(2)}, u32[]{:S(2)}) collective-permute-start(f32[512,1152]{1,0:T(8,128)} %pad_maximum_fusion.1), channel_id=1, source_target_pairs={{0,1},{1,0},{2,3},{3,2},{4,5},{5,4},{6,7},{7,6},{8,9},{9,8},{10,11... | collective-permute-start | bytes 7077896 | tf_op jit(solution)/shard_map/ppermute | solution.py:936
  504.4 15.9 %copy-start.29 = (f32[512,384]{1,0:T(8,128)S(1)}, f32[512,384]{1,0:T(8,128)}, u32[]{:S(2)}) copy-start(f32[512,384]{1,0:T(8,128)} %get-tuple-element.29) | copy-start | bytes 2359300
  504.4 16.0 %copy-start.28 = (f32[512,384]{1,0:T(8,128)S(1)}, f32[512,384]{1,0:T(8,128)}, u32[]{:S(2)}) copy-start(f32[512,384]{1,0:T(8,128)} %get-tuple-element.30) | copy-start | bytes 2359300
  520.3 15.2 %copy-start.7 = (f32[96,8,3,384]{3,1,2,0:T(8,128)S(1)}, f32[96,8,3,384]{3,1,2,0:T(8,128)}, u32[]{:S(2)}) copy-start(f32[96,8,3,384]{3,1,2,0:T(8,128)} %copy.50) | copy-start | bytes 10616836
  521.5 19.2 %copy-start.16 = (f32[512,1152]{1,0:T(8,128)}, f32[512,1152]{1,0:T(8,128)S(1)}, u32[]{:S(2)}) copy-start(f32[512,1152]{1,0:T(8,128)S(1)} %constant_dynamic-update-slice_fusion) | copy-start | bytes 7077892
  521.5 19.2 %copy-start.9 = (f32[96,8,3,384]{3,1,2,0:T(8,128)S(1)}, f32[96,8,3,384]{3,1,2,0:T(8,128)}, u32[]{:S(2)}) copy-start(f32[96,8,3,384]{3,1,2,0:T(8,128)} %copy-done.8) | copy-start | bytes 10616836
  573.5 7.9 copy-start.14
  573.5 7.9 copy-start.21
  778.3 10.9 %copy-start.30 = (f32[192,768]{1,0:T(8,128)S(1)}, f32[192,768]{1,0:T(8,128)}, u32[]{:S(2)}) copy-start(f32[192,768]{1,0:T(8,128)} %get-tuple-element.98) | copy-start | bytes 1769476
  (16 other events, 38.1 us)
Sparse Core Ops, SparseCore 0:
  10.3 69.3 all-gather.8
  81.3 97.4 all-gather.6
  181.1 42.2 all-gather.10
  225.6 80.2 all-gather.12
  308.0 79.5 all-gather.14
  391.5 109.4 reduce-scatter.1

commit v3 on v2

--- a/solution.py
+++ b/solution.py
@@ -297,13 +297,14 @@
 
 
 def forward_kernel(pos_ref, seg_ref, *refs):
-    (q_own, k_own, v_own, q_in, k_in, v_in, seg_col, seg_row,
+    (own_ref, in_ref, seg_col, seg_row,
      o_own, o_out, lse_ref, tq, hk, tv, out_s) = refs
-    rows = q_own.shape[0]
+    rows = own_ref.shape[0]
     own = pl.multiple_of(pos_ref[0] * rows, rows)
     other = pl.multiple_of((1 - pos_ref[0]) * rows, rows)
-    for place, q, k, v in ((own, q_own, k_own, v_own), (other, q_in, k_in, v_in)):
+    for place, ref in ((own, own_ref), (other, in_ref)):
         span = pl.ds(place, rows)
+        q, k, v = (ref.at[:, i * LANES:(i + 1) * LANES] for i in range(3))
         for head, tile in enumerate(pair_tiles(q[...] * 0.125)):
             tq[head, span, :] = jnp.concatenate([tile, tile], axis=1)
         for head, tile in enumerate(spread_tiles(k[...])):
@@ -363,55 +364,44 @@
     o_out[...] = out_s[pl.ds(other, rows), :]
 
 
-def attend_forward(own, received, position, labels):
-    rows, columns = own.shape
-    width = columns // 3
-    pairs = width // LANES
+def attend_forward(own, received, position, labels, labels_wide, labels_row):
+    rows = own.shape[0]
     length = 2 * rows
-
-    def part(which):
-        return pl.BlockSpec((rows, LANES), lambda g, *_: (0, which * pairs + g))
-
-    whole = pl.BlockSpec((rows, LANES), lambda g, *_: (0, g))
+    smem = pl.BlockSpec(memory_space=pltpu.SMEM)
+    vmem = pl.BlockSpec(memory_space=pltpu.VMEM)
     return pl.pallas_call(
         forward_kernel,
-        grid_spec=pltpu.PrefetchScalarGridSpec(
-            num_scalar_prefetch=2,
-            grid=(pairs,),
-            in_specs=[part(0), part(1), part(2), part(0), part(1), part(2),
-                      pl.BlockSpec((length, LANES), lambda g, *_: (0, 0)),
-                      pl.BlockSpec((length // BLOCK, 1, BLOCK), lambda g, *_: (0, 0, 0))],
-            out_specs=[whole, whole, pl.BlockSpec((length, LANES), lambda g, *_: (0, g))],
-            scratch_shapes=[
-                pltpu.VMEM((2, length, 2 * LANES), BF),
-                pltpu.VMEM((2, length, 2 * LANES), BF),
-                pltpu.VMEM((2, length, LANES), BF),
-                pltpu.VMEM((length, LANES), F32),
-            ],
-        ),
+        in_specs=[smem, smem] + [vmem] * 4,
+        out_specs=[vmem] * 3,
+        scratch_shapes=[
+            pltpu.VMEM((2, length, 2 * LANES), BF),
+            pltpu.VMEM((2, length, 2 * LANES), BF),
+            pltpu.VMEM((2, length, LANES), BF),
+            pltpu.VMEM((length, LANES), F32),
+        ],
         out_shape=[
-            jax.ShapeDtypeStruct((rows, width), F32),
-            jax.ShapeDtypeStruct((rows, width), F32),
-            jax.ShapeDtypeStruct((length, width), F32),
+            jax.ShapeDtypeStruct((rows, LANES), F32),
+            jax.ShapeDtypeStruct((rows, LANES), F32),
+            jax.ShapeDtypeStruct((length, LANES), F32),
         ],
-        cost_estimate=pl.CostEstimate(flops=20 * 10**9, bytes_accessed=8 * rows * columns * 3, transcendentals=length * width * 8),
-        compiler_params=pltpu.CompilerParams(vmem_limit_bytes=48 * 1024 * 1024),
+        cost_estimate=pl.CostEstimate(flops=6 * 10**9, bytes_accessed=28 * rows * LANES, transcendentals=length * length),
+        compiler_params=pltpu.CompilerParams(vmem_limit_bytes=32 * 1024 * 1024),
         name="attend_forward",
-    )(position, labels, own, own, own, received, received, received,
-      jnp.broadcast_to(labels[:, None], (length, LANES)), labels.reshape(length // BLOCK, 1, BLOCK))
+    )(position, labels, own, received, labels_wide, labels_row)
 
 
 def backward_kernel(pos_ref, seg_ref, *refs):
-    (q_own, k_own, v_own, q_in, k_in, v_in, o_own, o_in, g_own, g_in, lse_ref, seg_col, seg_row,
-     gq_own, gk_own, gv_own, gq_out, gk_out, gv_out,
+    (own_ref, in_ref, o_own, o_in, g_own, g_in, lse_ref, seg_col, seg_row,
+     grad_own, grad_out,
      tq, hk, tk, hv, tg, lse_t, delta_t, gq_s, gk_s, gv_s) = refs
-    rows = q_own.shape[0]
+    rows = own_ref.shape[0]
     length = 2 * rows
     own = pl.multiple_of(pos_ref[0] * rows, rows)
     other = pl.multiple_of((1 - pos_ref[0]) * rows, rows)
     half = LANES // 2
-    for place, q, k, v, o, g in ((own, q_own, k_own, v_own, o_own, g_own), (other, q_in, k_in, v_in, o_in, g_in)):
+    for place, ref, o, g in ((own, own_ref, o_own, g_own), (other, in_ref, o_in, g_in)):
         span = pl.ds(place, rows)
+        q, k, v = (ref.at[:, i * LANES:(i + 1) * LANES] for i in range(3))
         for head, tile in enumerate(pair_tiles(q[...] * 0.125)):
             tq[head, span, :] = jnp.concatenate([tile, tile], axis=1)
         for head, tile in enumerate(pair_tiles(g[...])):
@@ -473,70 +463,59 @@
 
     lax.fori_loop(0, blocks, key_block, 0)
     wide = low_lanes(rows)
-    for place, gq, gk, gv in ((own, gq_own, gk_own, gv_own), (other, gq_out, gk_out, gv_out)):
+    for place, ref in ((own, grad_own), (other, grad_out)):
         span = pl.ds(place, rows)
         left, right = gq_s[0, span, :], gq_s[1, span, :]
-        gq[...] = jnp.where(wide, left + roll_half(left), right + roll_half(right)) * 0.125
-        gk[...] = gk_s[span, :]
-        gv[...] = gv_s[span, :]
-
-
-def attend_backward(own, received, out_own, out_in, grad_own, grad_in, logs, position, labels):
-    rows, columns = own.shape
-    width = columns // 3
-    pairs = width // LANES
+        ref[:, :LANES] = jnp.where(wide, left + roll_half(left), right + roll_half(right)) * 0.125
+        ref[:, LANES:2 * LANES] = gk_s[span, :]
+        ref[:, 2 * LANES:] = gv_s[span, :]
+
+
+def attend_backward(own, received, out_own, out_in, grad_own, grad_in, logs, position, labels, labels_wide, labels_row):
+    rows = own.shape[0]
     length = 2 * rows
-
-    def part(which):
-        return pl.BlockSpec((rows, LANES), lambda g, *_: (0, which * pairs + g))
-
-    whole = pl.BlockSpec((rows, LANES), lambda g, *_: (0, g))
-    outs = pl.pallas_call(
+    smem = pl.BlockSpec(memory_space=pltpu.SMEM)
+    vmem = pl.BlockSpec(memory_space=pltpu.VMEM)
+    return pl.pallas_call(
         backward_kernel,
-        grid_spec=pltpu.PrefetchScalarGridSpec(
-            num_scalar_prefetch=2,
-            grid=(pairs,),
-            in_specs=[part(0), part(1), part(2), part(0), part(1), part(2), whole, whole, whole, whole,
-                      pl.BlockSpec((length, LANES), lambda g, *_: (0, g)),
-                      pl.BlockSpec((length, LANES), lambda g, *_: (0, 0)),
-                      pl.BlockSpec((length // BLOCK, 1, BLOCK), lambda g, *_: (0, 0, 0))],
-            out_specs=[whole] * 6,
-            scratch_shapes=[
-                pltpu.VMEM((2, length, 2 * LANES), BF),
-                pltpu.VMEM((2, length, 2 * LANES), BF),
-                pltpu.VMEM((2, length, LANES), BF),
-                pltpu.VMEM((2, length, 2 * LANES), BF),
-                pltpu.VMEM((2, length, 2 * LANES), BF),
-                pltpu.VMEM((2, 8, length), F32),
-                pltpu.VMEM((2, 8, length), F32),
-                pltpu.VMEM((2, length, LANES), F32),
-                pltpu.VMEM((length, LANES), F32),
-                pltpu.VMEM((length, LANES), F32),
-            ],
-        ),
-        out_shape=[jax.ShapeDtypeStruct((rows, width), F32)] * 6,
-        cost_estimate=pl.CostEstimate(flops=40 * 10**9, bytes_accessed=8 * rows * columns * 5, transcendentals=length * width * 8),
-        compiler_params=pltpu.CompilerParams(vmem_limit_bytes=56 * 1024 * 1024),
+        in_specs=[smem, smem] + [vmem] * 9,
+        out_specs=[vmem] * 2,
+        scratch_shapes=[
+            pltpu.VMEM((2, length, 2 * LANES), BF),
+            pltpu.VMEM((2, length, 2 * LANES), BF),
+            pltpu.VMEM((2, length, LANES), BF),
+            pltpu.VMEM((2, length, 2 * LANES), BF),
+            pltpu.VMEM((2, length, 2 * LANES), BF),
+            pltpu.VMEM((2, 8, length), F32),
+            pltpu.VMEM((2, 8, length), F32),
+            pltpu.VMEM((2, length, LANES), F32),
+            pltpu.VMEM((length, LANES), F32),
+            pltpu.VMEM((length, LANES), F32),
+        ],
+        out_shape=[jax.ShapeDtypeStruct((rows, 3 * LANES), F32)] * 2,
+        cost_estimate=pl.CostEstimate(flops=13 * 10**9, bytes_accessed=60 * rows * LANES, transcendentals=length * length),
+        compiler_params=pltpu.CompilerParams(vmem_limit_bytes=40 * 1024 * 1024),
         name="attend_backward",
-    )(position, labels, own, own, own, received, received, received, out_own, out_in, grad_own, grad_in, logs,
-      jnp.broadcast_to(labels[:, None], (length, LANES)), labels.reshape(length // BLOCK, 1, BLOCK))
-    return outs
+    )(position, labels, own, received, out_own, out_in, grad_own, grad_in, logs, labels_wide, labels_row)
 
 
 MESH = pl.DeviceIdType.MESH
 PIECE = 48
 
 
-def scatter_kernel(plan, *refs):
+def scatter_kernel(plan, groups, *refs):
     count = len(plan)
     units = sum(plan)
     pairs = units // 2
-    turned, grads = refs[:count], refs[count:2 * count]
-    stream_ref, weight_ref, norms_ref, extra_ref = refs[2 * count:2 * count + 4]
-    total_ref, patch_ref, norm_total_ref, extra_total_ref = refs[2 * count + 4:2 * count + 8]
+    turned, refs = refs[:count], refs[count:]
+    grads = []
+    for group in groups:
+        grads.append(refs[:group] if group > 1 else refs[0])
+        refs = refs[group:]
+    stream_ref, weight_ref, norms_ref, extra_ref, total_ref, patch_ref, norm_total_ref, extra_total_ref = refs[:8]
     (t_buf, g_buf, g_high, g_low, part, s_high, s_low, w_buf, p_buf, land_a, n_x, n_z, n_y, y_y, y_x, y_z, done,
      v_c, v_x, v_y, v_z, extra_in,
-     load_sem, w_sem, p_sem, a_sem, nx_sem, nz_sem, ny_sem, yy_sem, yx_sem, yz_sem, ye_sem, v_sem, o_sem) = refs[2 * count + 8:]
+     load_sem, w_sem, p_sem, a_sem, nx_sem, nz_sem, ny_sem, yy_sem, yx_sem, yz_sem, ye_sem, v_sem, o_sem) = refs[8:]
     fsdp = lax.axis_index("fsdp")
     row = lax.axis_index("sp")
     z, x, core = fsdp // 4, (fsdp // 2) % 2, fsdp % 2
@@ -575,6 +554,22 @@
                     act(pltpu.make_async_copy(source, t_buf.at[slot, side], load_sem.at[slot, side]))
                 grad = grads[which]
                 width = g_buf.shape[2]
+                if groups[which] > 1:
+                    parts = groups[which] // 2
+                    for unit_at in range(plan[which]):
+                        @pl.when(j == unit_at)
+                        def _(unit_at=unit_at):
+                            for place in range(2):
+                                side, part = divmod(2 * unit_at + place, parts)
+                                for mine in range(2):
+                                    @pl.when((row == side) == (mine == 1))
+                                    def _(place=place, part=part, mine=mine):
+                                        act(pltpu.make_async_copy(
+                                            grad[part if mine else parts + part],
+                                            g_buf.at[slot, :, pl.ds(place * (width // 2), width // 2)],
+                                            load_sem.at[slot, 2 + place],
+                                        ))
+                    return
                 if grad.shape[1] > width:
                     grad = grad.at[:, pl.ds(pl.multiple_of(j * width, width), width)]
                 act(pltpu.make_async_copy(grad, g_buf.at[slot], load_sem.at[slot, 2]))
@@ -820,28 +815,33 @@
 def reduce_gradients(turned, grads, grad_stream, weight, norms, extra):
     rows, width = grad_stream.shape
     plan, views = [], []
+    flat, groups = [], []
     for left, right in zip(turned, grads):
         tall = left.shape[0] // (16 * PIECE)
-        plan.append(tall * (right.shape[1] // width))
+        parts = list(right) if isinstance(right, (tuple, list)) else [right]
+        flat += parts
+        groups.append(len(parts))
+        plan.append(tall * (sum(part.shape[1] for part in parts) // width))
         views.append(left.reshape(8, 2, tall, PIECE, rows))
     units = sum(plan)
     pairs = units // 2
     owners = 16
     block = weight.shape[0] // owners
+    assert units == owners
     half = PIECE // 2
     dma = pltpu.SemaphoreType.DMA
     any_space = pl.BlockSpec(memory_space=pl.ANY)
     vmem = pl.BlockSpec(memory_space=pltpu.VMEM)
     flops = 6 * rows * width * (units * 16 * PIECE + weight.shape[0])
     return pl.pallas_call(
-        functools.partial(scatter_kernel, tuple(plan)),
+        functools.partial(scatter_kernel, tuple(plan), tuple(groups)),
         out_shape=[
             jax.ShapeDtypeStruct((units, PIECE, width), F32),
             jax.ShapeDtypeStruct((rows, weight.shape[0]), F32),
             jax.ShapeDtypeStruct(norms.shape, F32),
             jax.ShapeDtypeStruct(extra.shape, F32),
         ],
-        in_specs=[any_space] * (2 * len(plan)) + [vmem, any_space, vmem, vmem],
+        in_specs=[any_space] * (len(views) + len(flat)) + [vmem, any_space, vmem, vmem],
         out_specs=[any_space, any_space, vmem, vmem],
         scratch_shapes=[
             pltpu.VMEM((2, 2, 8, PIECE, rows), F32),
@@ -866,7 +866,7 @@
             pltpu.VMEM(norms.shape, F32),
             pltpu.VMEM((3,) + norms.shape, F32),
             pltpu.VMEM(extra.shape, F32),
-            dma((2, 3)), dma((2,)), dma((2,)),
+            dma((2, 4)), dma((2,)), dma((2,)),
             dma((2, units)), dma((2, pairs)), dma((2, pairs, 3)), dma((2, pairs)),
             dma((2, pairs)), dma((2, pairs)), dma((2, pairs, 3)), dma((2, pairs)),
             dma((2, 7)), dma,
@@ -876,85 +876,601 @@
             collective_id=0, has_side_effects=True, vmem_limit_bytes=67043328
         ),
         name="reduce_gradients",
-    )(*views, *grads, grad_stream, weight.reshape(owners, block, width), norms, extra)
+    )(*views, *flat, grad_stream, weight.reshape(owners, block, width), norms, extra)
+
+
+CUT_ROWS = 128
+CUT_COLUMNS = 128
+NARROW = 384
+
+
+def three(product, left, right):
+    return product(left[0], right[0]) + product(left[0], right[1]) + product(left[1], right[0])
+
+
+def normalized(values):
+    average = jnp.mean(values, axis=-1, keepdims=True)
+    centred = values - average
+    spread = jnp.mean(centred * centred, axis=-1, keepdims=True)
+    scale = lax.rsqrt(spread + EPSILON)
+    return centred * scale, scale
+
+
+def gather_kernel(patch_ref, in_ref, qkv_ref, out_ref, vector_ref,
+                  stream_ref, normed_ref, turned_ref, patch_turned_ref, in_full, qkv_full, out_full, vectors_ref,
+                  sent_0, sent_1, sent_2,
+                  patch_buf, in_buf, qkv_buf, out_buf, turn_buf, acc, v_c, v_x, v_z, sent_buf,
+                  z_sem, x_sem, y_sem, c_sem, v_sem, own_sem, patch_sem, turn_sem, full_sem, last_sem):
+    fsdp = lax.axis_index("fsdp")
+    row = lax.axis_index("sp")
+    z, x, core = fsdp // 4, (fsdp // 2) % 2, fsdp % 2
+    block, width = in_ref.shape
+    across_count = width // CUT_COLUMNS
+    in_units = (block // CUT_ROWS) * across_count
+    narrow = NARROW
+    out_units = width // narrow
+    units = in_units + qkv_ref.shape[1] // narrow + out_units
+
+    def device(z_at, x_at, core_at, row_at):
+        return ((z_at * 2 + x_at) * 2 + core_at, row_at)
+
+    sibling = device(z, x, 1 - core, row)
+    beside = device(z, 1 - x, core, row)
+    across = device(z, x, core, 1 - row)
+    along = [device((z + step) % 4, x, core, row) for step in (1, 2, 3)]
+    barrier = pltpu.get_barrier_semaphore()
+    for peer in [sibling, beside, across] + along:
+        pl.semaphore_signal(barrier, inc=1, device_id=peer, device_id_type=MESH)
+
+    def remote(source, target, sems, index, peer):
+        return pltpu.make_async_remote_copy(
+            src_ref=source, dst_ref=target, send_sem=sems.at[(0,) + index], recv_sem=sems.at[(1,) + index],
+            device_id=peer, device_id_type=MESH,
+        )
+
+    patch_copy = pltpu.make_async_copy(patch_ref, patch_buf, patch_sem)
+
+    def span(first, size, step=None):
+        return pl.ds(pl.multiple_of(first, step or size), size)
+
+    def places(kind, unit, part):
+        if kind == "in":
+            j, column = unit // across_count, unit % across_count
+            columns = span(column * CUT_COLUMNS, CUT_COLUMNS)
+            base, rows, edge = j * CUT_ROWS, CUT_ROWS, 40
+        else:
+            rows, edge = out_ref.shape[0], 16
+            first = in_units if kind == "qkv" else units - out_units
+            base, columns = 0, span((unit - first) * narrow, narrow)
+        if part is None:
+            return span(base, rows, 8), columns
+        which, side = part
+        if which == 0:
+            return span(base + side * (rows - edge), edge, 8), columns
+        return span(base + side * edge, rows - edge, 8), columns
+
+    sources = {"in": (in_ref, in_buf), "qkv": (qkv_ref, qkv_buf), "out": (out_ref, out_buf)}
+
+    def each_kind(unit, act):
+        ranges = (("in", 0, in_units), ("qkv", in_units, units - out_units), ("out", units - out_units, units))
+        for kind, first, last in ranges:
+            @pl.when((unit >= first) & (unit < last))
+            def _(kind=kind):
+                act(kind)
+
+    own_copies = []
+    for kind, firsts in (("in", range(0, block, CUT_ROWS)), ("qkv", (0,)), ("out", (0,))):
+        source, buf = sources[kind]
+        for first in firsts:
+            rows = places(kind, first // CUT_ROWS * across_count if kind == "in" else in_units, (1, row))[0]
+            own_copies.append(
+                pltpu.make_async_copy(source.at[rows], buf.at[z, x, core, rows], own_sem.at[len(own_copies)])
+            )
+
+    def z_copy(kind, unit, step):
+        source, buf = sources[kind]
+        at = places(kind, unit, (1, row))
+        return remote(source.at[at], buf.at[(z, x, core) + at], z_sem, (unit, step), along[step])
+
+    def x_copy(kind, unit):
+        ref = sources[kind][1].at[(slice(None), x, core) + places(kind, unit, (1, row))]
+        return remote(ref, ref, x_sem, (unit,), beside)
+
+    def y_copy(kind, unit):
+        ref = sources[kind][1].at[(slice(None), slice(None), core) + places(kind, unit, (0, row))]
+        return remote(ref, ref, y_sem, (unit,), across)
+
+    def c_copy(kind, unit, index):
+        part = (1, row) if index == 0 else (0, 1 - row)
+        ref = sources[kind][1].at[(slice(None), slice(None), core) + places(kind, unit, part)]
+        return remote(ref, ref, c_sem, (unit, index), sibling)
+
+    def z_stage(unit):
+        def act(kind):
+            for step in range(3):
+                z_copy(kind, unit, step).start()
+
+        each_kind(unit, act)
+
+    def x_stage(unit):
+        def act(kind):
+            for step in range(3):
+                z_copy(kind, unit, step).wait_recv()
+            x_copy(kind, unit).start()
+
+        each_kind(unit, act)
+
+    def spread_stage(unit):
+        def act(kind):
+            x_copy(kind, unit).wait_recv()
+            y_copy(kind, unit).start()
+            c_copy(kind, unit, 0).start()
+
+        each_kind(unit, act)
+
+    def y_stage(unit):
+        def act(kind):
+            y_copy(kind, unit).wait_recv()
+            c_copy(kind, unit, 1).start()
+
+        each_kind(unit, act)
+
+    def ready(unit):
+        def act(kind):
+            c_copy(kind, unit, 0).wait_recv()
+            c_copy(kind, unit, 1).wait_recv()
+            full_copy(kind, unit).start()
+
+        each_kind(unit, act)
+
+    def full_copy(kind, unit):
+        at = (slice(None), slice(None), slice(None)) + places(kind, unit, None)
+        full = {"in": in_full, "qkv": qkv_full, "out": out_full}[kind]
+        return pltpu.make_async_copy(sources[kind][1].at[at], full.at[at], full_sem.at[unit])
+
+    def multiply(unit):
+        j, column = unit // across_count, unit % across_count
+        columns = span(column * CUT_COLUMNS, CUT_COLUMNS)
+        rows = span(j * CUT_ROWS, CUT_ROWS)
+
+        def step(pair, carry):
+            first = pair * 2 * block + j * CUT_ROWS
+            left = jnp.concatenate(
+                [patch_buf[:, span(first, CUT_ROWS)], patch_buf[:, span(first + block, CUT_ROWS)]], axis=1
+            )
+            right = in_buf[pair // 2, pair % 2, :, rows, columns].reshape(2 * CUT_ROWS, CUT_COLUMNS)
+            acc[:, columns] = acc[:, columns] + three(nn, split_bf(left), split_bf(right))
+            return carry
+
+        lax.fori_loop(0, 8, step, 0)
+
+    tiles = patch_ref.shape[1] // LANES
+    each = turn_buf.shape[0]
+
+    def turn_copy(tile, slot):
+        return pltpu.make_async_copy(turn_buf.at[slot], patch_turned_ref.at[span(tile * LANES, LANES)], turn_sem.at[slot])
+
+    def turn(group):
+        for slot in range(each):
+            @pl.when(group > 0)
+            def _(slot=slot):
+                turn_copy((group - 1) * each + slot, slot).wait()
+
+            turn_buf[slot] = jnp.transpose(patch_buf[:, span((group * each + slot) * LANES, LANES)])
+            turn_copy(group * each + slot, slot).start()
+
+    pl.semaphore_wait(barrier, 6)
+    z_stage(jnp.int32(0))
+    z_stage(jnp.int32(1))
+    for copy in own_copies:
+        copy.start()
+    patch_copy.start()
+    v_copies = [
+        remote(vector_ref, v_c, v_sem, (0,), sibling),
+        remote(v_c, v_x, v_sem, (1,), beside),
+    ] + [remote(v_x, v_z.at[step], v_sem, (2 + step,), along[step]) for step in range(3)]
+    v_copies[0].start()
+    acc[...] = jnp.zeros_like(acc)
+    for copy in own_copies:
+        copy.wait()
+
+    def iteration(t, carry):
+        z_stage(t + 2)
+        x_stage(t)
+        spread_stage(t - 2)
+        y_stage(t - 4)
+
+        @pl.when(t == 0)
+        def _():
+            patch_copy.wait()
+            v_copies[0].wait_recv()
+            v_c[...] = v_c[...] + vector_ref[...]
+            v_copies[1].start()
+
+        @pl.when(t == 1)
+        def _():
+            v_copies[1].wait_recv()
+            v_x[...] = v_x[...] + v_c[...]
+            for step in range(3):
+                v_copies[2 + step].start()
+
+        @pl.when(t == 2)
+        def _():
+            for step in range(3):
+                v_copies[2 + step].wait_recv()
+            vectors_ref[...] = v_x[...] + v_z[0] + v_z[1] + v_z[2]
+
+        @pl.when(t < tiles // each)
+        def _():
+            turn(t)
+
+        ready(t - 5)
+
+        @pl.when((t >= 5) & (t < in_units + 5))
+        def _():
+            multiply(t - 5)
+
+        @pl.when(t == in_units + 5)
+        def _():
+            stream = acc[...]
+            stream_ref[...] = stream
+            zhat, _ = normalized(stream)
+            acc[...] = zhat * vectors_ref[0:1, :] + vectors_ref[1:2, :]
+            normed_ref[...] = acc[...]
+            turned_ref[...] = jnp.transpose(acc[...])
+
+        return carry
+
+    lax.fori_loop(0, units + 5, iteration, 0)
+    left = split_bf(acc[...])
+    group_width = sent_0.shape[1]
+    last = []
+    for group, ref in enumerate((sent_0, sent_1, sent_2)):
+        columns = span((1 - row) * 3 * group_width + group * group_width, group_width)
+        right = qkv_buf[:, :, :, :, columns].reshape(width, group_width)
+        sent_buf[group] = three(nn, left, split_bf(right))
+        copy = pltpu.make_async_copy(sent_buf.at[group], ref, last_sem.at[group])
+        copy.start()
+        last.append(copy)
+
+    def finish(unit, carry):
+        def act(kind):
+            for step in range(3):
+                z_copy(kind, unit, step).wait_send()
+            x_copy(kind, unit).wait_send()
+            y_copy(kind, unit).wait_send()
+            c_copy(kind, unit, 0).wait_send()
+            c_copy(kind, unit, 1).wait_send()
+            full_copy(kind, unit).wait()
+
+        each_kind(unit, act)
+        return carry
+
+    lax.fori_loop(0, units, finish, 0)
+    for copy in v_copies:
+        copy.wait_send()
+    for slot in range(each):
+        turn_copy(tiles - each + slot, slot).wait()
+    for copy in last:
+        copy.wait()
+
+
+def gather_stream(patch_rows, w_in, w_qkv, w_out, vectors):
+    rows, patch_width = patch_rows.shape
+    block, width = w_in.shape
+    piece, columns = w_qkv.shape
+    group = columns // 6
+    any_space = pl.BlockSpec(memory_space=pl.ANY)
+    vmem = pl.BlockSpec(memory_space=pltpu.VMEM)
+    dma = pltpu.SemaphoreType.DMA
+    units = (block // CUT_ROWS) * (width // CUT_COLUMNS) + (columns + width) // NARROW
+    owners = (4, 2, 2)
+
+    def array(*shape):
+        return jax.ShapeDtypeStruct(shape, F32)
+
+    return pl.pallas_call(
+        gather_kernel,
+        out_shape=[
+            array(rows, width), array(rows, width), array(width, rows), array(patch_width, rows),
+            array(*owners, block, width), array(*owners, piece, columns), array(*owners, piece, width),
+            array(*vectors.shape), array(rows, group), array(rows, group), array(rows, group),
+        ],
+        in_specs=[any_space] * 4 + [vmem],
+        out_specs=[vmem, vmem, vmem] + [any_space] * 4 + [vmem] + [any_space] * 3,
+        scratch_shapes=[
+            pltpu.VMEM((rows, patch_width), F32),
+            pltpu.VMEM(owners + (block, width), F32),
+            pltpu.VMEM(owners + (piece, columns), F32),
+            pltpu.VMEM(owners + (piece, width), F32),
+            pltpu.VMEM((4, LANES, rows), F32),
+            pltpu.VMEM((rows, width), F32),
+            pltpu.VMEM(vectors.shape, F32),
+            pltpu.VMEM(vectors.shape, F32),
+            pltpu.VMEM((3,) + vectors.shape, F32),
+            pltpu.VMEM((3, rows, group), F32),
+            dma((2, units, 3)), dma((2, units)), dma((2, units)), dma((2, units, 2)), dma((2, 5)),
+            dma((block // CUT_ROWS + 2,)), dma, dma((4,)), dma((units,)), dma((3,)),
+        ],
+        cost_estimate=pl.CostEstimate(flops=6 * rows * patch_width * width, bytes_accessed=90 * 10**6, transcendentals=0),
+        compiler_params=pltpu.CompilerParams(collective_id=1, has_side_effects=True, vmem_limit_bytes=67043328),
+        name="gather_stream",
+    )(patch_rows, w_in, w_qkv, w_out, vectors)
+
+
+def own_kernel(pos_ref, normed_ref, weight_ref, *outs):
+    step = pl.program_id(0)
+    weight = weight_ref[...].reshape(normed_ref.shape[1], weight_ref.shape[4])
+    product = three(nn, split_bf(normed_ref[...]), split_bf(weight))
+    for i, ref in enumerate(outs):
+        @pl.when(step == i)
+        def _(ref=ref):
+            ref[...] = product
+
+
+def project_own(position, normed, qkv_full):
+    rows, width = normed.shape
+    owners, columns = qkv_full.shape[:4], qkv_full.shape[4]
+    group = columns // 6
+    return pl.pallas_call(
+        own_kernel,
+        grid_spec=pltpu.PrefetchScalarGridSpec(
+            num_scalar_prefetch=1,
+            grid=(3,),
+            in_specs=[
+                pl.BlockSpec((rows, width), lambda g, pos: (0, 0)),
+                pl.BlockSpec(owners + (group,), lambda g, pos: (0, 0, 0, 0, pos[0] * 3 + g)),
+            ],
+            out_specs=[pl.BlockSpec((rows, group), lambda g, pos: (0, 0))] * 3,
+        ),
+        out_shape=[jax.ShapeDtypeStruct((rows, group), F32)] * 3,
+        cost_estimate=pl.CostEstimate(flops=3 * rows * width * columns, bytes_accessed=8 * 10**6, transcendentals=0),
+        compiler_params=pltpu.CompilerParams(vmem_limit_bytes=40 * 1024 * 1024),
+        name="project_own",
+    )(position, normed, qkv_full)
+
+
+def gelu_and_slope(values):
+    root = 0.7978845608028654
+    square = values * values
+    bent = jnp.tanh(root * (values + 0.044715 * values * square))
+    half = 0.5 + 0.5 * bent
+    slope = half + 0.5 * values * (1.0 - bent * bent) * (root * (1.0 + 0.134145 * square))
+    return values * half, slope
+
+
+def norm_back(grad, values, gain):
+    zhat, scale = normalized(values)
+    scaled = grad * gain
+    back = scale * (
+        scaled - jnp.mean(scaled, axis=-1, keepdims=True) - zhat * jnp.mean(scaled * zhat, axis=-1, keepdims=True)
+    )
+    return back, jnp.sum(grad * zhat, axis=0, keepdims=True), jnp.sum(grad, axis=0, keepdims=True)
+
+
+def middle_kernel(pos_ref, *refs):
+    own_parts, in_parts = refs[0:3], refs[3:6]
+    (stream_ref, cot_ref, out_ref, vectors_ref, up_ref, down_ref,
+     block_ref, grad_pre_ref, grad_down_ref, grad_resid_ref, turned_ref, attended_ref) = refs[6:18]
+    sent_refs, own_refs, sums_ref = refs[18:21], refs[21:24], refs[24]
+    residual, norm_high, norm_low, cot_high, cot_low, grad_norm = refs[25:]
+    step = pl.program_id(0)
+    width = out_ref.shape[0]
+    half = width // 2
+    own = pl.ds(pl.multiple_of(pos_ref[0] * half, half), half)
+    other = pl.ds(pl.multiple_of((1 - pos_ref[0]) * half, half), half)
+
+    @pl.when(step == 0)
+    def _():
+        total = stream_ref[...]
+        for span, parts in ((own, own_parts), (other, in_parts)):
+            left = jnp.concatenate([part[...] for part in parts], axis=1)
+            attended_ref[span, :] = jnp.transpose(left)
+            total = total + three(nn, split_bf(left), split_bf(out_ref[span, :]))
+        residual[...] = total
+        block_ref[...] = total
+        zhat, _ = normalized(total)
+        normed = zhat * vectors_ref[2:3, :] + vectors_ref[3:4, :]
+        turned_ref[...] = jnp.transpose(normed)
+        norm_high[...], norm_low[...] = split_bf(normed)
+        cot_high[...], cot_low[...] = split_bf(cot_ref[...])
+        grad_norm[...] = jnp.zeros_like(grad_norm)
+
+    up = split_bf(up_ref[...].reshape(width, width))
+    hidden, slope = gelu_and_slope(three(nn, (norm_high[...], norm_low[...]), up))
+    down = split_bf(down_ref[...].reshape(width, width))
+    cot = (cot_high[...], cot_low[...])
+    grad_pre = three(nt, cot, down) * slope
+    grad_pre_ref[...] = grad_pre
+    parts = split_bf(hidden)
+    block_ref[...] = block_ref[...] + three(nn, parts, down)
+    grad_down_ref[...] = three(tn, parts, cot).reshape(grad_down_ref.shape)
+    grad_norm[...] = grad_norm[...] + three(nt, split_bf(grad_pre), up)
+
+    @pl.when(step == pl.num_programs(0) - 1)
+    def _():
+        back, gain, offset = norm_back(grad_norm[...], residual[...], vectors_ref[2:3, :])
+        grad = cot_ref[...] + back
+        grad_resid_ref[...] = grad
+        sums_ref[...] = jnp.zeros_like(sums_ref)
+        sums_ref[2:3, :] = gain
+        sums_ref[3:4, :] = offset
+        left = split_bf(grad)
+        for span, outs in ((other, sent_refs), (own, own_refs)):
+            product = three(nt, left, split_bf(out_ref[span, :]))
+            for i, ref in enumerate(outs):
+                ref[...] = product[:, i * LANES:(i + 1) * LANES]
+
+
+def middle(position, out_own, out_in, stream, cotangent, w_out, vectors, weights):
+    rows, width = stream.shape
+    owners, stacked = weights.shape[0], weights.shape[1]
+    piece = width // owners
+    steps = stacked // piece // 2
+    whole = lambda *shape: pl.BlockSpec(shape, lambda j, *_: (0,) * len(shape))
+    array = lambda *shape: jax.ShapeDtypeStruct(shape, F32)
+    head = whole(rows, LANES)
+    return pl.pallas_call(
+        middle_kernel,
+        grid_spec=pltpu.PrefetchScalarGridSpec(
+            num_scalar_prefetch=1,
+            grid=(steps,),
+            in_specs=[head] * 6 + [
+                whole(rows, width), whole(rows, width), whole(width, width), whole(*vectors.shape),
+                pl.BlockSpec((owners, piece, width), lambda j, *_: (0, j, 0)),
+                pl.BlockSpec((owners, piece, width), lambda j, *_: (0, steps + j, 0)),
+            ],
+            out_specs=[
+                whole(rows, width),
+                pl.BlockSpec((rows, width), lambda j, *_: (0, j)),
+                pl.BlockSpec((owners, piece, width), lambda j, *_: (0, j, 0)),
+                whole(rows, width), whole(width, rows), whole(width, rows),
+            ] + [head] * 6 + [whole(*vectors.shape)],
+            scratch_shapes=[
+                pltpu.VMEM((rows, width), F32),
+                pltpu.VMEM((rows, width), BF), pltpu.VMEM((rows, width), BF),
+                pltpu.VMEM((rows, width), BF), pltpu.VMEM((rows, width), BF),
+                pltpu.VMEM((rows, width), F32),
+            ],
+        ),
+        out_shape=[
+            array(rows, width), array(rows, steps * width), array(owners, steps * piece, width),
+            array(rows, width), array(width, rows), array(width, rows),
+        ] + [array(rows, LANES)] * 6 + [array(*vectors.shape)],
+        cost_estimate=pl.CostEstimate(
+            flops=6 * rows * width * width * (5 * steps + 2), bytes_accessed=60 * 10**6, transcendentals=rows * steps * width
+        ),
+        compiler_params=pltpu.CompilerParams(vmem_limit_bytes=62 * 1024 * 1024),
+        name="feed_forward",
+    )(position, *out_own, *out_in, stream, cotangent, w_out, vectors, weights, weights)
+
+
+def partial_kernel(pos_ref, g0, g1, g2, weight_ref, out_ref):
+    width = out_ref.shape[1]
+    weight = weight_ref[...].reshape(width, weight_ref.shape[4])
+    left = jnp.concatenate([g0[...], g1[...], g2[...]], axis=1)
+    out_ref[...] = three(nt, split_bf(left), split_bf(weight))
+
+
+def grad_normed_part(position, grads, qkv_full):
+    rows = grads[0].shape[0]
+    owners, columns = qkv_full.shape[:4], qkv_full.shape[4]
+    width = owners[0] * owners[1] * owners[2] * owners[3]
+    part = pl.BlockSpec((rows, columns // 6), lambda i, pos: (0, 0))
+    return pl.pallas_call(
+        partial_kernel,
+        grid_spec=pltpu.PrefetchScalarGridSpec(
+            num_scalar_prefetch=1,
+            grid=(1,),
+            in_specs=[part] * 3 + [pl.BlockSpec(owners + (columns // 2,), lambda i, pos: (0, 0, 0, 0, pos[0]))],
+            out_specs=pl.BlockSpec((rows, width), lambda i, pos: (0, 0)),
+        ),
+        out_shape=jax.ShapeDtypeStruct((rows, width), F32),
+        cost_estimate=pl.CostEstimate(flops=3 * rows * width * columns, bytes_accessed=8 * 10**6, transcendentals=0),
+        compiler_params=pltpu.CompilerParams(vmem_limit_bytes=40 * 1024 * 1024),
+        name="grad_normed_part",
+    )(position, *grads, qkv_full)
+
+
+def stream_kernel(pos_ref, g0, g1, g2, weight_ref, part_ref, stream_ref, resid_ref, vectors_ref, before_ref, out_ref, sums_ref):
+    width = out_ref.shape[1]
+    weight = weight_ref[...].reshape(width, weight_ref.shape[4])
+    left = jnp.concatenate([g0[...], g1[...], g2[...]], axis=1)
+    grad = part_ref[...] + three(nt, split_bf(left), split_bf(weight))
+    back, gain, offset = norm_back(grad, stream_ref[...], vectors_ref[0:1, :])
+    out_ref[...] = resid_ref[...] + back
+    sums_ref[...] = before_ref[...]
+    sums_ref[0:1, :] = gain
+    sums_ref[1:2, :] = offset
+
+
+def grad_of_stream(position, grads, qkv_full, part, stream, grad_resid, vectors, sums):
+    rows, width = stream.shape
+    owners, columns = qkv_full.shape[:4], qkv_full.shape[4]
+    whole = lambda *shape: pl.BlockSpec(shape, lambda i, pos: (0,) * len(shape))
+    return pl.pallas_call(
+        stream_kernel,
+        grid_spec=pltpu.PrefetchScalarGridSpec(
+            num_scalar_prefetch=1,
+            grid=(1,),
+            in_specs=[whole(rows, columns // 6)] * 3
+            + [pl.BlockSpec(owners + (columns // 2,), lambda i, pos: (0, 0, 0, 0, 1 - pos[0]))]
+            + [whole(rows, width)] * 3 + [whole(*vectors.shape)] * 2,
+            out_specs=[whole(rows, width), whole(*vectors.shape)],
+        ),
+        out_shape=[jax.ShapeDtypeStruct((rows, width), F32), jax.ShapeDtypeStruct(vectors.shape, F32)],
+        cost_estimate=pl.CostEstimate(flops=3 * rows * width * columns, bytes_accessed=14 * 10**6, transcendentals=0),
+        compiler_params=pltpu.CompilerParams(vmem_limit_bytes=48 * 1024 * 1024),
+        name="grad_of_stream",
+    )(position, *grads, qkv_full, part, stream, grad_resid, vectors, sums)
 
 
 def fast_shards(
     patches, segments, w_in, norm1_gain, norm1_bias, w_qkv, w_out, norm2_gain, norm2_bias, w_up, w_down, cotangent
 ):
     _, rows, patch_width = patches.shape
-    width = w_out.shape[1]
+    piece, width = w_out.shape
+    hidden = w_up.shape[1]
+    owners = lax.axis_size("fsdp")
     position = lax.axis_index("sp")
+    index = lax.axis_index("fsdp")
     places = position[None].astype(jnp.int32)
     labels = segments[0]
-    norm_params = jnp.stack([norm1_gain, norm1_bias, norm2_gain, norm2_bias])
-    in_full = lax.all_gather(w_in, "fsdp", axis=0, tiled=True)
-    norm_full = lax.all_gather(norm_params, "fsdp", axis=1, tiled=True)
-    qkv_full = lax.all_gather(w_qkv, "fsdp", axis=0, tiled=True)
-    out_full = lax.all_gather(w_out, "fsdp", axis=0, tiled=True)
-    up_full = lax.all_gather(w_up, "fsdp", axis=0, tiled=True)
-    down_full = lax.all_gather(w_down, "fsdp", axis=0, tiled=True)
-    patch_rows = patches[0]
-    stream = matmul(patch_rows, in_full)
-    normed, norm1_pull = jax.vjp(layer_norm, stream, norm_full[0], norm_full[1])
-    half = width // 2
-    by_half = qkv_full.reshape(width, 3, 2, half)
+    length = labels.shape[0]
+    labels_wide = jnp.broadcast_to(labels[:, None], (length, LANES))
+    labels_row = labels.reshape(length // BLOCK, 1, BLOCK)
+    blocks = hidden // width
     swap = [(0, 1), (1, 0)]
 
-    def columns_of(which):
-        return lax.dynamic_index_in_dim(by_half, which, 2, keepdims=False).reshape(width, 3 * half)
-
-    own_columns = columns_of(position)
-    sent_columns = columns_of(1 - position)
-    received = lax.ppermute(matmul(normed, sent_columns), "sp", swap)
-    own = matmul(normed, own_columns)
-    out_own, out_sent, logs = attend_forward(own, received, places, labels)
-    out_in = lax.ppermute(out_sent, "sp", swap)
-
-    def whole_rows(mine, theirs):
-        return jnp.where(position == 0, jnp.concatenate([mine, theirs], 1), jnp.concatenate([theirs, mine], 1))
-
-    attended_rows = whole_rows(out_own, out_in)
-    residual = stream + matmul(attended_rows, out_full)
-    normed_two, norm2_pull = jax.vjp(layer_norm, residual, norm_full[2], norm_full[3])
-    hidden_pre = matmul(normed_two, up_full)
-    hidden, gelu_pull = jax.vjp(gelu_tanh, hidden_pre)
-    block_out = residual + matmul(hidden, down_full)
-    grad_rows = cotangent[0]
-    grad_down = matmul_tn(hidden, grad_rows)
-    down_part = lax.psum_scatter(grad_down, "fsdp", scatter_dimension=0, tiled=True)
-    later_rows, _ = lax.optimization_barrier((grad_rows, grad_down))
-    (grad_pre,) = gelu_pull(matmul_nt(later_rows, down_full))
-    grad_resid_norm, grad_gain_two, grad_offset_two = norm2_pull(matmul_nt(grad_pre, up_full))
-    grad_resid = grad_rows + grad_resid_norm
-    out_by_half = out_full.reshape(2, half, width)
-    grad_sent = matmul_nt(grad_resid, lax.dynamic_index_in_dim(out_by_half, 1 - position, 0, keepdims=False))
-    grad_in = lax.ppermute(grad_sent, "sp", swap)
-    grad_own = matmul_nt(grad_resid, lax.dynamic_index_in_dim(out_by_half, position, 0, keepdims=False))
-    parts = attend_backward(own, received, out_own, out_sent, grad_own, grad_in, logs, places, labels)
-    mine = jnp.concatenate(parts[:3], axis=1)
-    theirs = lax.ppermute(jnp.concatenate(parts[3:], axis=1), "sp", swap)
-    grad_normed = matmul_nt(mine, own_columns) + matmul_nt(theirs, sent_columns)
-    low = jnp.where(position == 0, mine, theirs).reshape(rows, 3, 1, half)
-    high = jnp.where(position == 0, theirs, mine).reshape(rows, 3, 1, half)
-    grad_proj = jnp.concatenate([low, high], axis=2).reshape(rows, 3 * width)
-    grad_stream_norm, grad_gain_one, grad_offset_one = norm1_pull(grad_normed)
-    grad_stream = grad_resid + grad_stream_norm
-    vectors = jnp.stack([grad_gain_one, grad_offset_one, grad_gain_two, grad_offset_two] + [jnp.zeros_like(grad_gain_one)] * 4)
+    qkv_own = w_qkv.reshape(piece, 3, 2, 3, LANES).transpose(0, 2, 3, 1, 4).reshape(piece, 3 * width)
+    vectors_own = lax.dynamic_update_slice(
+        jnp.zeros((8, width), F32),
+        jnp.concatenate([jnp.stack([norm1_gain, norm1_bias, norm2_gain, norm2_bias]), jnp.zeros((4, piece), F32)]),
+        (0, index * piece),
+    )
+    (stream, normed, normed_turned, patches_turned, in_full, qkv_full, out_full, vectors, *sent) = gather_stream(
+        patches[0], w_in, qkv_own, w_out, vectors_own
+    )
+    up_own = w_up.reshape(piece, owners, blocks, piece).transpose(2, 0, 1, 3).reshape(blocks * piece, width)
+    stacked = jnp.concatenate([up_own, w_down], axis=0)
+    stacked, _ = lax.optimization_barrier((stacked, vectors))
+    weights = lax.all_gather(stacked, "fsdp", axis=0, tiled=True).reshape(owners, 2 * blocks * piece, width)
+    received = [lax.ppermute(part, "sp", swap) for part in sent]
+    own = project_own(places, normed, qkv_full)
+    attended = [attend_forward(a, b, places, labels, labels_wide, labels_row) for a, b in zip(own, received)]
+    out_in = [lax.ppermute(part[1], "sp", swap) for part in attended]
+    (block_out, grad_pre, grad_down, grad_resid, normed_two_turned, attended_turned,
+     *grads) = middle(
+        places, [part[0] for part in attended], out_in, stream, cotangent[0], out_full.reshape(width, width), vectors, weights
+    )
+    grad_sent, grad_own, sums = grads[:3], grads[3:6], grads[6]
+    down_part = lax.psum_scatter(
+        grad_down.reshape(hidden, width), "fsdp", scatter_dimension=0, tiled=True
+    )
+    grad_in = [lax.ppermute(part, "sp", swap) for part in grad_sent]
+    both = [
+        attend_backward(own[i], received[i], attended[i][0], attended[i][1], grad_own[i], grad_in[i], attended[i][2],
+                        places, labels, labels_wide, labels_row)
+        for i in range(3)
+    ]
+    mine = [pair[0] for pair in both]
+    theirs = [lax.ppermute(pair[1], "sp", swap) for pair in both]
+    part = grad_normed_part(places, mine, qkv_full)
+    grad_stream, sums = grad_of_stream(places, theirs, qkv_full, part, stream, grad_resid, vectors, sums)
     pieces, grad_patch, vector_sums, total_down = reduce_gradients(
-        [normed_two.T, attended_rows.T, normed.T, patch_rows.T],
-        [grad_pre, grad_resid, grad_proj, grad_stream],
-        grad_stream, in_full, vectors, down_part,
-    )
-    own_part = w_out.shape[0]
-    vector_sums = lax.dynamic_slice(vector_sums, (0, lax.axis_index("fsdp") * own_part), (4, own_part))
-
-    def across(first, last):
-        return jnp.concatenate([pieces[i] for i in range(first, last)], axis=1)
-
+        [normed_two_turned, attended_turned, normed_turned, patches_turned],
+        [grad_pre, grad_resid, mine + theirs, grad_stream],
+        grad_stream, in_full.reshape(owners * in_full.shape[3], width), sums, down_part,
+    )
+    vector_sums = lax.dynamic_slice(vector_sums, (0, index * piece), (4, piece))
+    grad_up = pieces[:blocks].reshape(blocks, piece, owners, piece).transpose(1, 2, 0, 3).reshape(piece, hidden)
+    first = blocks + 1
+    grad_qkv = jnp.concatenate([pieces[first + i] for i in range(3)], axis=1)
+    grad_qkv = grad_qkv.reshape(piece, 2, 3, 3, LANES).transpose(0, 3, 1, 2, 4).reshape(piece, 3 * width)
+    grad_w_in = pieces[first + 3:].reshape(w_in.shape)
     return (
-        block_out[None], grad_patch[None], pieces[8:16].reshape(8 * PIECE, width), vector_sums[0], vector_sums[1],
-        across(5, 8), pieces[4], vector_sums[2], vector_sums[3], across(0, 4), total_down,
+        block_out[None], grad_patch[None], grad_w_in, vector_sums[0], vector_sums[1],
+        grad_qkv, pieces[blocks], vector_sums[2], vector_sums[3], grad_up, total_down,
     )
 
 

time: 807 us -> 656 us (0.81)
  Pallas kernels: 256 us -> 447 us
  waiting for transfers between devices: 251 us -> 125 us
  matrix products: 113 us -> 0 us
  local copies, waits for them, and re-layouts: 110 us -> 47.1 us
  blocking collectives: 23.5 us -> 0 us
  other arithmetic: 22.4 us -> 1.12 us
    pallas_call x3 -> x12, Pallas kernels: 256 us -> 447 us  [the longest x1 191 us: reduce_gradients(): pl.pallas_call(functools.partial(scatter_kernel, tuple(plan), tuple(group...]
    all_gather x5 -> x1, waiting for transfers between devices: 153 us -> 26.3 us  [fast_shards(): lax.all_gather(stacked, 'fsdp', axis=0, tiled=True)]
    dot_general x13 -> x0, matrix products: 113 us -> none  [the longest x6 59.7 us: matmul(): jnp.dot(left_side, right_side, precision=lax.Precision.HIGH, preferred_el...]
    dynamic_slice x2 -> x1, local copies, waits for them, and re-layouts: 28.6 us -> 0.77 us  [fast_shards(): vector_sums = lax.dynamic_slice(vector_sums, (0, index * piece), (4, piece))]
    reduce_scatter x1, waiting for transfers between devices: 0.01 us -> 26 us  [fast_shards(): lax.psum_scatter(grad_down.reshape(hidden, width), 'fsdp', scatter_dimens...]
    all_gather x1 -> x0, blocking collectives: 23.5 us -> none  [fast_shards(): norm_full = lax.all_gather(norm_params, 'fsdp', axis=1, tiled=True)]
    ppermute x4 -> x12, waiting for transfers between devices: 95.5 us -> 72.9 us  [the longest x3 34.6 us: fast_shards(): received = [lax.ppermute(part, 'sp', swap) for part in sent]]
    transpose x2 -> x3, local copies, waits for them, and re-layouts: 15.8 us -> 1.32 us  [the longest x1 1.01 us: fast_shards(): pieces[:blocks].reshape(blocks, piece, owners, piece).transpose(1, 2, 0, 3)]
  transfers between devices with their start and end apart: 10 -> 14, of which waited for: 7 -> 8; matrix products, arithmetic and copies ran while one was open for 27% -> 0% of each run, Pallas kernels for 8% -> 9%
where the time goes in v3:
time: 656 us; the launch traced here: 649 us
  Pallas kernels  447 us (68%)
  waiting for transfers between devices  125 us (19%)
  local copies, waits for them, and re-layouts  47.1 us (7%)
  between operations  14.9 us (2%)
  starting transfers between devices  13.1 us (2%)
    pallas_call x1, Pallas kernels, reduce_gradients(): pl.pallas_call(functools.partial(scatter_kernel, tuple(plan), tuple(group...  191 us
    pallas_call x1, Pallas kernels, gather_stream(): pl.pallas_call(gather_kernel, out_shape=[array(rows, width), array(rows,...  139 us
    pallas_call x1, Pallas kernels, middle(): pl.pallas_call(middle_kernel, grid_spec=pltpu.PrefetchScalarGridSpec(num_...  56.4 us
    ppermute x3, waiting for transfers between devices, fast_shards(): received = [lax.ppermute(part, 'sp', swap) for part in sent]  34.6 us
    ppermute x3, waiting for transfers between devices, fast_shards(): theirs = [lax.ppermute(pair[1], 'sp', swap) for pair in both]  29.2 us
    unnamed x106, local copies, waits for them, and re-layouts  27.8 us
    all_gather x1, waiting for transfers between devices, fast_shards(): lax.all_gather(stacked, 'fsdp', axis=0, tiled=True)  26.3 us
    reduce_scatter x1, waiting for transfers between devices, fast_shards(): lax.psum_scatter(grad_down.reshape(hidden, width), 'fsdp', scatter_dimens...  26 us
  transfers between devices with their start and end apart: 14, of which 8 were waited for; matrix products, arithmetic and copies ran while one was open for 0% of the time, Pallas kernels for 9%

profile of v3, /device:TPU:0, one launch (start us, length us, event | category | flops | bytes accessed | tf_op | source)
XLA Modules:
  0.0 648.8 jit_solution(8894760924781761252)
XLA Ops:
  9.6 2.6 reshape.74
  16.5 139.5 %gather_stream.1 = (f32[512,768]{1,0:T(8,128)}, f32[512,768]{1,0:T(8,128)}, f32[768,512]{1,0:T(8,128)}, f32[6144,512]{1,0:T(8,128)}, f32[4,2,2,384,768]{4,3,2,1,...) custom-call(f32[512,6144]{1,0:T(8,128)} %bitcast.72, ...), custom_call_target="tpu_custom_call" | custom-call | flops 14495514624 | bytes 90000000 | tf_op jit(solution)/shard_map/gather_stream/pallas_call | solution.py:1172
  157.2 1.5 collective-permute-start
  159.2 3.0 copy-done
  162.2 1.4 copy-done.18
  163.6 4.7 project_own.1
  168.3 8.6 %collective-permute-done.2.refs_1_ = f32[512,384]{1,0:T(8,128)S(1)} collective-permute-done((f32[512,384]{1,0:T(8,128)}, f32[512,384]{1,0:T(8,128)S(1)}, u32[]{:S(2)}, u32[]{:S(2)}) %collective-permute-start.2) | collective-permute-done | bytes 786464 | tf_op jit(solution)/shard_map/ppermute | solution.py:1438
  177.1 6.8 %attend_forward.5 = (f32[512,128]{1,0:T(8,128)S(1)}, f32[512,128]{1,0:T(8,128)S(1)}, f32[1024,128]{1,0:T(8,128)S(1)}) custom-call(s32[1]{0:T(128)} %bitcast.pos_ref, s32[1024]{0:T(1024)S(1)} %bitcast.47, f32[512,384]{1,0:T(8,128)S(1)} %get-tuple-element.68.refs_0_, f32[512,384]{1,0:T(8,128)S(1)} %collective-permute-done.2.refs_1_, ...), custom_call_target="tpu_custom_call" | custom-call | flops 6000000000 | bytes 1835008 | tf_op jit(solution)/shard_map/attend_forward/pallas_call | solution.py:372
  184.6 26.0 %collective-permute-done.1.refs_1_ = f32[512,384]{1,0:T(8,128)S(1)} collective-permute-done((f32[512,384]{1,0:T(8,128)}, f32[512,384]{1,0:T(8,128)S(1)}, u32[]{:S(2)}, u32[]{:S(2)}) %collective-permute-start.1) | collective-permute-done | bytes 786464 | tf_op jit(solution)/shard_map/ppermute | solution.py:1438
  210.6 6.8 %attend_forward.4 = (f32[512,128]{1,0:T(8,128)S(1)}, f32[512,128]{1,0:T(8,128)S(1)}, f32[1024,128]{1,0:T(8,128)S(1)}) custom-call(s32[1]{0:T(128)} %bitcast.pos_ref, s32[1024]{0:T(1024)S(1)} %bitcast.49, f32[512,384]{1,0:T(8,128)S(1)} %get-tuple-element.65.refs_0_, f32[512,384]{1,0:T(8,128)S(1)} %collective-permute-done.1.refs_1_, ...), custom_call_target="tpu_custom_call" | custom-call | flops 6000000000 | bytes 1835008 | tf_op jit(solution)/shard_map/attend_forward/pallas_call | solution.py:372
  218.7 6.8 %attend_forward.3 = (f32[512,128]{1,0:T(8,128)S(1)}, f32[512,128]{1,0:T(8,128)S(1)}, f32[1024,128]{1,0:T(8,128)S(1)}) custom-call(s32[1]{0:T(128)} %bitcast.pos_ref, s32[1024]{0:T(1024)S(1)} %bitcast.51, f32[512,384]{1,0:T(8,128)S(1)} %get-tuple-element.62.refs_0_, f32[512,384]{1,0:T(8,128)S(1)} %collective-permute-done.refs_1_, ...), custom_call_target="tpu_custom_call" | custom-call | flops 6000000000 | bytes 1835008 | tf_op jit(solution)/shard_map/attend_forward/pallas_call | solution.py:372
  227.1 1.5 collective-permute-start.3
  230.0 3.6 collective-permute-done.3.refs_3_
  233.5 26.3 %all-gather.2.cloned.1.call-done = f32[6144,768]{1,0:T(8,128)} async-done(((f32[384,768]{1,0:T(8,128)}), f32[6144,768]{1,0:T(8,128)}) %all-gather.2.cloned.1.call-update) | async-done | bytes 18874384 | tf_op jit(solution)/shard_map/all_gather | solution.py:1437
  259.8 56.4 %feed_forward.1 = (f32[512,768]{1,0:T(8,128)}, f32[512,3072]{1,0:T(8,128)}, f32[16,192,768]{2,1,0:T(8,128)}, f32[512,768]{1,0:T(8,128)}, f32[768,512]{1,0:T(8,12...) custom-call(s32[1]{0:T(128)} %bitcast.pos_ref, ...), custom_call_target="tpu_custom_call" | custom-call | flops 39862665216 | bytes 60000000 | tf_op jit(solution)/shard_map/feed_forward/pallas_call | solution.py:1313
  317.2 1.5 collective-permute-start.8
  319.3 1.5 collective-permute-start.7
  320.7 5.6 collective-permute-done.8.refs_5_
  329.6 8.3 %attend_backward.5 = (f32[512,384]{1,0:T(8,128)S(1)}, f32[512,384]{1,0:T(8,128)S(1)}) custom-call(s32[1]{0:T(128)} %bitcast.pos_ref, s32[1024]{0:T(1024)S(1)} %bitcast.53, f32[512,384]{1,0:T(8,128)S(1)} %copy-done.24, f32[512,384]{1,0:T(8,128)S(1)} %copy-done.14, f32[512,128]{1,0:T(8,128)S(1)} %copy-done.36, f32[512,128]{1,0:T(8,128)S(1)} %get-tuple-element.73.refs_3_, ...), custom_call_target="tpu_custom_call" | custom-call | flops 12999999488 | bytes 3932160 | tf_op jit(solution)/shard_map/attend_backward/pallas_call | solution.py:479
  337.8 1.6 collective-permute-start.11
  339.5 8.3 %attend_backward.4 = (f32[512,384]{1,0:T(8,128)S(1)}, f32[512,384]{1,0:T(8,128)S(1)}) custom-call(s32[1]{0:T(128)} %bitcast.pos_ref, s32[1024]{0:T(1024)S(1)} %bitcast.55, f32[512,384]{1,0:T(8,128)S(1)} %copy-done.22, f32[512,384]{1,0:T(8,128)S(1)} %copy-done.12, f32[512,128]{1,0:T(8,128)S(1)} %copy-done.34, f32[512,128]{1,0:T(8,128)S(1)} %copy-done.16, ...), custom_call_target="tpu_custom_call" | custom-call | flops 12999999488 | bytes 3932160 | tf_op jit(solution)/shard_map/attend_backward/pallas_call | solution.py:479
  348.5 8.7 %attend_backward.3 = (f32[512,384]{1,0:T(8,128)S(1)}, f32[512,384]{1,0:T(8,128)S(1)}) custom-call(s32[1]{0:T(128)} %bitcast.pos_ref, s32[1024]{0:T(1024)S(1)} %bitcast.57, f32[512,384]{1,0:T(8,128)S(1)} %copy-done.20, f32[512,384]{1,0:T(8,128)S(1)} %collective-permute-done.refs_1_, f32[512,128]{1,0:T(8,128)S(1)} %copy-done.32, ...), custom_call_target="tpu_custom_call" | custom-call | flops 12999999488 | bytes 3932160 | tf_op jit(solution)/shard_map/attend_backward/pallas_call | solution.py:479
  357.2 1.6 collective-permute-start.9
  358.8 3.3 grad_normed_part.1.part_ref
  362.1 12.3 %collective-permute-done.10.g1.refs_10_ = f32[512,384]{1,0:T(8,128)S(1)} collective-permute-done((f32[512,384]{1,0:T(8,128)S(1)}, f32[512,384]{1,0:T(8,128)S(1)}, u32[]{:S(2)}, u32[]{:S(2)}) %collective-permute-start.10) | collective-permute-done | bytes 786464 | tf_op jit(solution)/shard_map/ppermute | solution.py:1457
  374.4 16.9 %collective-permute-done.9.g0.refs_9_ = f32[512,384]{1,0:T(8,128)S(1)} collective-permute-done((f32[512,384]{1,0:T(8,128)S(1)}, f32[512,384]{1,0:T(8,128)S(1)}, u32[]{:S(2)}, u32[]{:S(2)}) %collective-permute-start.9) | collective-permute-done | bytes 786464 | tf_op jit(solution)/shard_map/ppermute | solution.py:1457
  391.3 7.0 %grad_of_stream.1 = (f32[512,768]{1,0:T(8,128)S(1)}, f32[8,768]{1,0:T(8,128)S(1)}) custom-call(s32[1]{0:T(128)} %bitcast.pos_ref, f32[512,384]{1,0:T(8,128)S(1)} %collective-permute-done.9.g0.refs_9_, f32[512,384]{1,0:T(8,128)S(1)} %collective-permute-done.10.g1.refs_10_, f32[512,384]{1,0:T(8,128)S(1)} %collective-permute-done.11.g2.refs_11_, ...), custom_call_target="tpu_custom_call" | custom-call | flops 2717908992 | bytes 14000000 | tf_op jit(solution)/shard_map/grad_of_stream/pallas_call | solution.py:1391
  401.8 26.0 %reduce-scatter.2.cloned.1.call-done.refs_16_ = f32[192,768]{1,0:T(8,128)} async-done(((f32[3072,768]{1,0:T(8,128)}), f32[192,768]{1,0:T(8,128)}) %reduce-scatter.2.cloned.1.call-update) | async-done | bytes 589840 | tf_op jit(solution)/shard_map/reduce_scatter | solution.py:1447
  427.8 190.8 %reduce_gradients.1 = (f32[16,48,768]{2,1,0:T(8,128)}, f32[512,6144]{1,0:T(8,128)}, f32[8,768]{1,0:T(8,128)}, f32[192,768]{1,0:T(8,128)}) custom-call(f32[8,2,1,48,512]{4,3,2,1,0:T(8,128)} %bitcast.79, f32[8,2,1,48,512]{4,3,2,1,0:T(8,128)} %bitcast.80, f32[8,2,1,48,512]{4,3,2,1,0:T(8,128)} %bitcast.77, f32[8,2,8,48,512]{4,3,2,1,0:T(8,128)} %bitcast.75, ...), custom_call_target="tpu_custom_call" | custom-call | flops 43486543872 | bytes 120000000 | tf_op jit(solution)/shard_map/reduce_gradients/pallas_call | solution.py:836
  620.0 1.8 slice_bitcast_fusion
  627.4 2.6 reshape.86
  630.1 10.9 %copy.36 = f32[1,512,6144]{2,1,0:T(8,128)} copy(f32[1,512,6144]{2,1,0:T(8,128)} %bitcast.59) | data formatting | bytes 25165824
  (141 shorter events, 29.9 us)
Async XLA Ops:
  7.2 252.7 %all-gather.2.cloned.1.call-start = ((), (), s32[]{:S(2)}) async-start(), calls=%async_computation.1 | async-start | bytes 20054016 | tf_op jit(solution)/shard_map/all_gather | solution.py:1437
  156.0 271.9 %reduce-scatter.2.cloned.1.call-start = ((), (), s32[]{:S(2)}) async-start(), calls=%async_computation.2 | async-start | bytes 10027008 | tf_op jit(solution)/shard_map/reduce_scatter | solution.py:1447
  156.6 20.3 %collective-permute-start.2 = (f32[512,384]{1,0:T(8,128)}, f32[512,384]{1,0:T(8,128)S(1)}, u32[]{:S(2)}, u32[]{:S(2)}) collective-permute-start(f32[512,384]{1,0:T(8,128)} %get-tuple-element.69), channel_id=1, source_target_pairs={{0,1},{1,0},{2,3},{3,2},{4,5},{5,4},{6,7},{7,6},{8,9},{9,8},{10,11... | collective-permute-start | bytes 2359304 | tf_op jit(solution)/shard_map/ppermute | solution.py:1438
  157.2 61.5 %collective-permute-start = (f32[512,384]{1,0:T(8,128)}, f32[512,384]{1,0:T(8,128)S(1)}, u32[]{:S(2)}, u32[]{:S(2)}) collective-permute-start(f32[512,384]{1,0:T(8,128)} %get-tuple-element.63), channel_id=1, source_target_pairs={{0,1},{1,0},{2,3},{3,2},{4,5},{5,4},{6,7},{7,6},{8,9},{9,8},{10,11... | collective-permute-start | bytes 2359304 | tf_op jit(solution)/shard_map/ppermute | solution.py:1438
  158.7 51.9 %collective-permute-start.1 = (f32[512,384]{1,0:T(8,128)}, f32[512,384]{1,0:T(8,128)S(1)}, u32[]{:S(2)}, u32[]{:S(2)}) collective-permute-start(f32[512,384]{1,0:T(8,128)} %get-tuple-element.66), channel_id=1, source_target_pairs={{0,1},{1,0},{2,3},{3,2},{4,5},{5,4},{6,7},{7,6},{8,9},{9,8},{10,11... | collective-permute-start | bytes 2359304 | tf_op jit(solution)/shard_map/ppermute | solution.py:1438
  163.6 13.3 %copy-start.9 = (s32[1,1024]{1,0:T(1,128)S(1)}, s32[1,1024]{1,0:T(1,128)}, u32[]{:S(2)}) copy-start(s32[1,1024]{1,0:T(1,128)} %param.13) | copy-start | bytes 12292
  168.3 15.6 %copy-start.23 = (f32[512,384]{1,0:T(8,128)}, f32[512,384]{1,0:T(8,128)S(1)}, u32[]{:S(2)}) copy-start(f32[512,384]{1,0:T(8,128)S(1)} %get-tuple-element.68.refs_0_) | copy-start | bytes 2359300
  168.3 42.3 %copy-start.21 = (f32[512,384]{1,0:T(8,128)}, f32[512,384]{1,0:T(8,128)S(1)}, u32[]{:S(2)}) copy-start(f32[512,384]{1,0:T(8,128)S(1)} %get-tuple-element.65.refs_0_) | copy-start | bytes 2359300
  168.3 50.4 %copy-start.19 = (f32[512,384]{1,0:T(8,128)}, f32[512,384]{1,0:T(8,128)S(1)}, u32[]{:S(2)}) copy-start(f32[512,384]{1,0:T(8,128)S(1)} %get-tuple-element.62.refs_0_) | copy-start | bytes 2359300
  183.9 33.5 %copy-start.29 = (f32[1024,128]{1,0:T(8,128)}, f32[1024,128]{1,0:T(8,128)S(1)}, u32[]{:S(2)}) copy-start(f32[1024,128]{1,0:T(8,128)S(1)} %get-tuple-element.95.refs_6_) | copy-start | bytes 1572868
  183.9 33.5 %copy-start.35 = (f32[512,128]{1,0:T(8,128)}, f32[512,128]{1,0:T(8,128)S(1)}, u32[]{:S(2)}) copy-start(f32[512,128]{1,0:T(8,128)S(1)} %get-tuple-element.70.refs_2_) | copy-start | bytes 786436
  184.0 44.6 %collective-permute-start.5 = (f32[512,128]{1,0:T(8,128)S(1)}, f32[512,128]{1,0:T(8,128)S(1)}, u32[]{:S(2)}, u32[]{:S(2)}) collective-permute-start(f32[512,128]{1,0:T(8,128)S(1)} %get-tuple-element.73.refs_3_), channel_id=1, source_target_pairs={{0,1},{1,0},{2,3},{3,2},{4,5},{5,4},{6,7},{7,6},{8,9},{9,8},{10,11... | collective-permute-start | bytes 786440 | tf_op jit(solution)/shard_map/ppermute | solution.py:1441
  218.2 10.4 %collective-permute-start.4 = (f32[512,128]{1,0:T(8,128)S(1)}, f32[512,128]{1,0:T(8,128)S(1)}, u32[]{:S(2)}, u32[]{:S(2)}) collective-permute-start(f32[512,128]{1,0:T(8,128)S(1)} %get-tuple-element.72.refs_3_), channel_id=1, source_target_pairs={{0,1},{1,0},{2,3},{3,2},{4,5},{5,4},{6,7},{7,6},{8,9},{9,8},{10,11... | collective-permute-start | bytes 786440 | tf_op jit(solution)/shard_map/ppermute | solution.py:1441
  227.1 6.5 collective-permute-start.3
  316.3 10.1 %copy-start.14 = (f32[512,384]{1,0:T(8,128)S(1)}, f32[512,384]{1,0:T(8,128)}, u32[]{:S(2)}) copy-start(f32[512,384]{1,0:T(8,128)} %copy-done.13) | copy-start | bytes 2359300
  316.3 10.1 %copy-start.30 = (f32[1024,128]{1,0:T(8,128)S(1)}, f32[1024,128]{1,0:T(8,128)}, u32[]{:S(2)}) copy-start(f32[1024,128]{1,0:T(8,128)} %copy-done.29) | copy-start | bytes 1572868
  317.2 9.1 %collective-permute-start.8 = (f32[512,128]{1,0:T(8,128)S(1)}, f32[512,128]{1,0:T(8,128)S(1)}, u32[]{:S(2)}, u32[]{:S(2)}) collective-permute-start(f32[512,128]{1,0:T(8,128)S(1)} %copy-done.49), channel_id=1, source_target_pairs={{0,1},{1,0},{2,3},{3,2},{4,5},{5,4},{6,7},{7,6},{8,9},{9,8},{10,11... | collective-permute-start | bytes 786440 | tf_op jit(solution)/shard_map/ppermute | solution.py:1450
  318.7 29.7 %collective-permute-start.6 = (f32[512,128]{1,0:T(8,128)}, f32[512,128]{1,0:T(8,128)S(1)}, u32[]{:S(2)}, u32[]{:S(2)}) collective-permute-start(f32[512,128]{1,0:T(8,128)} %get-tuple-element.86), channel_id=1, source_target_pairs={{0,1},{1,0},{2,3},{3,2},{4,5},{5,4},{6,7},{7,6},{8,9},{9,8},{10,11... | collective-permute-start | bytes 786440 | tf_op jit(solution)/shard_map/ppermute | solution.py:1450
  319.3 20.2 %collective-permute-start.7 = (f32[512,128]{1,0:T(8,128)}, f32[512,128]{1,0:T(8,128)S(1)}, u32[]{:S(2)}, u32[]{:S(2)}) collective-permute-start(f32[512,128]{1,0:T(8,128)} %get-tuple-element.90), channel_id=1, source_target_pairs={{0,1},{1,0},{2,3},{3,2},{4,5},{5,4},{6,7},{7,6},{8,9},{9,8},{10,11... | collective-permute-start | bytes 786440 | tf_op jit(solution)/shard_map/ppermute | solution.py:1450
  329.5 9.9 %copy-start.34 = (f32[512,128]{1,0:T(8,128)S(1)}, f32[512,128]{1,0:T(8,128)}, u32[]{:S(2)}) copy-start(f32[512,128]{1,0:T(8,128)} %copy-done.33) | copy-start | bytes 786436
  329.6 9.9 %copy-start.38 = (f32[512,128]{1,0:T(8,128)S(1)}, f32[512,128]{1,0:T(8,128)}, u32[]{:S(2)}) copy-start(f32[512,128]{1,0:T(8,128)} %get-tuple-element.89.refs_4_) | copy-start | bytes 786436
  337.8 20.9 %copy-start.4 = (f32[512,384]{1,0:T(8,128)}, f32[512,384]{1,0:T(8,128)S(1)}, u32[]{:S(2)}) copy-start(f32[512,384]{1,0:T(8,128)S(1)} %get-tuple-element.96.g2.refs_8_) | copy-start | bytes 2359300
  337.8 24.2 %collective-permute-start.11 = (f32[512,384]{1,0:T(8,128)S(1)}, f32[512,384]{1,0:T(8,128)S(1)}, u32[]{:S(2)}, u32[]{:S(2)}) collective-permute-start(f32[512,384]{1,0:T(8,128)S(1)} %get-tuple-element.99), channel_id=1, source_target_pairs={{0,1},{1,0},{2,3},{3,2},{4,5},{5,4},{6,7},{7,6},{8,9},{9,8},{10,11... | collective-permute-start | bytes 2359304 | tf_op jit(solution)/shard_map/ppermute | solution.py:1457
  339.5 19.2 %slice-start = ((s8[7077888]{0:T(1024)(128)(4,1)}), s8[4194304]{0:T(1024)(128)(4,1)S(1)}, s32[]{:S(2)}) async-start(s8[7077888]{0:T(1024)(128)(4,1)} %bitcast.44), calls=%async_computation.3 | async-start | bytes 8388608
  347.8 10.9 %copy-start.5 = (f32[512,384]{1,0:T(8,128)}, f32[512,384]{1,0:T(8,128)S(1)}, u32[]{:S(2)}) copy-start(f32[512,384]{1,0:T(8,128)S(1)} %get-tuple-element.92.g1.refs_7_) | copy-start | bytes 2359300
  347.8 26.6 %collective-permute-start.10 = (f32[512,384]{1,0:T(8,128)S(1)}, f32[512,384]{1,0:T(8,128)S(1)}, u32[]{:S(2)}, u32[]{:S(2)}) collective-permute-start(f32[512,384]{1,0:T(8,128)S(1)} %get-tuple-element.98), channel_id=1, source_target_pairs={{0,1},{1,0},{2,3},{3,2},{4,5},{5,4},{6,7},{7,6},{8,9},{9,8},{10,11... | collective-permute-start | bytes 2359304 | tf_op jit(solution)/shard_map/ppermute | solution.py:1457
  348.4 10.3 %slice-start.1 = ((s8[7077888]{0:T(1024)(128)(4,1)}), s8[2883584]{0:T(1024)(128)(4,1)S(1)}, s32[]{:S(2)}) async-start(s8[7077888]{0:T(1024)(128)(4,1)} %bitcast.44), calls=%async_computation.4 | async-start | bytes 5767168
  357.2 34.1 %collective-permute-start.9 = (f32[512,384]{1,0:T(8,128)S(1)}, f32[512,384]{1,0:T(8,128)S(1)}, u32[]{:S(2)}, u32[]{:S(2)}) collective-permute-start(f32[512,384]{1,0:T(8,128)S(1)} %get-tuple-element.97), channel_id=1, source_target_pairs={{0,1},{1,0},{2,3},{3,2},{4,5},{5,4},{6,7},{7,6},{8,9},{9,8},{10,11... | collective-permute-start | bytes 2359304 | tf_op jit(solution)/shard_map/ppermute | solution.py:1457
  358.7 32.5 %copy-start.7 = (f32[8,768]{1,0:T(8,128)S(1)}, f32[8,768]{1,0:T(8,128)}, u32[]{:S(2)}) copy-start(f32[8,768]{1,0:T(8,128)} %get-tuple-element.76.refs_9_.vectors_ref) | copy-start | bytes 73732
  358.8 32.5 %copy-start.8 = (f32[8,768]{1,0:T(8,128)S(1)}, f32[8,768]{1,0:T(8,128)}, u32[]{:S(2)}) copy-start(f32[8,768]{1,0:T(8,128)} %get-tuple-element.100.before_ref) | copy-start | bytes 73732
  362.1 36.2 %copy-start.1 = (f32[512,384]{1,0:T(8,128)}, f32[512,384]{1,0:T(8,128)S(1)}, u32[]{:S(2)}) copy-start(f32[512,384]{1,0:T(8,128)S(1)} %collective-permute-done.11.g2.refs_11_) | copy-start | bytes 2359300
  630.1 10.9 %copy-start.41 = (f32[192,768]{1,0:T(8,128)S(1)}, f32[192,768]{1,0:T(8,128)}, u32[]{:S(2)}) copy-start(f32[192,768]{1,0:T(8,128)} %get-tuple-element.138) | copy-start | bytes 1769476
  (34 other events, 134.6 us)
Sparse Core Ops, SparseCore 0:
  156.1 103.6 all-gather.1
  316.5 111.3 reduce-scatter.1

commit v4 on v3

--- a/solution.py
+++ b/solution.py
@@ -501,21 +501,24 @@
 
 MESH = pl.DeviceIdType.MESH
 PIECE = 48
-
-
-def scatter_kernel(plan, groups, *refs):
-    count = len(plan)
+FLAT_PAIRS = 2
+
+
+def back_kernel(plan, *refs):
+    up_units, out_units, qkv_units, in_units = plan
     units = sum(plan)
     pairs = units // 2
-    turned, refs = refs[:count], refs[count:]
-    grads = []
-    for group in groups:
-        grads.append(refs[:group] if group > 1 else refs[0])
-        refs = refs[group:]
-    stream_ref, weight_ref, norms_ref, extra_ref, total_ref, patch_ref, norm_total_ref, extra_total_ref = refs[:8]
-    (t_buf, g_buf, g_high, g_low, part, s_high, s_low, w_buf, p_buf, land_a, n_x, n_z, n_y, y_y, y_x, y_z, done,
-     v_c, v_x, v_y, v_z, extra_in,
-     load_sem, w_sem, p_sem, a_sem, nx_sem, nz_sem, ny_sem, yy_sem, yx_sem, yz_sem, ye_sem, v_sem, o_sem) = refs[8:]
+    first_qkv = up_units + out_units
+    first_in = first_qkv + qkv_units
+    (up_turned, out_turned, qkv_turned, in_turned, grad_pre, grad_resid, mine_0, mine_1, mine_2, got_0, sent_1, sent_2,
+     qkv_ref, stream_ref, weight_ref, vectors_ref, sums_ref,
+     up_total, out_total, qkv_total, in_total, patch_ref, norm_total_ref, got_1, got_2,
+     t_buf, g_buf, g_high, g_low, part, s_high, s_low, w_buf, p_buf, q_buf, acc, land_a, n_x, n_z, n_y, y_y, y_x, y_z, done,
+     v_own, v_c, v_x, v_y, v_z,
+     load_sem, w_sem, p_sem, q_sem, norm_sem, swap_sem,
+     a_sem, nx_sem, nz_sem, ny_sem, yy_sem, yx_sem, yz_sem, ye_sem, v_sem, o_sem) = refs
+    mine, got = (mine_0, mine_1, mine_2), (got_0, got_1, got_2)
+    width = g_buf.shape[2]
     fsdp = lax.axis_index("fsdp")
     row = lax.axis_index("sp")
     z, x, core = fsdp // 4, (fsdp // 2) % 2, fsdp % 2
@@ -539,40 +542,15 @@
             device_id=peer, device_id_type=MESH,
         )
 
-    def loads(unit, slot, act):
-        base = 0
-        for which in range(count):
-            first, last = base, base + plan[which]
-            base = last
-
-            @pl.when((unit >= first) & (unit < last))
-            def _(which=which, first=first):
-                j = unit - first
-                for side in range(2):
-                    rows_ref = turned[which]
-                    source = rows_ref.at[:, side, j] if rows_ref.shape[2] > 1 else rows_ref.at[:, side, 0]
-                    act(pltpu.make_async_copy(source, t_buf.at[slot, side], load_sem.at[slot, side]))
-                grad = grads[which]
-                width = g_buf.shape[2]
-                if groups[which] > 1:
-                    parts = groups[which] // 2
-                    for unit_at in range(plan[which]):
-                        @pl.when(j == unit_at)
-                        def _(unit_at=unit_at):
-                            for place in range(2):
-                                side, part = divmod(2 * unit_at + place, parts)
-                                for mine in range(2):
-                                    @pl.when((row == side) == (mine == 1))
-                                    def _(place=place, part=part, mine=mine):
-                                        act(pltpu.make_async_copy(
-                                            grad[part if mine else parts + part],
-                                            g_buf.at[slot, :, pl.ds(place * (width // 2), width // 2)],
-                                            load_sem.at[slot, 2 + place],
-                                        ))
-                    return
-                if grad.shape[1] > width:
-                    grad = grad.at[:, pl.ds(pl.multiple_of(j * width, width), width)]
-                act(pltpu.make_async_copy(grad, g_buf.at[slot], load_sem.at[slot, 2]))
+    def span(first, size):
+        return pl.ds(pl.multiple_of(first, size), size)
+
+    def loop(number, body):
+        def step(i, carry):
+            body(i)
+            return carry
+
+        lax.fori_loop(0, number, step, 0)
 
     def start(copy):
         copy.start()
@@ -580,31 +558,82 @@
     def wait(copy):
         copy.wait()
 
+    def loads(unit, slot, act):
+        def left(view):
+            for side in range(2):
+                act(pltpu.make_async_copy(view.at[:, side], t_buf.at[slot, side], load_sem.at[slot, side]))
+
+        def right(source):
+            act(pltpu.make_async_copy(source, g_buf.at[slot], load_sem.at[slot, 2]))
+
+        @pl.when(unit < up_units)
+        def _():
+            left(up_turned)
+            right(grad_pre.at[:, span(unit * width, width)])
+
+        @pl.when((unit >= up_units) & (unit < first_qkv))
+        def _():
+            left(out_turned)
+            right(grad_resid.at[:, span((unit - up_units) * width, width)])
+
+        @pl.when((unit >= first_qkv) & (unit < first_in))
+        def _():
+            left(qkv_turned)
+            for j in range(qkv_units):
+                kind, side = divmod(j, 2)
+                for sources, own in ((mine, True), (got, False)):
+                    @pl.when((unit == first_qkv + j) & ((row == side) == own))
+                    def _(kind=kind, sources=sources):
+                        for i, source in enumerate(sources):
+                            act(pltpu.make_async_copy(
+                                source.at[:, kind * LANES:(kind + 1) * LANES],
+                                g_buf.at[slot, :, i * LANES:(i + 1) * LANES],
+                                load_sem.at[slot, 2 + i],
+                            ))
+
+        @pl.when(unit >= first_in)
+        def _():
+            j = (unit - first_in) // 2
+            for side in range(2):
+                act(pltpu.make_async_copy(in_turned.at[:, side, j], t_buf.at[slot, side], load_sem.at[slot, side]))
+
     def weight_copy(block, slot):
         return pltpu.make_async_copy(weight_ref.at[block], w_buf.at[slot], w_sem.at[slot])
 
     def patch_copy(block, slot):
         columns = w_buf.shape[1]
-        return pltpu.make_async_copy(
-            p_buf.at[slot], patch_ref.at[:, pl.ds(pl.multiple_of(block * columns, columns), columns)], p_sem.at[slot]
-        )
+        return pltpu.make_async_copy(p_buf.at[slot], patch_ref.at[:, span(block * columns, columns)], p_sem.at[slot])
+
+    def q_copy(j):
+        return pltpu.make_async_copy(qkv_ref.at[:, :, :, :, span(j * width, width)], q_buf, q_sem)
+
+    rows = stream_ref.shape[0]
+    cut = w_buf.shape[1]
+    norm_copies = [
+        pltpu.make_async_copy(stream_ref.at[:, 0:width], p_buf.at[0], norm_sem.at[0]),
+        pltpu.make_async_copy(stream_ref.at[:, width:], p_buf.at[1], norm_sem.at[1]),
+        pltpu.make_async_copy(grad_resid.at[0:cut], w_buf.at[0], norm_sem.at[2]),
+        pltpu.make_async_copy(grad_resid.at[cut:], w_buf.at[1, 0:rows - cut], norm_sem.at[3]),
+    ]
+    swap_copies = [
+        remote(sent_1, got_1, swap_sem, (0,), across),
+        remote(sent_2, got_2, swap_sem, (1,), across),
+    ]
 
     def core_copy(unit, slot):
         return remote(part.at[slot, 1 - core], land_a.at[unit], a_sem, (unit,), sibling)
 
-    def nx_copy(p):
-        return remote(land_a.at[2 * p, :, 1 - x], n_x.at[p], nx_sem, (p,), beside)
-
-    def nz_copy(p, step):
-        return remote(n_x.at[p, (z + step + 1) % 4], n_z.at[p, step], nz_sem, (p, step), along[step])
-
-    def ny_copy(p):
-        return remote(n_x.at[p, z], n_y.at[p], ny_sem, (p,), across)
-
-    def yy_copy(p):
-        return remote(
-            land_a.at[2 * p + 1, :, :, pl.ds(pl.multiple_of((1 - row) * half, half), half)], y_y.at[p], yy_sem, (p,), across
-        )
+    def nx_copy(unit, n):
+        return remote(land_a.at[unit, :, 1 - x], n_x.at[n], nx_sem, (n,), beside)
+
+    def nz_copy(n, step):
+        return remote(n_x.at[n, (z + step + 1) % 4], n_z.at[n, step], nz_sem, (n, step), along[step])
+
+    def ny_copy(n):
+        return remote(n_x.at[n, z], n_y.at[n], ny_sem, (n,), across)
+
+    def yy_copy(unit, p):
+        return remote(land_a.at[unit, :, :, span((1 - row) * half, half)], y_y.at[p], yy_sem, (p,), across)
 
     def yx_copy(p):
         return remote(y_y.at[p, :, 1 - x], y_x.at[p], yx_sem, (p,), beside)
@@ -612,24 +641,53 @@
     def yz_copy(p, step):
         return remote(y_x.at[p, (z + step + 1) % 4], y_z.at[p, step], yz_sem, (p, step), along[step])
 
-    def ye_copy(p):
-        place = pl.ds(pl.multiple_of(row * half, half), half)
-        return remote(y_x.at[p, z], done.at[2 * p + 1, place], ye_sem, (p,), across)
-
-    loads(0, 0, start)
-    weight_copy(0, 0).start()
-    s_high[...] = stream_ref[...].astype(BF)
-    s_low[...] = (stream_ref[...] - s_high[...].astype(F32)).astype(BF)
-    pl.semaphore_wait(barrier, 6)
+    def ye_copy(unit, p):
+        return remote(y_x.at[p, z], done.at[unit, span(row * half, half)], ye_sem, (p,), across)
+
+    def flat_number(pair):
+        return pairs + pair
+
+    def other_number(pair):
+        return pair - FLAT_PAIRS
+
+    def odd(pair, flat, other):
+        @pl.when(pair < FLAT_PAIRS)
+        def _():
+            flat(2 * pair + 1, flat_number(pair))
+
+        @pl.when(pair >= FLAT_PAIRS)
+        def _():
+            other(2 * pair + 1, other_number(pair))
 
     v_copies = [
-        remote(norms_ref, v_c, v_sem, (0,), sibling),
+        remote(v_own, v_c, v_sem, (0,), sibling),
         remote(v_c, v_x, v_sem, (1,), beside),
         remote(v_x, v_y, v_sem, (2,), across),
     ] + [remote(v_y, v_z.at[step], v_sem, (3 + step,), along[step]) for step in range(3)]
-    v_copies[0].start()
-    extra_copy = remote(extra_ref, extra_in, v_sem, (6,), across)
-    extra_copy.start()
+
+    loads(jnp.int32(0), 0, start)
+    q_copy(0).start()
+    for copy in norm_copies:
+        copy.start()
+    pl.semaphore_wait(barrier, 6)
+    for copy in swap_copies:
+        copy.start()
+
+    def norm_backward():
+        for copy in norm_copies:
+            copy.wait()
+        values = jnp.concatenate([p_buf[0], p_buf[1]], axis=1)
+        back, gain, offset = norm_back(acc[...], values, vectors_ref[0:1, :])
+        v_own[...] = sums_ref[...]
+        v_own[0:1, :] = gain
+        v_own[1:2, :] = offset
+        acc[...] = back
+        acc[0:cut, :] = acc[0:cut, :] + w_buf[0]
+        acc[cut:, :] = acc[cut:, :] + w_buf[1, 0:rows - cut]
+        s_high[...] = acc[...].astype(BF)
+        s_low[...] = (acc[...] - s_high[...].astype(F32)).astype(BF)
+        weight_copy(0, 0).start()
+        v_copies[0].start()
 
     def compute(unit, slot):
         loads(unit, slot, wait)
@@ -642,9 +700,17 @@
         def _():
             core_copy(unit - 2, slot).wait_send()
 
-        grad = g_buf[slot]
-        g_high[...] = grad.astype(BF)
-        g_low[...] = (grad - g_high[...].astype(F32)).astype(BF)
+        @pl.when(unit < first_in)
+        def _():
+            grad = g_buf[slot]
+            g_high[...] = grad.astype(BF)
+            g_low[...] = (grad - g_high[...].astype(F32)).astype(BF)
+
+        @pl.when(unit >= first_in)
+        def _():
+            columns = span(((unit - first_in) % 2) * width, width)
+            g_high[...] = s_high[:, columns]
+            g_low[...] = s_low[:, columns]
 
         def side_of(turn, carry):
             side = jnp.where(turn == 0, 1 - core, core)
@@ -660,6 +726,17 @@
 
         lax.fori_loop(0, 2, side_of, 0)
 
+        @pl.when((unit >= first_qkv) & (unit < first_in))
+        def _():
+            j = unit - first_qkv
+            q_copy(j).wait()
+            weight = split_bf(q_buf[...].reshape(acc.shape[1], width))
+            acc[...] = acc[...] + three(nt, (g_high[...], g_low[...]), weight)
+
+            @pl.when(j + 1 < qkv_units)
+            def _():
+                q_copy(j + 1).start()
+
     def patch_block(block, slot):
         weight_copy(block, slot).wait()
 
@@ -671,16 +748,8 @@
         def _():
             patch_copy(block - 2, slot).wait()
 
-        high, low = split_bf(w_buf[slot])
-        p_buf[slot] = nt(s_high[...], high) + nt(s_high[...], low) + nt(s_low[...], high)
+        p_buf[slot] = three(nt, (s_high[...], s_low[...]), split_bf(w_buf[slot]))
         patch_copy(block, slot).start()
-
-    def loop(number, body):
-        def step(i, carry):
-            body(i)
-            return carry
-
-        lax.fori_loop(0, number, step, 0)
 
     def after_core(unit, slot):
         core_copy(unit, slot).wait_recv()
@@ -691,192 +760,250 @@
 
         loop(4, add)
 
+    def flat_x(unit, n):
+        nx_copy(unit, n).wait_recv()
+
+        def add(i):
+            n_x[n, i] = n_x[n, i] + land_a[unit, i, x]
+
+        loop(4, add)
+        for step in range(3):
+            nz_copy(n, step).start()
+
+    def flat_z(unit, n):
+        for step in range(3):
+            nz_copy(n, step).wait_recv()
+        n_x[n, z] = n_x[n, z] + n_z[n, 0] + n_z[n, 1] + n_z[n, 2]
+        ny_copy(n).start()
+
+    def flat_y(unit, n):
+        ny_copy(n).wait_recv()
+        done[unit] = n_x[n, z] + n_y[n]
+
+    def other_y(unit, p):
+        yy_copy(unit, p).wait_recv()
+        own = span(row * half, half)
+
+        def add(i):
+            for b in range(2):
+                y_y[p, i, b] = y_y[p, i, b] + land_a[unit, i, b, own]
+
+        loop(4, add)
+        yx_copy(p).start()
+
+    def other_x(unit, p):
+        yx_copy(p).wait_recv()
+
+        def add(i):
+            y_x[p, i] = y_x[p, i] + y_y[p, i, x]
+
+        loop(4, add)
+        for step in range(3):
+            yz_copy(p, step).start()
+
+    def other_z(unit, p):
+        for step in range(3):
+            yz_copy(p, step).wait_recv()
+        total = y_x[p, z] + y_z[p, 0] + y_z[p, 1] + y_z[p, 2]
+        y_x[p, z] = total
+        done[unit, span(row * half, half)] = total
+        ye_copy(unit, p).start()
+
+    acc[...] = jnp.zeros_like(acc)
+
     def iteration(p, carry):
+        @pl.when(p == first_qkv // 2 - 1)
+        def _():
+            for copy in swap_copies:
+                copy.wait_recv()
+
         @pl.when(p < pairs)
         def _():
             compute(2 * p, 0)
             compute(2 * p + 1, 1)
             after_core(2 * p, 0)
-            nx_copy(p).start()
+            nx_copy(2 * p, p).start()
             after_core(2 * p + 1, 1)
-            yy_copy(p).start()
+            odd(p, lambda unit, n: nx_copy(unit, n).start(), lambda unit, i: yy_copy(unit, i).start())
+
+        @pl.when(p == first_in // 2 - 1)
+        def _():
+            norm_backward()
 
         q = p - 1
 
         @pl.when((q >= 0) & (q < pairs))
         def _():
-            nx_copy(q).wait_recv()
-
-            def add_n(i):
-                n_x[q, i] = n_x[q, i] + land_a[2 * q, i, x]
-
-            loop(4, add_n)
-            for step in range(3):
-                nz_copy(q, step).start()
-            yy_copy(q).wait_recv()
-            own = pl.ds(pl.multiple_of(row * half, half), half)
-
-            def add_y(i):
-                for b in range(2):
-                    y_y[q, i, b] = y_y[q, i, b] + land_a[2 * q + 1, i, b, own]
-
-            loop(4, add_y)
-            yx_copy(q).start()
-
-        @pl.when(p < pairs)
-        def _():
-            patch_block(2 * p, 0)
-            patch_block(2 * p + 1, 1)
+            flat_x(2 * q, q)
+            odd(q, flat_x, other_y)
+
+        @pl.when((p >= first_in // 2) & (p < pairs))
+        def _():
+            patch_block(2 * p - first_in, 0)
+            patch_block(2 * p - first_in + 1, 1)
 
         r = p - 2
 
         @pl.when((r >= 0) & (r < pairs))
         def _():
-            for step in range(3):
-                nz_copy(r, step).wait_recv()
-            n_x[r, z] = n_x[r, z] + n_z[r, 0] + n_z[r, 1] + n_z[r, 2]
-            ny_copy(r).start()
-            yx_copy(r).wait_recv()
-
-            def add_x(i):
-                y_x[r, i] = y_x[r, i] + y_y[r, i, x]
-
-            loop(4, add_x)
-            for step in range(3):
-                yz_copy(r, step).start()
+            flat_z(2 * r, r)
+            odd(r, flat_z, other_x)
 
         s = p - 3
 
         @pl.when((s >= 0) & (s < pairs))
         def _():
-            ny_copy(s).wait_recv()
-            done[2 * s] = n_x[s, z] + n_y[s]
-            for step in range(3):
-                yz_copy(s, step).wait_recv()
-            total = y_x[s, z] + y_z[s, 0] + y_z[s, 1] + y_z[s, 2]
-            y_x[s, z] = total
-            done[2 * s + 1, pl.ds(pl.multiple_of(row * half, half), half)] = total
-            ye_copy(s).start()
-
-        @pl.when(p == 0)
+            flat_y(2 * s, s)
+            odd(s, flat_y, other_z)
+
+        turn = p - first_in // 2
+
+        @pl.when(turn == 0)
         def _():
             v_copies[0].wait_recv()
-            v_c[...] = v_c[...] + norms_ref[...]
+            v_c[...] = v_c[...] + v_own[...]
             v_copies[1].start()
 
-        @pl.when(p == 1)
+        @pl.when(turn == 1)
         def _():
             v_copies[1].wait_recv()
             v_x[...] = v_x[...] + v_c[...]
             v_copies[2].start()
 
-        @pl.when(p == 2)
+        @pl.when(turn == 2)
         def _():
             v_copies[2].wait_recv()
             v_y[...] = v_y[...] + v_x[...]
             for step in range(3):
                 v_copies[3 + step].start()
 
-        @pl.when(p == 3)
+        @pl.when(turn == 3)
         def _():
             for step in range(3):
                 v_copies[3 + step].wait_recv()
             norm_total_ref[...] = v_y[...] + v_z[0] + v_z[1] + v_z[2]
-            extra_copy.wait_recv()
-            extra_total_ref[...] = extra_ref[...] + extra_in[...]
 
         return carry
 
     lax.fori_loop(0, pairs + 3, iteration, 0)
 
-    def finish(p):
-        ye_copy(p).wait()
-        nx_copy(p).wait_send()
-        ny_copy(p).wait_send()
-        yy_copy(p).wait_send()
+    def flat_end(unit, n):
+        nx_copy(unit, n).wait_send()
+        ny_copy(n).wait_send()
+        for step in range(3):
+            nz_copy(n, step).wait_send()
+
+    def other_end(unit, p):
+        ye_copy(unit, p).wait()
+        yy_copy(unit, p).wait_send()
         yx_copy(p).wait_send()
         for step in range(3):
-            nz_copy(p, step).wait_send()
             yz_copy(p, step).wait_send()
 
+    def finish(p):
+        flat_end(2 * p, p)
+        odd(p, flat_end, other_end)
+
     loop(pairs, finish)
-    out = pltpu.make_async_copy(done, total_ref, o_sem)
-    out.start()
-    for copy in v_copies + [extra_copy]:
+
+    def out_copy(unit, act):
+        @pl.when(unit < up_units)
+        def _():
+            act(pltpu.make_async_copy(done.at[unit], up_total.at[:, span(unit * width, width)], o_sem.at[unit]))
+
+        @pl.when((unit >= up_units) & (unit < first_qkv))
+        def _():
+            act(pltpu.make_async_copy(done.at[unit], out_total.at[:, span((unit - up_units) * width, width)], o_sem.at[unit]))
+
+        @pl.when((unit >= first_qkv) & (unit < first_in))
+        def _():
+            act(pltpu.make_async_copy(done.at[unit], qkv_total.at[:, span((unit - first_qkv) * width, width)], o_sem.at[unit]))
+
+        @pl.when(unit >= first_in)
+        def _():
+            j = unit - first_in
+            act(pltpu.make_async_copy(
+                done.at[unit], in_total.at[span((j // 2) * PIECE, PIECE), span((j % 2) * width, width)], o_sem.at[unit]
+            ))
+
+    loop(units, lambda unit: out_copy(unit, start))
+    for copy in v_copies + swap_copies:
         copy.wait_send()
     core_copy(units - 2, 0).wait_send()
     core_copy(units - 1, 1).wait_send()
     blocks = weight_ref.shape[0]
     patch_copy(blocks - 2, 0).wait()
     patch_copy(blocks - 1, 1).wait()
-    out.wait()
-
-
-def reduce_gradients(turned, grads, grad_stream, weight, norms, extra):
-    rows, width = grad_stream.shape
-    plan, views = [], []
-    flat, groups = [], []
-    for left, right in zip(turned, grads):
-        tall = left.shape[0] // (16 * PIECE)
-        parts = list(right) if isinstance(right, (tuple, list)) else [right]
-        flat += parts
-        groups.append(len(parts))
-        plan.append(tall * (sum(part.shape[1] for part in parts) // width))
-        views.append(left.reshape(8, 2, tall, PIECE, rows))
+    loop(units, lambda unit: out_copy(unit, wait))
+
+
+def back_and_reduce(turned, grad_pre, grad_resid, mine, got, sent, qkv_full, stream, weights, vectors, sums):
+    rows, full = stream.shape
+    width = full // 2
+    owners, block, _ = weights.shape
+    piece = full // owners
+    columns = [grad_pre.shape[1], full, qkv_full.shape[4], full]
+    plan = [c // width for c in columns]
+    plan[3] *= block // piece
+    views = [left.reshape(8, 2, piece, rows) for left in turned[:3]] + [turned[3].reshape(8, 2, block // piece, piece, rows)]
     units = sum(plan)
     pairs = units // 2
-    owners = 16
-    block = weight.shape[0] // owners
-    assert units == owners
+    flats, others = pairs + FLAT_PAIRS, pairs - FLAT_PAIRS
+    assert piece == PIECE and plan[3] == owners and (plan[0] + plan[1]) % 2 == 0 and plan[2] == 6
     half = PIECE // 2
     dma = pltpu.SemaphoreType.DMA
     any_space = pl.BlockSpec(memory_space=pl.ANY)
     vmem = pl.BlockSpec(memory_space=pltpu.VMEM)
-    flops = 6 * rows * width * (units * 16 * PIECE + weight.shape[0])
+
+    def array(*shape):
+        return jax.ShapeDtypeStruct(shape, F32)
+
     return pl.pallas_call(
-        functools.partial(scatter_kernel, tuple(plan), tuple(groups)),
+        functools.partial(back_kernel, tuple(plan)),
         out_shape=[
-            jax.ShapeDtypeStruct((units, PIECE, width), F32),
-            jax.ShapeDtypeStruct((rows, weight.shape[0]), F32),
-            jax.ShapeDtypeStruct(norms.shape, F32),
-            jax.ShapeDtypeStruct(extra.shape, F32),
+            array(piece, columns[0]), array(piece, full), array(piece, columns[2]), array(block, full),
+            array(rows, owners * block), array(*vectors.shape), array(*got.shape), array(*got.shape),
         ],
-        in_specs=[any_space] * (len(views) + len(flat)) + [vmem, any_space, vmem, vmem],
-        out_specs=[any_space, any_space, vmem, vmem],
+        in_specs=[any_space] * 15 + [vmem, vmem],
+        out_specs=[any_space] * 5 + [vmem, any_space, any_space],
         scratch_shapes=[
             pltpu.VMEM((2, 2, 8, PIECE, rows), F32),
             pltpu.VMEM((2, rows, width), F32),
             pltpu.VMEM((rows, width), BF),
             pltpu.VMEM((rows, width), BF),
             pltpu.VMEM((2, 2, 4, 2, PIECE, width), F32),
-            pltpu.VMEM((rows, width), BF),
-            pltpu.VMEM((rows, width), BF),
-            pltpu.VMEM((2, block, width), F32),
+            pltpu.VMEM((rows, full), BF),
+            pltpu.VMEM((rows, full), BF),
+            pltpu.VMEM((2, block, full), F32),
             pltpu.VMEM((2, rows, block), F32),
+            pltpu.VMEM((4, 2, 2, PIECE, width), F32),
+            pltpu.VMEM((rows, full), F32),
             pltpu.VMEM((units, 4, 2, PIECE, width), F32),
-            pltpu.VMEM((pairs, 4, PIECE, width), F32),
-            pltpu.VMEM((pairs, 3, PIECE, width), F32),
-            pltpu.VMEM((pairs, PIECE, width), F32),
-            pltpu.VMEM((pairs, 4, 2, half, width), F32),
-            pltpu.VMEM((pairs, 4, half, width), F32),
-            pltpu.VMEM((pairs, 3, half, width), F32),
+            pltpu.VMEM((flats, 4, PIECE, width), F32),
+            pltpu.VMEM((flats, 3, PIECE, width), F32),
+            pltpu.VMEM((flats, PIECE, width), F32),
+            pltpu.VMEM((others, 4, 2, half, width), F32),
+            pltpu.VMEM((others, 4, half, width), F32),
+            pltpu.VMEM((others, 3, half, width), F32),
             pltpu.VMEM((units, PIECE, width), F32),
-            pltpu.VMEM(norms.shape, F32),
-            pltpu.VMEM(norms.shape, F32),
-            pltpu.VMEM(norms.shape, F32),
-            pltpu.VMEM((3,) + norms.shape, F32),
-            pltpu.VMEM(extra.shape, F32),
-            dma((2, 4)), dma((2,)), dma((2,)),
-            dma((2, units)), dma((2, pairs)), dma((2, pairs, 3)), dma((2, pairs)),
-            dma((2, pairs)), dma((2, pairs)), dma((2, pairs, 3)), dma((2, pairs)),
-            dma((2, 7)), dma,
+            pltpu.VMEM(vectors.shape, F32),
+            pltpu.VMEM(vectors.shape, F32),
+            pltpu.VMEM(vectors.shape, F32),
+            pltpu.VMEM(vectors.shape, F32),
+            pltpu.VMEM((3,) + vectors.shape, F32),
+            dma((2, 5)), dma((2,)), dma((2,)), dma, dma((4,)), dma((2, 2)),
+            dma((2, units)), dma((2, flats)), dma((2, flats, 3)), dma((2, flats)),
+            dma((2, others)), dma((2, others)), dma((2, others, 3)), dma((2, others)),
+            dma((2, 6)), dma((units,)),
         ],
-        cost_estimate=pl.CostEstimate(flops=flops, bytes_accessed=120 * 10**6, transcendentals=0),
+        cost_estimate=pl.CostEstimate(
+            flops=6 * rows * full * (units * 8 * PIECE + owners * block), bytes_accessed=130 * 10**6, transcendentals=0
+        ),
         compiler_params=pltpu.CompilerParams(
             collective_id=0, has_side_effects=True, vmem_limit_bytes=67043328
         ),
-        name="reduce_gradients",
-    )(*views, *flat, grad_stream, weight.reshape(owners, block, width), norms, extra)
+        name="back_and_reduce",
+    )(*views, grad_pre, grad_resid, *mine, got, *sent, qkv_full, stream, weights, vectors, sums)[:6]
 
 
 CUT_ROWS = 128
@@ -1123,11 +1250,15 @@
 
     lax.fori_loop(0, units + 5, iteration, 0)
     left = split_bf(acc[...])
-    group_width = sent_0.shape[1]
     last = []
     for group, ref in enumerate((sent_0, sent_1, sent_2)):
-        columns = span((1 - row) * 3 * group_width + group * group_width, group_width)
-        right = qkv_buf[:, :, :, :, columns].reshape(width, group_width)
+        right = jnp.concatenate(
+            [
+                qkv_buf[:, :, :, :, span(which * width + (1 - row) * (width // 2) + group * LANES, LANES)].reshape(width, LANES)
+                for which in range(3)
+            ],
+            axis=1,
+        )
         sent_buf[group] = three(nn, left, split_bf(right))
         copy = pltpu.make_async_copy(sent_buf.at[group], ref, last_sem.at[group])
         copy.start()
@@ -1198,9 +1329,9 @@
     )(patch_rows, w_in, w_qkv, w_out, vectors)
 
 
-def own_kernel(pos_ref, normed_ref, weight_ref, *outs):
+def own_kernel(pos_ref, normed_ref, q_ref, k_ref, v_ref, *outs):
     step = pl.program_id(0)
-    weight = weight_ref[...].reshape(normed_ref.shape[1], weight_ref.shape[4])
+    weight = jnp.concatenate([ref[...].reshape(normed_ref.shape[1], LANES) for ref in (q_ref, k_ref, v_ref)], axis=1)
     product = three(nn, split_bf(normed_ref[...]), split_bf(weight))
     for i, ref in enumerate(outs):
         @pl.when(step == i)
@@ -1219,7 +1350,9 @@
             grid=(3,),
             in_specs=[
                 pl.BlockSpec((rows, width), lambda g, pos: (0, 0)),
-                pl.BlockSpec(owners + (group,), lambda g, pos: (0, 0, 0, 0, pos[0] * 3 + g)),
+                pl.BlockSpec(owners + (LANES,), lambda g, pos: (0, 0, 0, 0, pos[0] * 3 + g)),
+                pl.BlockSpec(owners + (LANES,), lambda g, pos: (0, 0, 0, 0, 6 + pos[0] * 3 + g)),
+                pl.BlockSpec(owners + (LANES,), lambda g, pos: (0, 0, 0, 0, 12 + pos[0] * 3 + g)),
             ],
             out_specs=[pl.BlockSpec((rows, group), lambda g, pos: (0, 0))] * 3,
         ),
@@ -1227,7 +1360,7 @@
         cost_estimate=pl.CostEstimate(flops=3 * rows * width * columns, bytes_accessed=8 * 10**6, transcendentals=0),
         compiler_params=pltpu.CompilerParams(vmem_limit_bytes=40 * 1024 * 1024),
         name="project_own",
-    )(position, normed, qkv_full)
+    )(position, normed, qkv_full, qkv_full, qkv_full)
 
 
 def gelu_and_slope(values):
@@ -1318,12 +1451,12 @@
             in_specs=[head] * 6 + [
                 whole(rows, width), whole(rows, width), whole(width, width), whole(*vectors.shape),
                 pl.BlockSpec((owners, piece, width), lambda j, *_: (0, j, 0)),
-                pl.BlockSpec((owners, piece, width), lambda j, *_: (0, steps + j, 0)),
+                pl.BlockSpec((owners // steps, steps * piece, width), lambda j, *_: (j, 1, 0)),
             ],
             out_specs=[
                 whole(rows, width),
                 pl.BlockSpec((rows, width), lambda j, *_: (0, j)),
-                pl.BlockSpec((owners, piece, width), lambda j, *_: (0, j, 0)),
+                pl.BlockSpec((owners // steps, steps * piece, width), lambda j, *_: (j, 0, 0)),
                 whole(rows, width), whole(width, rows), whole(width, rows),
             ] + [head] * 6 + [whole(*vectors.shape)],
             scratch_shapes=[
@@ -1345,66 +1478,6 @@
     )(position, *out_own, *out_in, stream, cotangent, w_out, vectors, weights, weights)
 
 
-def partial_kernel(pos_ref, g0, g1, g2, weight_ref, out_ref):
-    width = out_ref.shape[1]
-    weight = weight_ref[...].reshape(width, weight_ref.shape[4])
-    left = jnp.concatenate([g0[...], g1[...], g2[...]], axis=1)
-    out_ref[...] = three(nt, split_bf(left), split_bf(weight))
-
-
-def grad_normed_part(position, grads, qkv_full):
-    rows = grads[0].shape[0]
-    owners, columns = qkv_full.shape[:4], qkv_full.shape[4]
-    width = owners[0] * owners[1] * owners[2] * owners[3]
-    part = pl.BlockSpec((rows, columns // 6), lambda i, pos: (0, 0))
-    return pl.pallas_call(
-        partial_kernel,
-        grid_spec=pltpu.PrefetchScalarGridSpec(
-            num_scalar_prefetch=1,
-            grid=(1,),
-            in_specs=[part] * 3 + [pl.BlockSpec(owners + (columns // 2,), lambda i, pos: (0, 0, 0, 0, pos[0]))],
-            out_specs=pl.BlockSpec((rows, width), lambda i, pos: (0, 0)),
-        ),
-        out_shape=jax.ShapeDtypeStruct((rows, width), F32),
-        cost_estimate=pl.CostEstimate(flops=3 * rows * width * columns, bytes_accessed=8 * 10**6, transcendentals=0),
-        compiler_params=pltpu.CompilerParams(vmem_limit_bytes=40 * 1024 * 1024),
-        name="grad_normed_part",
-    )(position, *grads, qkv_full)
-
-
-def stream_kernel(pos_ref, g0, g1, g2, weight_ref, part_ref, stream_ref, resid_ref, vectors_ref, before_ref, out_ref, sums_ref):
-    width = out_ref.shape[1]
-    weight = weight_ref[...].reshape(width, weight_ref.shape[4])
-    left = jnp.concatenate([g0[...], g1[...], g2[...]], axis=1)
-    grad = part_ref[...] + three(nt, split_bf(left), split_bf(weight))
-    back, gain, offset = norm_back(grad, stream_ref[...], vectors_ref[0:1, :])
-    out_ref[...] = resid_ref[...] + back
-    sums_ref[...] = before_ref[...]
-    sums_ref[0:1, :] = gain
-    sums_ref[1:2, :] = offset
-
-
-def grad_of_stream(position, grads, qkv_full, part, stream, grad_resid, vectors, sums):
-    rows, width = stream.shape
-    owners, columns = qkv_full.shape[:4], qkv_full.shape[4]
-    whole = lambda *shape: pl.BlockSpec(shape, lambda i, pos: (0,) * len(shape))
-    return pl.pallas_call(
-        stream_kernel,
-        grid_spec=pltpu.PrefetchScalarGridSpec(
-            num_scalar_prefetch=1,
-            grid=(1,),
-            in_specs=[whole(rows, columns // 6)] * 3
-            + [pl.BlockSpec(owners + (columns // 2,), lambda i, pos: (0, 0, 0, 0, 1 - pos[0]))]
-            + [whole(rows, width)] * 3 + [whole(*vectors.shape)] * 2,
-            out_specs=[whole(rows, width), whole(*vectors.shape)],
-        ),
-        out_shape=[jax.ShapeDtypeStruct((rows, width), F32), jax.ShapeDtypeStruct(vectors.shape, F32)],
-        cost_estimate=pl.CostEstimate(flops=3 * rows * width * columns, bytes_accessed=14 * 10**6, transcendentals=0),
-        compiler_params=pltpu.CompilerParams(vmem_limit_bytes=48 * 1024 * 1024),
-        name="grad_of_stream",
-    )(position, *grads, qkv_full, part, stream, grad_resid, vectors, sums)
-
-
 def fast_shards(
     patches, segments, w_in, norm1_gain, norm1_bias, w_qkv, w_out, norm2_gain, norm2_bias, w_up, w_down, cotangent
 ):
@@ -1422,16 +1495,12 @@
     blocks = hidden // width
     swap = [(0, 1), (1, 0)]
 
-    qkv_own = w_qkv.reshape(piece, 3, 2, 3, LANES).transpose(0, 2, 3, 1, 4).reshape(piece, 3 * width)
-    vectors_own = lax.dynamic_update_slice(
-        jnp.zeros((8, width), F32),
-        jnp.concatenate([jnp.stack([norm1_gain, norm1_bias, norm2_gain, norm2_bias]), jnp.zeros((4, piece), F32)]),
-        (0, index * piece),
-    )
+    vectors_own = jnp.tile(jnp.stack([norm1_gain, norm1_bias, norm2_gain, norm2_bias] + [norm1_gain] * 4), (1, owners))
+    vectors_own = jnp.where(jnp.arange(width)[None, :] // piece == index, vectors_own, 0.0)
     (stream, normed, normed_turned, patches_turned, in_full, qkv_full, out_full, vectors, *sent) = gather_stream(
-        patches[0], w_in, qkv_own, w_out, vectors_own
-    )
-    up_own = w_up.reshape(piece, owners, blocks, piece).transpose(2, 0, 1, 3).reshape(blocks * piece, width)
+        patches[0], w_in, w_qkv, w_out, vectors_own
+    )
+    up_own = w_up.reshape(piece, blocks, width).transpose(1, 0, 2).reshape(blocks * piece, width)
     stacked = jnp.concatenate([up_own, w_down], axis=0)
     stacked, _ = lax.optimization_barrier((stacked, vectors))
     weights = lax.all_gather(stacked, "fsdp", axis=0, tiled=True).reshape(owners, 2 * blocks * piece, width)
@@ -1445,7 +1514,7 @@
     )
     grad_sent, grad_own, sums = grads[:3], grads[3:6], grads[6]
     down_part = lax.psum_scatter(
-        grad_down.reshape(hidden, width), "fsdp", scatter_dimension=0, tiled=True
+        grad_down.reshape(hidden, width), ("fsdp", "sp"), scatter_dimension=0, tiled=True
     )
     grad_in = [lax.ppermute(part, "sp", swap) for part in grad_sent]
     both = [
@@ -1454,23 +1523,20 @@
         for i in range(3)
     ]
     mine = [pair[0] for pair in both]
-    theirs = [lax.ppermute(pair[1], "sp", swap) for pair in both]
-    part = grad_normed_part(places, mine, qkv_full)
-    grad_stream, sums = grad_of_stream(places, theirs, qkv_full, part, stream, grad_resid, vectors, sums)
-    pieces, grad_patch, vector_sums, total_down = reduce_gradients(
-        [normed_two_turned, attended_turned, normed_turned, patches_turned],
-        [grad_pre, grad_resid, mine + theirs, grad_stream],
-        grad_stream, in_full.reshape(owners * in_full.shape[3], width), sums, down_part,
+    got = lax.ppermute(both[0][1], "sp", swap)
+    grad_up, grad_out, grad_qkv, grad_w_in, grad_patch, vector_sums = back_and_reduce(
+        [normed_two_turned, attended_turned, normed_turned, patches_turned], grad_pre, grad_resid,
+        mine, got, [both[1][1], both[2][1]], qkv_full, stream, in_full.reshape(owners, in_full.shape[3], width), vectors, sums,
     )
     vector_sums = lax.dynamic_slice(vector_sums, (0, index * piece), (4, piece))
-    grad_up = pieces[:blocks].reshape(blocks, piece, owners, piece).transpose(1, 2, 0, 3).reshape(piece, hidden)
-    first = blocks + 1
-    grad_qkv = jnp.concatenate([pieces[first + i] for i in range(3)], axis=1)
-    grad_qkv = grad_qkv.reshape(piece, 2, 3, 3, LANES).transpose(0, 3, 1, 2, 4).reshape(piece, 3 * width)
-    grad_w_in = pieces[first + 3:].reshape(w_in.shape)
+    down_part, _ = lax.optimization_barrier((down_part, vector_sums))
+    down_other = lax.ppermute(down_part, "sp", swap)
+    total_down = jnp.where(
+        position == 0, jnp.concatenate([down_part, down_other]), jnp.concatenate([down_other, down_part])
+    )
     return (
         block_out[None], grad_patch[None], grad_w_in, vector_sums[0], vector_sums[1],
-        grad_qkv, pieces[blocks], vector_sums[2], vector_sums[3], grad_up, total_down,
+        grad_qkv, grad_out, vector_sums[2], vector_sums[3], grad_up, total_down,
     )
 
 

time: 656 us -> 630 us (0.960)
  waiting for transfers between devices: 125 us -> 73 us
  Pallas kernels: 447 us -> 486 us
  local copies, waits for them, and re-layouts: 47.1 us -> 35.2 us
    pallas_call x3 -> x1, Pallas kernels: 201 us -> 233 us  [back_and_reduce(): pl.pallas_call(functools.partial(back_kernel, tuple(plan)), out_shape=[ar...]
    reduce_scatter x1, waiting for transfers between devices: 26 us -> 0.01 us  [fast_shards(): lax.psum_scatter(grad_down.reshape(hidden, width), ('fsdp', 'sp'), scatte...]
    ppermute x3 -> x2, waiting for transfers between devices: 29.2 us -> 5.5 us  [the longest x1 5.5 us: fast_shards(): down_other = lax.ppermute(down_part, 'sp', swap)]
    ppermute x3, waiting for transfers between devices: 34.6 us -> 24.5 us  [fast_shards(): received = [lax.ppermute(part, 'sp', swap) for part in sent]]
    reshape x9 -> x1, local copies, waits for them, and re-layouts: 10.3 us -> 1.11 us  [fast_shards(): w_up.reshape(piece, blocks, width).transpose(1, 0, 2)]
    unnamed x106 -> x87, local copies, waits for them, and re-layouts: 27.8 us -> 31.7 us
  transfers between devices with their start and end apart: 14 -> 13, of which waited for: 8 -> 7; matrix products, arithmetic and copies ran while one was open for 0% -> 0% of each run, Pallas kernels for 9% -> 46%
where the time goes in v4:
time: 630 us; the launch traced here: 625 us
  Pallas kernels  486 us (77%)
  waiting for transfers between devices  73 us (12%)
  local copies, waits for them, and re-layouts  35.2 us (6%)
  between operations  14.7 us (2%)
  starting transfers between devices  12.1 us (2%)
    pallas_call x1, Pallas kernels, back_and_reduce(): pl.pallas_call(functools.partial(back_kernel, tuple(plan)), out_shape=[ar...  233 us
    pallas_call x1, Pallas kernels, gather_stream(): pl.pallas_call(gather_kernel, out_shape=[array(rows, width), array(rows,...  140 us
    pallas_call x1, Pallas kernels, middle(): pl.pallas_call(middle_kernel, grid_spec=pltpu.PrefetchScalarGridSpec(num_...  56.6 us
    all_gather x1, waiting for transfers between devices, fast_shards(): lax.all_gather(stacked, 'fsdp', axis=0, tiled=True)  32.3 us
    unnamed x87, local copies, waits for them, and re-layouts  31.7 us
    pallas_call x3, Pallas kernels, attend_backward(): pl.pallas_call(backward_kernel, in_specs=[smem, smem] + [vmem] * 9, out_s...  28.5 us
    ppermute x3, waiting for transfers between devices, fast_shards(): received = [lax.ppermute(part, 'sp', swap) for part in sent]  24.5 us
    pallas_call x3, Pallas kernels, attend_forward(): pl.pallas_call(forward_kernel, in_specs=[smem, smem] + [vmem] * 4, out_sp...  23.7 us
  transfers between devices with their start and end apart: 13, of which 7 were waited for; matrix products, arithmetic and copies ran while one was open for 0% of the time, Pallas kernels for 46%

profile of v4, /device:TPU:0, one launch (start us, length us, event | category | flops | bytes accessed | tf_op | source)
XLA Modules:
  0.0 624.7 jit_solution(15651139948063218426)
XLA Ops:
  8.2 1.1 copy.26
  10.0 1.1 pad_maximum_fusion
  11.0 139.5 %gather_stream.1 = (f32[512,768]{1,0:T(8,128)}, f32[512,768]{1,0:T(8,128)}, f32[768,512]{1,0:T(8,128)}, f32[6144,512]{1,0:T(8,128)}, f32[4,2,2,384,768]{4,3,2,1,...) custom-call(f32[512,6144]{1,0:T(8,128)} %bitcast.61, ...), custom_call_target="tpu_custom_call" | custom-call | flops 14495514624 | bytes 90000000 | tf_op jit(solution)/shard_map/gather_stream/pallas_call | solution.py:1303
  151.5 1.4 collective-permute-start.1
  153.6 3.0 copy-done
  156.6 1.4 copy-done.1
  158.0 4.8 project_own.1
  162.8 8.4 %collective-permute-done.2.refs_1_ = f32[512,384]{1,0:T(8,128)S(1)} collective-permute-done((f32[512,384]{1,0:T(8,128)}, f32[512,384]{1,0:T(8,128)S(1)}, u32[]{:S(2)}, u32[]{:S(2)}) %collective-permute-start.2) | collective-permute-done | bytes 786464 | tf_op jit(solution)/shard_map/ppermute | solution.py:1507
  171.3 7.7 %attend_forward.5 = (f32[512,128]{1,0:T(8,128)S(1)}, f32[512,128]{1,0:T(8,128)S(1)}, f32[1024,128]{1,0:T(8,128)S(1)}) custom-call(s32[1]{0:T(128)} %bitcast.pos_ref, s32[1024]{0:T(1024)S(1)} %bitcast.35, f32[512,384]{1,0:T(8,128)S(1)} %get-tuple-element.69.refs_0_, f32[512,384]{1,0:T(8,128)S(1)} %collective-permute-done.2.refs_1_, ...), custom_call_target="tpu_custom_call" | custom-call | flops 6000000000 | bytes 1835008 | tf_op jit(solution)/shard_map/attend_forward/pallas_call | solution.py:372
  180.4 7.6 %collective-permute-done.1.refs_1_ = f32[512,384]{1,0:T(8,128)S(1)} collective-permute-done((f32[512,384]{1,0:T(8,128)}, f32[512,384]{1,0:T(8,128)S(1)}, u32[]{:S(2)}, u32[]{:S(2)}) %collective-permute-start.1) | collective-permute-done | bytes 786464 | tf_op jit(solution)/shard_map/ppermute | solution.py:1507
  188.0 7.7 %attend_forward.4 = (f32[512,128]{1,0:T(8,128)S(1)}, f32[512,128]{1,0:T(8,128)S(1)}, f32[1024,128]{1,0:T(8,128)S(1)}) custom-call(s32[1]{0:T(128)} %bitcast.pos_ref, s32[1024]{0:T(1024)S(1)} %bitcast.37, f32[512,384]{1,0:T(8,128)S(1)} %get-tuple-element.66.refs_0_, f32[512,384]{1,0:T(8,128)S(1)} %collective-permute-done.1.refs_1_, ...), custom_call_target="tpu_custom_call" | custom-call | flops 6000000000 | bytes 1835008 | tf_op jit(solution)/shard_map/attend_forward/pallas_call | solution.py:372
  196.4 8.5 %collective-permute-done.refs_1_ = f32[512,384]{1,0:T(8,128)} collective-permute-done((f32[512,384]{1,0:T(8,128)}, f32[512,384]{1,0:T(8,128)}, u32[]{:S(2)}, u32[]{:S(2)}) %collective-permute-start) | collective-permute-done | bytes 786464 | tf_op jit(solution)/shard_map/ppermute | solution.py:1507
  205.0 8.3 %attend_forward.3 = (f32[512,128]{1,0:T(8,128)S(1)}, f32[512,128]{1,0:T(8,128)S(1)}, f32[1024,128]{1,0:T(8,128)S(1)}) custom-call(s32[1]{0:T(128)} %bitcast.pos_ref, s32[1024]{0:T(1024)S(1)} %bitcast.39, f32[512,384]{1,0:T(8,128)S(1)} %get-tuple-element.63.refs_0_, f32[512,384]{1,0:T(8,128)} %collective-permute-done.refs_1_, ...), custom_call_target="tpu_custom_call" | custom-call | flops 6000000000 | bytes 1835008 | tf_op jit(solution)/shard_map/attend_forward/pallas_call | solution.py:372
  217.5 4.7 collective-permute-done.3.refs_3_
  222.3 32.3 %all-gather.2.cloned.1.call-done = f32[6144,768]{1,0:T(8,128)} async-done(((f32[384,768]{1,0:T(8,128)}), f32[6144,768]{1,0:T(8,128)}) %all-gather.2.cloned.1.call-update) | async-done | bytes 18874384 | tf_op jit(solution)/shard_map/all_gather | solution.py:1506
  254.5 56.6 %feed_forward.1 = (f32[512,768]{1,0:T(8,128)}, f32[512,3072]{1,0:T(8,128)}, f32[16,192,768]{2,1,0:T(8,128)}, f32[512,768]{1,0:T(8,128)}, f32[768,512]{1,0:T(8,12...) custom-call(s32[1]{0:T(128)} %bitcast.pos_ref, ...), custom_call_target="tpu_custom_call" | custom-call | flops 39862665216 | bytes 60000000 | tf_op jit(solution)/shard_map/feed_forward/pallas_call | solution.py:1446
  311.1 1.5 collective-permute-start.6
  313.2 1.5 collective-permute-start.7
  314.7 5.9 collective-permute-done.6.refs_5_
  320.7 1.1 copy-done.18
  321.7 1.0 copy-done.24
  322.7 1.0 copy-done.32
  323.7 10.0 %attend_backward.3 = (f32[512,384]{1,0:T(8,128)S(1)}, f32[512,384]{1,0:T(8,128)S(1)}) custom-call(s32[1]{0:T(128)} %bitcast.pos_ref, s32[1024]{0:T(1024)S(1)} %bitcast.41, f32[512,384]{1,0:T(8,128)S(1)} %copy-done.10, f32[512,384]{1,0:T(8,128)} %collective-permute-done.refs_1_, f32[512,128]{1,0:T(8,128)S(1)} %copy-done.24, f32[512,128]{1,0:T(8,128)S(1)} %copy-done.12, ...), custom_call_target="tpu_custom_call" | custom-call | flops 12999999488 | bytes 3932160 | tf_op jit(solution)/shard_map/attend_backward/pallas_call | solution.py:479
  334.6 1.5 collective-permute-start.9
  336.1 9.2 %attend_backward.5 = (f32[512,384]{1,0:T(8,128)S(1)}, f32[512,384]{1,0:T(8,128)S(1)}) custom-call(s32[1]{0:T(128)} %bitcast.pos_ref, s32[1024]{0:T(1024)S(1)} %bitcast.43, f32[512,384]{1,0:T(8,128)S(1)} %copy-done.8, f32[512,384]{1,0:T(8,128)S(1)} %copy-done.4, f32[512,128]{1,0:T(8,128)S(1)} %copy-done.22, f32[512,128]{1,0:T(8,128)S(1)} %get-tuple-element.74.refs_3_, ...), custom_call_target="tpu_custom_call" | custom-call | flops 12999999488 | bytes 3932160 | tf_op jit(solution)/shard_map/attend_backward/pallas_call | solution.py:479
  347.2 9.2 %attend_backward.4 = (f32[512,384]{1,0:T(8,128)S(1)}, f32[512,384]{1,0:T(8,128)S(1)}) custom-call(s32[1]{0:T(128)} %bitcast.pos_ref, s32[1024]{0:T(1024)S(1)} %bitcast.45, f32[512,384]{1,0:T(8,128)S(1)} %copy-done.6, f32[512,384]{1,0:T(8,128)S(1)} %collective-permute-done.1.refs_1_, f32[512,128]{1,0:T(8,128)S(1)} %copy-done.20, ...), custom_call_target="tpu_custom_call" | custom-call | flops 12999999488 | bytes 3932160 | tf_op jit(solution)/shard_map/attend_backward/pallas_call | solution.py:479
  359.2 233.2 %back_and_reduce.1 = (f32[48,3072]{1,0:T(8,128)}, f32[48,768]{1,0:T(8,128)}, f32[48,2304]{1,0:T(8,128)}, f32[384,768]{1,0:T(8,128)}, f32[512,6144]{1,0:T(8,128)}...) custom-call(f32[8,2,48,512]{3,2,1,0:T(8,128)} %bitcast.68, f32[8,2,48,512]{3,2,1,0:T(8,128)} %bitcast.69, ...), custom_call_target="tpu_custom_call" | custom-call | flops 43486543872 | bytes 130000000 | tf_op jit(solution)/shard_map/back_and_reduce/pallas_call | solution.py:961
  593.2 2.1 collective-permute-start.10
  595.8 5.5 collective-permute-done.10
  601.3 1.9 maximum_select_fusion
  603.2 10.9 %copy.32 = f32[1,512,6144]{2,1,0:T(8,128)} copy(f32[1,512,6144]{2,1,0:T(8,128)} %bitcast.47) | data formatting | bytes 25165824
  614.1 1.0 copy.33
  (104 shorter events, 19.5 us)
Async XLA Ops:
  7.2 247.3 %all-gather.2.cloned.1.call-start = ((), (), s32[]{:S(2)}) async-start(), calls=%async_computation.1 | async-start | bytes 20054016 | tf_op jit(solution)/shard_map/all_gather | solution.py:1506
  150.6 442.6 %reduce-scatter.2.cloned.1.call-start = ((), (), s32[]{:S(2)}) async-start(), calls=%async_computation.2 | async-start | bytes 9732096 | tf_op jit(solution)/shard_map/reduce_scatter | solution.py:1516
  150.8 20.3 %collective-permute-start.2 = (f32[512,384]{1,0:T(8,128)}, f32[512,384]{1,0:T(8,128)S(1)}, u32[]{:S(2)}, u32[]{:S(2)}) collective-permute-start(f32[512,384]{1,0:T(8,128)} %get-tuple-element.70), channel_id=1, source_target_pairs={{0,1},{1,0},{2,3},{3,2},{4,5},{5,4},{6,7},{7,6},{8,9},{9,8},{10,11... | collective-permute-start | bytes 2359304 | tf_op jit(solution)/shard_map/ppermute | solution.py:1507
  151.5 36.5 %collective-permute-start.1 = (f32[512,384]{1,0:T(8,128)}, f32[512,384]{1,0:T(8,128)S(1)}, u32[]{:S(2)}, u32[]{:S(2)}) collective-permute-start(f32[512,384]{1,0:T(8,128)} %get-tuple-element.67), channel_id=1, source_target_pairs={{0,1},{1,0},{2,3},{3,2},{4,5},{5,4},{6,7},{7,6},{8,9},{9,8},{10,11... | collective-permute-start | bytes 2359304 | tf_op jit(solution)/shard_map/ppermute | solution.py:1507
  152.9 52.0 %collective-permute-start = (f32[512,384]{1,0:T(8,128)}, f32[512,384]{1,0:T(8,128)}, u32[]{:S(2)}, u32[]{:S(2)}) collective-permute-start(f32[512,384]{1,0:T(8,128)} %get-tuple-element.64), channel_id=1, source_target_pairs={{0,1},{1,0},{2,3},{3,2},{4,5},{5,4},{6,7},{7,6},{8,9},{9,8},{10,11... | collective-permute-start | bytes 2359304 | tf_op jit(solution)/shard_map/ppermute | solution.py:1507
  158.0 13.2 %copy-start.2 = (s32[1,1024]{1,0:T(1,128)S(1)}, s32[1,1024]{1,0:T(1,128)}, u32[]{:S(2)}) copy-start(s32[1,1024]{1,0:T(1,128)} %param.13) | copy-start | bytes 12292
  162.7 16.3 %copy-start.7 = (f32[512,384]{1,0:T(8,128)}, f32[512,384]{1,0:T(8,128)S(1)}, u32[]{:S(2)}) copy-start(f32[512,384]{1,0:T(8,128)S(1)} %get-tuple-element.69.refs_0_) | copy-start | bytes 2359300
  162.8 25.2 %copy-start.5 = (f32[512,384]{1,0:T(8,128)}, f32[512,384]{1,0:T(8,128)S(1)}, u32[]{:S(2)}) copy-start(f32[512,384]{1,0:T(8,128)S(1)} %get-tuple-element.66.refs_0_) | copy-start | bytes 2359300
  162.8 42.2 %copy-start.9 = (f32[512,384]{1,0:T(8,128)}, f32[512,384]{1,0:T(8,128)S(1)}, u32[]{:S(2)}) copy-start(f32[512,384]{1,0:T(8,128)S(1)} %get-tuple-element.63.refs_0_) | copy-start | bytes 2359300
  179.8 15.9 %copy-start.15 = (f32[1024,128]{1,0:T(8,128)}, f32[1024,128]{1,0:T(8,128)S(1)}, u32[]{:S(2)}) copy-start(f32[1024,128]{1,0:T(8,128)S(1)} %get-tuple-element.96.refs_6_) | copy-start | bytes 1572868
  179.8 36.3 %collective-permute-start.5 = (f32[512,128]{1,0:T(8,128)S(1)}, f32[512,128]{1,0:T(8,128)S(1)}, u32[]{:S(2)}, u32[]{:S(2)}) collective-permute-start(f32[512,128]{1,0:T(8,128)S(1)} %get-tuple-element.74.refs_3_), channel_id=1, source_target_pairs={{0,1},{1,0},{2,3},{3,2},{4,5},{5,4},{6,7},{7,6},{8,9},{9,8},{10,11... | collective-permute-start | bytes 786440 | tf_op jit(solution)/shard_map/ppermute | solution.py:1510
  195.7 17.5 %copy-start.13 = (f32[1024,128]{1,0:T(8,128)}, f32[1024,128]{1,0:T(8,128)S(1)}, u32[]{:S(2)}) copy-start(f32[1024,128]{1,0:T(8,128)S(1)} %get-tuple-element.92.refs_6_) | copy-start | bytes 1572868
  195.7 17.5 %copy-start.19 = (f32[512,128]{1,0:T(8,128)}, f32[512,128]{1,0:T(8,128)S(1)}, u32[]{:S(2)}) copy-start(f32[512,128]{1,0:T(8,128)S(1)} %get-tuple-element.68.refs_1_.refs_2_) | copy-start | bytes 786436
  195.7 20.4 %collective-permute-start.4 = (f32[512,128]{1,0:T(8,128)S(1)}, f32[512,128]{1,0:T(8,128)S(1)}, u32[]{:S(2)}, u32[]{:S(2)}) collective-permute-start(f32[512,128]{1,0:T(8,128)S(1)} %get-tuple-element.73.refs_3_), channel_id=1, source_target_pairs={{0,1},{1,0},{2,3},{3,2},{4,5},{5,4},{6,7},{7,6},{8,9},{9,8},{10,11... | collective-permute-start | bytes 786440 | tf_op jit(solution)/shard_map/ppermute | solution.py:1510
  214.8 7.5 %collective-permute-start.3 = (f32[512,128]{1,0:T(8,128)S(1)}, f32[512,128]{1,0:T(8,128)}, u32[]{:S(2)}, u32[]{:S(2)}) collective-permute-start(f32[512,128]{1,0:T(8,128)S(1)} %get-tuple-element.72.refs_3_), channel_id=1, source_target_pairs={{0,1},{1,0},{2,3},{3,2},{4,5},{5,4},{6,7},{7,6},{8,9},{9,8},{10,11... | collective-permute-start | bytes 786440 | tf_op jit(solution)/shard_map/ppermute | solution.py:1510
  311.1 9.6 %copy-start.10 = (f32[512,384]{1,0:T(8,128)S(1)}, f32[512,384]{1,0:T(8,128)}, u32[]{:S(2)}) copy-start(f32[512,384]{1,0:T(8,128)} %copy-done.9) | copy-start | bytes 2359300
  311.1 9.6 %copy-start.12 = (f32[512,128]{1,0:T(8,128)S(1)}, f32[512,128]{1,0:T(8,128)}, u32[]{:S(2)}) copy-start(f32[512,128]{1,0:T(8,128)} %copy-done.11) | copy-start | bytes 786436
  311.1 9.5 %collective-permute-start.6 = (f32[512,128]{1,0:T(8,128)}, f32[512,128]{1,0:T(8,128)}, u32[]{:S(2)}, u32[]{:S(2)}) collective-permute-start(f32[512,128]{1,0:T(8,128)} %get-tuple-element.87), channel_id=1, source_target_pairs={{0,1},{1,0},{2,3},{3,2},{4,5},{5,4},{6,7},{7,6},{8,9},{9,8},{10,11... | collective-permute-start | bytes 786440 | tf_op jit(solution)/shard_map/ppermute | solution.py:1519
  312.7 23.4 %collective-permute-start.8 = (f32[512,128]{1,0:T(8,128)}, f32[512,128]{1,0:T(8,128)S(1)}, u32[]{:S(2)}, u32[]{:S(2)}) collective-permute-start(f32[512,128]{1,0:T(8,128)} %get-tuple-element.95), channel_id=1, source_target_pairs={{0,1},{1,0},{2,3},{3,2},{4,5},{5,4},{6,7},{7,6},{8,9},{9,8},{10,11... | collective-permute-start | bytes 786440 | tf_op jit(solution)/shard_map/ppermute | solution.py:1519
  313.2 34.0 %collective-permute-start.7 = (f32[512,128]{1,0:T(8,128)}, f32[512,128]{1,0:T(8,128)S(1)}, u32[]{:S(2)}, u32[]{:S(2)}) collective-permute-start(f32[512,128]{1,0:T(8,128)} %get-tuple-element.91), channel_id=1, source_target_pairs={{0,1},{1,0},{2,3},{3,2},{4,5},{5,4},{6,7},{7,6},{8,9},{9,8},{10,11... | collective-permute-start | bytes 786440 | tf_op jit(solution)/shard_map/ppermute | solution.py:1519
  323.6 12.4 %copy-start.4 = (f32[512,384]{1,0:T(8,128)S(1)}, f32[512,384]{1,0:T(8,128)}, u32[]{:S(2)}) copy-start(f32[512,384]{1,0:T(8,128)} %copy-done.3) | copy-start | bytes 2359300
  323.7 12.4 %copy-start.8 = (f32[512,384]{1,0:T(8,128)S(1)}, f32[512,384]{1,0:T(8,128)}, u32[]{:S(2)}) copy-start(f32[512,384]{1,0:T(8,128)} %copy-done.7) | copy-start | bytes 2359300
  323.7 12.4 %copy-start.16 = (f32[1024,128]{1,0:T(8,128)S(1)}, f32[1024,128]{1,0:T(8,128)}, u32[]{:S(2)}) copy-start(f32[1024,128]{1,0:T(8,128)} %copy-done.15) | copy-start | bytes 1572868
  323.7 12.4 %copy-start.22 = (f32[512,128]{1,0:T(8,128)S(1)}, f32[512,128]{1,0:T(8,128)}, u32[]{:S(2)}) copy-start(f32[512,128]{1,0:T(8,128)} %copy-done.21) | copy-start | bytes 786436
  323.7 12.4 %copy-start.31 = (f32[512,128]{1,0:T(8,128)S(1)}, f32[512,128]{1,0:T(8,128)}, u32[]{:S(2)}) copy-start(f32[512,128]{1,0:T(8,128)} %get-tuple-element.94.refs_4_) | copy-start | bytes 786436
  334.6 23.7 %collective-permute-start.9 = (f32[512,384]{1,0:T(8,128)S(1)}, f32[512,384]{1,0:T(8,128)S(1)}, u32[]{:S(2)}, u32[]{:S(2)}) collective-permute-start(f32[512,384]{1,0:T(8,128)S(1)} %get-tuple-element.98), channel_id=1, source_target_pairs={{0,1},{1,0},{2,3},{3,2},{4,5},{5,4},{6,7},{7,6},{8,9},{9,8},{10,11... | collective-permute-start | bytes 2359304 | tf_op jit(solution)/shard_map/ppermute | solution.py:1526
  336.1 11.1 %copy-start.6 = (f32[512,384]{1,0:T(8,128)S(1)}, f32[512,384]{1,0:T(8,128)}, u32[]{:S(2)}) copy-start(f32[512,384]{1,0:T(8,128)} %copy-done.5) | copy-start | bytes 2359300
  336.1 11.1 %copy-start.14 = (f32[1024,128]{1,0:T(8,128)S(1)}, f32[1024,128]{1,0:T(8,128)}, u32[]{:S(2)}) copy-start(f32[1024,128]{1,0:T(8,128)} %copy-done.13) | copy-start | bytes 1572868
  336.1 11.1 %copy-start.20 = (f32[512,128]{1,0:T(8,128)S(1)}, f32[512,128]{1,0:T(8,128)}, u32[]{:S(2)}) copy-start(f32[512,128]{1,0:T(8,128)} %copy-done.19) | copy-start | bytes 786436
  336.1 11.1 %copy-start.30 = (f32[512,128]{1,0:T(8,128)S(1)}, f32[512,128]{1,0:T(8,128)}, u32[]{:S(2)}) copy-start(f32[512,128]{1,0:T(8,128)} %get-tuple-element.90.refs_4_) | copy-start | bytes 786436
  593.2 8.1 %collective-permute-start.10 = (f32[96,768]{1,0:T(8,128)}, f32[96,768]{1,0:T(8,128)S(1)}, u32[]{:S(2)}, u32[]{:S(2)}) collective-permute-start(f32[96,768]{1,0:T(8,128)} %reduce-scatter.2.cloned.1.call-done), channel_id=1, source_target_pairs={{0,1},{1,0},{2,3},{3,2},{4,5},{5,4},{6,7},{7,6},{8,9},{9,8},{10,11... | collective-permute-start | bytes 884744 | tf_op jit(solution)/shard_map/ppermute | solution.py:1533
  603.2 10.9 %copy-start.33 = (f32[384,768]{1,0:T(8,128)S(1)}, f32[384,768]{1,0:T(8,128)}, u32[]{:S(2)}) copy-start(f32[384,768]{1,0:T(8,128)} %get-tuple-element.128) | copy-start | bytes 3538948
  (22 other events, 33.9 us)
Sparse Core Ops, SparseCore 0:
  150.7 103.7 all-gather.1
  311.3 173.6 reduce-scatter.1

commit v5 on v4

--- a/solution.py
+++ b/solution.py
@@ -1201,6 +1201,11 @@
     for copy in own_copies:
         copy.wait()
 
+    sent_copies = [
+        pltpu.make_async_copy(sent_buf.at[group], ref, last_sem.at[group])
+        for group, ref in enumerate((sent_0, sent_1, sent_2))
+    ]
+
     def iteration(t, carry):
         z_stage(t + 2)
         x_stage(t)
@@ -1246,24 +1251,25 @@
             normed_ref[...] = acc[...]
             turned_ref[...] = jnp.transpose(acc[...])
 
+        @pl.when(t == units - out_units + 4)
+        def _():
+            left = split_bf(acc[...])
+            for group in range(3):
+                right = jnp.concatenate(
+                    [
+                        qkv_buf[:, :, :, :, span(which * width + (1 - row) * (width // 2) + group * LANES, LANES)].reshape(
+                            width, LANES
+                        )
+                        for which in range(3)
+                    ],
+                    axis=1,
+                )
+                sent_buf[group] = three(nn, left, split_bf(right))
+                sent_copies[group].start()
+
         return carry
 
     lax.fori_loop(0, units + 5, iteration, 0)
-    left = split_bf(acc[...])
-    last = []
-    for group, ref in enumerate((sent_0, sent_1, sent_2)):
-        right = jnp.concatenate(
-            [
-                qkv_buf[:, :, :, :, span(which * width + (1 - row) * (width // 2) + group * LANES, LANES)].reshape(width, LANES)
-                for which in range(3)
-            ],
-            axis=1,
-        )
-        sent_buf[group] = three(nn, left, split_bf(right))
-        copy = pltpu.make_async_copy(sent_buf.at[group], ref, last_sem.at[group])
-        copy.start()
-        last.append(copy)
-
     def finish(unit, carry):
         def act(kind):
             for step in range(3):
@@ -1282,7 +1288,7 @@
         copy.wait_send()
     for slot in range(each):
         turn_copy(tiles - each + slot, slot).wait()
-    for copy in last:
+    for copy in sent_copies:
         copy.wait()
 
 
@@ -1381,12 +1387,48 @@
     return back, jnp.sum(grad * zhat, axis=0, keepdims=True), jnp.sum(grad, axis=0, keepdims=True)
 
 
+def residual_kernel(pos_ref, *refs):
+    own_parts, in_parts = refs[0:3], refs[3:6]
+    (stream_ref, cot_ref, out_ref, vectors_ref,
+     residual_ref, norm_high, norm_low, cot_high, cot_low, turned_ref, attended_ref) = refs[6:]
+    half = out_ref.shape[0] // 2
+    own = pl.ds(pl.multiple_of(pos_ref[0] * half, half), half)
+    other = pl.ds(pl.multiple_of((1 - pos_ref[0]) * half, half), half)
+    total = stream_ref[...]
+    for span, parts in ((own, own_parts), (other, in_parts)):
+        left = jnp.concatenate([part[...] for part in parts], axis=1)
+        attended_ref[span, :] = jnp.transpose(left)
+        total = total + three(nn, split_bf(left), split_bf(out_ref[span, :]))
+    residual_ref[...] = total
+    zhat, _ = normalized(total)
+    normed = zhat * vectors_ref[2:3, :] + vectors_ref[3:4, :]
+    turned_ref[...] = jnp.transpose(normed)
+    norm_high[...], norm_low[...] = split_bf(normed)
+    cot_high[...], cot_low[...] = split_bf(cot_ref[...])
+
+
+def residual_norm(position, out_own, out_in, stream, cotangent, w_out, vectors):
+    rows, width = stream.shape
+    vmem = pl.BlockSpec(memory_space=pltpu.VMEM)
+
+    def array(*shape, kind=F32):
+        return jax.ShapeDtypeStruct(shape, kind)
+
+    return pl.pallas_call(
+        residual_kernel,
+        in_specs=[pl.BlockSpec(memory_space=pltpu.SMEM)] + [vmem] * 10,
+        out_specs=[vmem] * 7,
+        out_shape=[array(rows, width)] + [array(rows, width, kind=BF)] * 4 + [array(width, rows)] * 2,
+        cost_estimate=pl.CostEstimate(flops=6 * rows * width * width, bytes_accessed=18 * 10**6, transcendentals=0),
+        compiler_params=pltpu.CompilerParams(vmem_limit_bytes=40 * 1024 * 1024),
+        name="residual_norm",
+    )(position, *out_own, *out_in, stream, cotangent, w_out, vectors)
+
+
 def middle_kernel(pos_ref, *refs):
-    own_parts, in_parts = refs[0:3], refs[3:6]
-    (stream_ref, cot_ref, out_ref, vectors_ref, up_ref, down_ref,
-     block_ref, grad_pre_ref, grad_down_ref, grad_resid_ref, turned_ref, attended_ref) = refs[6:18]
-    sent_refs, own_refs, sums_ref = refs[18:21], refs[21:24], refs[24]
-    residual, norm_high, norm_low, cot_high, cot_low, grad_norm = refs[25:]
+    (residual, norm_high, norm_low, cot_high, cot_low, cot_ref, out_ref, vectors_ref, up_ref, down_ref,
+     block_ref, grad_pre_ref, grad_down_ref, grad_resid_ref) = refs[:14]
+    sent_refs, own_refs, sums_ref, grad_norm = refs[14:17], refs[17:20], refs[20], refs[21]
     step = pl.program_id(0)
     width = out_ref.shape[0]
     half = width // 2
@@ -1395,18 +1437,7 @@
 
     @pl.when(step == 0)
     def _():
-        total = stream_ref[...]
-        for span, parts in ((own, own_parts), (other, in_parts)):
-            left = jnp.concatenate([part[...] for part in parts], axis=1)
-            attended_ref[span, :] = jnp.transpose(left)
-            total = total + three(nn, split_bf(left), split_bf(out_ref[span, :]))
-        residual[...] = total
-        block_ref[...] = total
-        zhat, _ = normalized(total)
-        normed = zhat * vectors_ref[2:3, :] + vectors_ref[3:4, :]
-        turned_ref[...] = jnp.transpose(normed)
-        norm_high[...], norm_low[...] = split_bf(normed)
-        cot_high[...], cot_low[...] = split_bf(cot_ref[...])
+        block_ref[...] = residual[...]
         grad_norm[...] = jnp.zeros_like(grad_norm)
 
     up = split_bf(up_ref[...].reshape(width, width))
@@ -1435,8 +1466,8 @@
                 ref[...] = product[:, i * LANES:(i + 1) * LANES]
 
 
-def middle(position, out_own, out_in, stream, cotangent, w_out, vectors, weights):
-    rows, width = stream.shape
+def middle(position, residual, norm, cot, cotangent, w_out, vectors, weights):
+    rows, width = residual.shape
     owners, stacked = weights.shape[0], weights.shape[1]
     piece = width // owners
     steps = stacked // piece // 2
@@ -1448,8 +1479,8 @@
         grid_spec=pltpu.PrefetchScalarGridSpec(
             num_scalar_prefetch=1,
             grid=(steps,),
-            in_specs=[head] * 6 + [
-                whole(rows, width), whole(rows, width), whole(width, width), whole(*vectors.shape),
+            in_specs=[whole(rows, width)] * 6 + [
+                whole(width, width), whole(*vectors.shape),
                 pl.BlockSpec((owners, piece, width), lambda j, *_: (0, j, 0)),
                 pl.BlockSpec((owners // steps, steps * piece, width), lambda j, *_: (j, 1, 0)),
             ],
@@ -1457,25 +1488,19 @@
                 whole(rows, width),
                 pl.BlockSpec((rows, width), lambda j, *_: (0, j)),
                 pl.BlockSpec((owners // steps, steps * piece, width), lambda j, *_: (j, 0, 0)),
-                whole(rows, width), whole(width, rows), whole(width, rows),
+                whole(rows, width),
             ] + [head] * 6 + [whole(*vectors.shape)],
-            scratch_shapes=[
-                pltpu.VMEM((rows, width), F32),
-                pltpu.VMEM((rows, width), BF), pltpu.VMEM((rows, width), BF),
-                pltpu.VMEM((rows, width), BF), pltpu.VMEM((rows, width), BF),
-                pltpu.VMEM((rows, width), F32),
-            ],
+            scratch_shapes=[pltpu.VMEM((rows, width), F32)],
         ),
         out_shape=[
-            array(rows, width), array(rows, steps * width), array(owners, steps * piece, width),
-            array(rows, width), array(width, rows), array(width, rows),
+            array(rows, width), array(rows, steps * width), array(owners, steps * piece, width), array(rows, width),
         ] + [array(rows, LANES)] * 6 + [array(*vectors.shape)],
         cost_estimate=pl.CostEstimate(
-            flops=6 * rows * width * width * (5 * steps + 2), bytes_accessed=60 * 10**6, transcendentals=rows * steps * width
+            flops=6 * rows * width * width * (5 * steps + 1), bytes_accessed=60 * 10**6, transcendentals=rows * steps * width
         ),
         compiler_params=pltpu.CompilerParams(vmem_limit_bytes=62 * 1024 * 1024),
         name="feed_forward",
-    )(position, *out_own, *out_in, stream, cotangent, w_out, vectors, weights, weights)
+    )(position, residual, *norm, *cot, cotangent, w_out, vectors, weights, weights)
 
 
 def fast_shards(
@@ -1508,13 +1533,16 @@
     own = project_own(places, normed, qkv_full)
     attended = [attend_forward(a, b, places, labels, labels_wide, labels_row) for a, b in zip(own, received)]
     out_in = [lax.ppermute(part[1], "sp", swap) for part in attended]
-    (block_out, grad_pre, grad_down, grad_resid, normed_two_turned, attended_turned,
-     *grads) = middle(
-        places, [part[0] for part in attended], out_in, stream, cotangent[0], out_full.reshape(width, width), vectors, weights
+    w_out_full = out_full.reshape(width, width)
+    residual, *split, normed_two_turned, attended_turned = residual_norm(
+        places, [part[0] for part in attended], out_in, stream, cotangent[0], w_out_full, vectors
+    )
+    block_out, grad_pre, grad_down, grad_resid, *grads = middle(
+        places, residual, split[:2], split[2:], cotangent[0], w_out_full, vectors, weights
     )
     grad_sent, grad_own, sums = grads[:3], grads[3:6], grads[6]
     down_part = lax.psum_scatter(
-        grad_down.reshape(hidden, width), ("fsdp", "sp"), scatter_dimension=0, tiled=True
+        grad_down.reshape(hidden, width), "fsdp", scatter_dimension=0, tiled=True
     )
     grad_in = [lax.ppermute(part, "sp", swap) for part in grad_sent]
     both = [
@@ -1529,11 +1557,9 @@
         mine, got, [both[1][1], both[2][1]], qkv_full, stream, in_full.reshape(owners, in_full.shape[3], width), vectors, sums,
     )
     vector_sums = lax.dynamic_slice(vector_sums, (0, index * piece), (4, piece))
-    down_part, _ = lax.optimization_barrier((down_part, vector_sums))
-    down_other = lax.ppermute(down_part, "sp", swap)
-    total_down = jnp.where(
-        position == 0, jnp.concatenate([down_part, down_other]), jnp.concatenate([down_other, down_part])
-    )
+    down_part, _ = lax.optimization_barrier((down_part, grad_out))
+    total_down = down_part + lax.ppermute(down_part, "sp", swap)
+    grad_patch = grad_patch * lax.optimization_barrier(jnp.float32(1.0))
     return (
         block_out[None], grad_patch[None], grad_w_in, vector_sums[0], vector_sums[1],
         grad_qkv, grad_out, vector_sums[2], vector_sums[3], grad_up, total_down,

time: 630 us -> 610 us (0.968)
  waiting for transfers between devices: 73 us -> 49.3 us
  other arithmetic: 3.63 us -> 13.6 us
  local copies, waits for them, and re-layouts: 35.2 us -> 28.3 us
    all_gather x1, waiting for transfers between devices: 32.3 us -> 5.39 us  [fast_shards(): lax.all_gather(stacked, 'fsdp', axis=0, tiled=True)]
    pallas_call x1, Pallas kernels: 233 us -> 220 us  [back_and_reduce(): pl.pallas_call(functools.partial(back_kernel, tuple(plan)), out_shape=[ar...]
    broadcast_in_dim x0 -> x1, other arithmetic: none -> 11 us  [fast_shards(): grad_patch[None]]
    ppermute x3, waiting for transfers between devices: 24.5 us -> 32 us  [fast_shards(): received = [lax.ppermute(part, 'sp', swap) for part in sent]]
    unnamed x87 -> x120, local copies, waits for them, and re-layouts: 31.7 us -> 24.7 us
  transfers between devices with their start and end apart: 13 -> 13, of which waited for: 7 -> 5; matrix products, arithmetic and copies ran while one was open for 0% -> 2% of each run, Pallas kernels for 46% -> 49%
where the time goes in v5:
time: 610 us; the launch traced here: 603 us
  Pallas kernels  484 us (79%)
  waiting for transfers between devices  49.3 us (8%)
  local copies, waits for them, and re-layouts  28.3 us (5%)
  between operations  14.8 us (2%)
  other arithmetic  13.6 us (2%)
  starting transfers between devices  12.9 us (2%)
    pallas_call x1, Pallas kernels, back_and_reduce(): pl.pallas_call(functools.partial(back_kernel, tuple(plan)), out_shape=[ar...  220 us
    pallas_call x1, Pallas kernels, gather_stream(): pl.pallas_call(gather_kernel, out_shape=[array(rows, width), array(rows,...  138 us
    pallas_call x1, Pallas kernels, middle(): pl.pallas_call(middle_kernel, grid_spec=pltpu.PrefetchScalarGridSpec(num_...  52.3 us
    pallas_call x3, Pallas kernels, attend_backward(): pl.pallas_call(backward_kernel, in_specs=[smem, smem] + [vmem] * 9, out_s...  34.4 us
    ppermute x3, waiting for transfers between devices, fast_shards(): received = [lax.ppermute(part, 'sp', swap) for part in sent]  32 us
    pallas_call x3, Pallas kernels, attend_forward(): pl.pallas_call(forward_kernel, in_specs=[smem, smem] + [vmem] * 4, out_sp...  29.1 us
    unnamed x120, local copies, waits for them, and re-layouts  24.7 us
  transfers between devices with their start and end apart: 13, of which 5 were waited for; matrix products, arithmetic and copies ran while one was open for 2% of the time, Pallas kernels for 49%

profile of v5, /device:TPU:0, one launch (start us, length us, event | category | flops | bytes accessed | tf_op | source)
XLA Modules:
  0.0 603.3 jit_solution(6607111191295896761)
XLA Ops:
  8.2 1.1 copy.26
  10.0 1.1 pad_maximum_fusion
  11.0 137.8 %gather_stream.1 = (f32[512,768]{1,0:T(8,128)}, f32[512,768]{1,0:T(8,128)}, f32[768,512]{1,0:T(8,128)}, f32[6144,512]{1,0:T(8,128)}, f32[4,2,2,384,768]{4,3,2,1,...) custom-call(f32[512,6144]{1,0:T(8,128)} %bitcast.67, ...), custom_call_target="tpu_custom_call" | custom-call | flops 14495514624 | bytes 90000000 | tf_op jit(solution)/shard_map/gather_stream/pallas_call | solution.py:1309
  149.9 1.4 collective-permute-start
  151.9 3.0 copy-done
  154.9 1.4 copy-done.1
  156.3 4.8 project_own.1
  161.1 8.7 %collective-permute-done.2.refs_1_ = f32[512,384]{1,0:T(8,128)S(1)} collective-permute-done((f32[512,384]{1,0:T(8,128)}, f32[512,384]{1,0:T(8,128)S(1)}, u32[]{:S(2)}, u32[]{:S(2)}) %collective-permute-start.2) | collective-permute-done | bytes 786464 | tf_op jit(solution)/shard_map/ppermute | solution.py:1532
  170.1 9.5 %attend_forward.5 = (f32[512,128]{1,0:T(8,128)S(1)}, f32[512,128]{1,0:T(8,128)S(1)}, f32[1024,128]{1,0:T(8,128)S(1)}) custom-call(s32[1]{0:T(128)} %bitcast.pos_ref, s32[1024]{0:T(1024)S(1)} %bitcast.38, f32[512,384]{1,0:T(8,128)S(1)} %get-tuple-element.74.refs_0_, f32[512,384]{1,0:T(8,128)S(1)} %collective-permute-done.2.refs_1_, ...), custom_call_target="tpu_custom_call" | custom-call | flops 6000000000 | bytes 1835008 | tf_op jit(solution)/shard_map/attend_forward/pallas_call | solution.py:372
  180.3 23.3 %collective-permute-done.1.refs_1_ = f32[512,384]{1,0:T(8,128)S(1)} collective-permute-done((f32[512,384]{1,0:T(8,128)}, f32[512,384]{1,0:T(8,128)S(1)}, u32[]{:S(2)}, u32[]{:S(2)}) %collective-permute-start.1) | collective-permute-done | bytes 786464 | tf_op jit(solution)/shard_map/ppermute | solution.py:1532
  203.6 9.4 %attend_forward.4 = (f32[512,128]{1,0:T(8,128)S(1)}, f32[512,128]{1,0:T(8,128)S(1)}, f32[1024,128]{1,0:T(8,128)S(1)}) custom-call(s32[1]{0:T(128)} %bitcast.pos_ref, s32[1024]{0:T(1024)S(1)} %bitcast.40, f32[512,384]{1,0:T(8,128)S(1)} %get-tuple-element.71.refs_0_, f32[512,384]{1,0:T(8,128)S(1)} %collective-permute-done.1.refs_1_, ...), custom_call_target="tpu_custom_call" | custom-call | flops 6000000000 | bytes 1835008 | tf_op jit(solution)/shard_map/attend_forward/pallas_call | solution.py:372
  214.6 10.2 %attend_forward.3 = (f32[512,128]{1,0:T(8,128)S(1)}, f32[512,128]{1,0:T(8,128)S(1)}, f32[1024,128]{1,0:T(8,128)S(1)}) custom-call(s32[1]{0:T(128)} %bitcast.pos_ref, s32[1024]{0:T(1024)S(1)} %bitcast.42, f32[512,384]{1,0:T(8,128)S(1)} %get-tuple-element.68.refs_0_, f32[512,384]{1,0:T(8,128)} %collective-permute-done.refs_1_, ...), custom_call_target="tpu_custom_call" | custom-call | flops 6000000000 | bytes 1835008 | tf_op jit(solution)/shard_map/attend_forward/pallas_call | solution.py:372
  225.6 1.4 collective-permute-start.3
  227.7 6.0 collective-permute-done.3.refs_3_
  233.7 5.5 residual_norm.1
  239.9 1.2 copy-done.12
  241.1 1.2 copy-done.13
  242.3 1.2 copy-done.14
  247.1 5.4 all-gather.2.cloned.1.call-done
  252.4 52.3 %feed_forward.1 = (f32[512,768]{1,0:T(8,128)}, f32[512,3072]{1,0:T(8,128)}, f32[16,192,768]{2,1,0:T(8,128)}, f32[512,768]{1,0:T(8,128)}, f32[512,128]{1,0:T(8,12...) custom-call(s32[1]{0:T(128)} %bitcast.pos_ref, ...), custom_call_target="tpu_custom_call" | custom-call | flops 38050725888 | bytes 60000000 | tf_op jit(solution)/shard_map/feed_forward/pallas_call | solution.py:1477
  304.9 1.6 collective-permute-start.6
  307.2 1.3 collective-permute-start.8
  308.5 5.8 collective-permute-done.6.refs_5_
  314.3 1.1 copy-done.40
  315.4 12.0 %attend_backward.3 = (f32[512,384]{1,0:T(8,128)S(1)}, f32[512,384]{1,0:T(8,128)S(1)}) custom-call(s32[1]{0:T(128)} %bitcast.pos_ref, s32[1024]{0:T(1024)S(1)} %bitcast.44, f32[512,384]{1,0:T(8,128)S(1)} %copy-done.24, f32[512,384]{1,0:T(8,128)} %collective-permute-done.refs_1_, f32[512,128]{1,0:T(8,128)S(1)} %copy-done.9, f32[512,128]{1,0:T(8,128)S(1)} %copy-done.34, ...), custom_call_target="tpu_custom_call" | custom-call | flops 12999999488 | bytes 3932160 | tf_op jit(solution)/shard_map/attend_backward/pallas_call | solution.py:479
  328.3 1.5 collective-permute-start.9
  330.0 11.2 %attend_backward.4 = (f32[512,384]{1,0:T(8,128)S(1)}, f32[512,384]{1,0:T(8,128)S(1)}) custom-call(s32[1]{0:T(128)} %bitcast.pos_ref, s32[1024]{0:T(1024)S(1)} %bitcast.46, f32[512,384]{1,0:T(8,128)S(1)} %copy-done.22, f32[512,384]{1,0:T(8,128)S(1)} %copy-done.20, f32[512,128]{1,0:T(8,128)S(1)} %copy-done.7, f32[512,128]{1,0:T(8,128)S(1)} %copy-done.32, ...), custom_call_target="tpu_custom_call" | custom-call | flops 12999999488 | bytes 3932160 | tf_op jit(solution)/shard_map/attend_backward/pallas_call | solution.py:479
  343.1 11.2 %attend_backward.5 = (f32[512,384]{1,0:T(8,128)S(1)}, f32[512,384]{1,0:T(8,128)S(1)}) custom-call(s32[1]{0:T(128)} %bitcast.pos_ref, s32[1024]{0:T(1024)S(1)} %bitcast.48, f32[512,384]{1,0:T(8,128)S(1)} %copy-done.18, f32[512,384]{1,0:T(8,128)S(1)} %copy-done.16, f32[512,128]{1,0:T(8,128)S(1)} %get-tuple-element.76.refs_2_, f32[512,128]{1,0:T(8,128)S(1)} %copy-done.30, ...), custom_call_target="tpu_custom_call" | custom-call | flops 12999999488 | bytes 3932160 | tf_op jit(solution)/shard_map/attend_backward/pallas_call | solution.py:479
  357.0 220.4 %back_and_reduce.1 = (f32[48,3072]{1,0:T(8,128)}, f32[48,768]{1,0:T(8,128)}, f32[48,2304]{1,0:T(8,128)}, f32[384,768]{1,0:T(8,128)}, f32[512,6144]{1,0:T(8,128)}...) custom-call(f32[8,2,48,512]{3,2,1,0:T(8,128)} %bitcast.50, f32[8,2,48,512]{3,2,1,0:T(8,128)} %bitcast.51, ...), custom_call_target="tpu_custom_call" | custom-call | flops 43486543872 | bytes 130000000 | tf_op jit(solution)/shard_map/back_and_reduce/pallas_call | solution.py:961
  577.4 2.0 collective-permute-start.10
  579.4 11.0 %multiply_bitcast_fusion = f32[1,512,6144]{2,1,0:T(8,128)} fusion(f32[512,6144]{1,0:T(8,128)} %get-tuple-element.113, f32[]{:T(128)} %constant.24.clone.1), kind=kLoop, calls=%fused_computation | loop fusion | flops 3145728 | bytes 25165828 | tf_op jit(solution)/shard_map/broadcast_in_dim | solution.py:1564
  592.7 1.0 copy.31
  (139 shorter events, 22.5 us)
Async XLA Ops:
  7.2 245.3 %all-gather.2.cloned.1.call-start = ((), (), s32[]{:S(2)}) async-start(), calls=%async_computation.1 | async-start | bytes 20054016 | tf_op jit(solution)/shard_map/all_gather | solution.py:1531
  148.9 428.5 %reduce-scatter.2.cloned.1.call-start = ((), (), s32[]{:S(2)}) async-start(), calls=%async_computation.2 | async-start | bytes 10027008 | tf_op jit(solution)/shard_map/reduce_scatter | solution.py:1544
  149.2 20.7 %collective-permute-start.2 = (f32[512,384]{1,0:T(8,128)}, f32[512,384]{1,0:T(8,128)S(1)}, u32[]{:S(2)}, u32[]{:S(2)}) collective-permute-start(f32[512,384]{1,0:T(8,128)} %get-tuple-element.75), channel_id=1, source_target_pairs={{0,1},{1,0},{2,3},{3,2},{4,5},{5,4},{6,7},{7,6},{8,9},{9,8},{10,11... | collective-permute-start | bytes 2359304 | tf_op jit(solution)/shard_map/ppermute | solution.py:1532
  149.9 64.6 %collective-permute-start = (f32[512,384]{1,0:T(8,128)}, f32[512,384]{1,0:T(8,128)}, u32[]{:S(2)}, u32[]{:S(2)}) collective-permute-start(f32[512,384]{1,0:T(8,128)} %get-tuple-element.69), channel_id=1, source_target_pairs={{0,1},{1,0},{2,3},{3,2},{4,5},{5,4},{6,7},{7,6},{8,9},{9,8},{10,11... | collective-permute-start | bytes 2359304 | tf_op jit(solution)/shard_map/ppermute | solution.py:1532
  151.3 52.3 %collective-permute-start.1 = (f32[512,384]{1,0:T(8,128)}, f32[512,384]{1,0:T(8,128)S(1)}, u32[]{:S(2)}, u32[]{:S(2)}) collective-permute-start(f32[512,384]{1,0:T(8,128)} %get-tuple-element.72), channel_id=1, source_target_pairs={{0,1},{1,0},{2,3},{3,2},{4,5},{5,4},{6,7},{7,6},{8,9},{9,8},{10,11... | collective-permute-start | bytes 2359304 | tf_op jit(solution)/shard_map/ppermute | solution.py:1532
  156.3 13.5 %copy-start.11 = (s32[1,1024]{1,0:T(1,128)S(1)}, s32[1,1024]{1,0:T(1,128)}, u32[]{:S(2)}) copy-start(s32[1,1024]{1,0:T(1,128)} %param.13) | copy-start | bytes 12292
  161.1 18.4 %copy-start.17 = (f32[512,384]{1,0:T(8,128)}, f32[512,384]{1,0:T(8,128)S(1)}, u32[]{:S(2)}) copy-start(f32[512,384]{1,0:T(8,128)S(1)} %get-tuple-element.74.refs_0_) | copy-start | bytes 2359300
  161.1 42.5 %copy-start.21 = (f32[512,384]{1,0:T(8,128)}, f32[512,384]{1,0:T(8,128)S(1)}, u32[]{:S(2)}) copy-start(f32[512,384]{1,0:T(8,128)S(1)} %get-tuple-element.71.refs_0_) | copy-start | bytes 2359300
  161.1 53.4 %copy-start.23 = (f32[512,384]{1,0:T(8,128)}, f32[512,384]{1,0:T(8,128)S(1)}, u32[]{:S(2)}) copy-start(f32[512,384]{1,0:T(8,128)S(1)} %get-tuple-element.68.refs_0_) | copy-start | bytes 2359300
  170.1 44.5 %copy-start.4 = (s32[1024,128]{1,0:T(8,128)}, s32[1024,128]{1,0:T(8,128)S(1)}, u32[]{:S(2)}) copy-start(s32[1024,128]{1,0:T(8,128)S(1)} %broadcast_in_dim.30.refs_2_.refs_7_) | copy-start | bytes 1572868
  179.6 33.5 %copy-start.29 = (f32[512,128]{1,0:T(8,128)}, f32[512,128]{1,0:T(8,128)S(1)}, u32[]{:S(2)}) copy-start(f32[512,128]{1,0:T(8,128)S(1)} %get-tuple-element.79.refs_3_) | copy-start | bytes 786436
  179.6 33.5 %copy-start.35 = (f32[1024,128]{1,0:T(8,128)}, f32[1024,128]{1,0:T(8,128)S(1)}, u32[]{:S(2)}) copy-start(f32[1024,128]{1,0:T(8,128)S(1)} %get-tuple-element.106.refs_6_) | copy-start | bytes 1572868
  179.6 48.1 %collective-permute-start.5 = (f32[512,128]{1,0:T(8,128)S(1)}, f32[512,128]{1,0:T(8,128)S(1)}, u32[]{:S(2)}, u32[]{:S(2)}) collective-permute-start(f32[512,128]{1,0:T(8,128)S(1)} %get-tuple-element.79.refs_3_), channel_id=1, source_target_pairs={{0,1},{1,0},{2,3},{3,2},{4,5},{5,4},{6,7},{7,6},{8,9},{9,8},{10,11... | collective-permute-start | bytes 786440 | tf_op jit(solution)/shard_map/ppermute | solution.py:1535
  213.9 19.8 %copy-start.6 = (f32[512,128]{1,0:T(8,128)}, f32[512,128]{1,0:T(8,128)S(1)}, u32[]{:S(2)}) copy-start(f32[512,128]{1,0:T(8,128)S(1)} %get-tuple-element.73.refs_1_.refs_2_) | copy-start | bytes 786436
  213.9 13.8 %collective-permute-start.4 = (f32[512,128]{1,0:T(8,128)S(1)}, f32[512,128]{1,0:T(8,128)S(1)}, u32[]{:S(2)}, u32[]{:S(2)}) collective-permute-start(f32[512,128]{1,0:T(8,128)S(1)} %get-tuple-element.78.refs_3_), channel_id=1, source_target_pairs={{0,1},{1,0},{2,3},{3,2},{4,5},{5,4},{6,7},{7,6},{8,9},{9,8},{10,11... | collective-permute-start | bytes 786440 | tf_op jit(solution)/shard_map/ppermute | solution.py:1535
  214.5 19.2 %copy-start.2 = (f32[1,512,768]{2,1,0:T(8,128)S(1)}, f32[1,512,768]{2,1,0:T(8,128)}, u32[]{:S(2)}) copy-start(f32[1,512,768]{2,1,0:T(8,128)} %param.23) | copy-start | bytes 4718596
  214.5 19.2 %copy-start.3 = (f32[512,768]{1,0:T(8,128)S(1)}, f32[512,768]{1,0:T(8,128)}, u32[]{:S(2)}) copy-start(f32[512,768]{1,0:T(8,128)} %get-tuple-element.80.refs_6_.refs_13_) | copy-start | bytes 4718596
  214.6 19.2 %copy-start.10 = (f32[8,768]{1,0:T(8,128)S(1)}, f32[8,768]{1,0:T(8,128)}, u32[]{:S(2)}) copy-start(f32[8,768]{1,0:T(8,128)} %get-tuple-element.82.refs_9_.refs_7_.refs_15_) | copy-start | bytes 73732
  225.6 8.1 %collective-permute-start.3 = (f32[512,128]{1,0:T(8,128)S(1)}, f32[512,128]{1,0:T(8,128)S(1)}, u32[]{:S(2)}, u32[]{:S(2)}) collective-permute-start(f32[512,128]{1,0:T(8,128)S(1)} %get-tuple-element.77.refs_3_), channel_id=1, source_target_pairs={{0,1},{1,0},{2,3},{3,2},{4,5},{5,4},{6,7},{7,6},{8,9},{9,8},{10,11... | collective-permute-start | bytes 786440 | tf_op jit(solution)/shard_map/ppermute | solution.py:1535
  304.9 9.4 %collective-permute-start.6 = (f32[512,128]{1,0:T(8,128)}, f32[512,128]{1,0:T(8,128)S(1)}, u32[]{:S(2)}, u32[]{:S(2)}) collective-permute-start(f32[512,128]{1,0:T(8,128)} %get-tuple-element.97), channel_id=1, source_target_pairs={{0,1},{1,0},{2,3},{3,2},{4,5},{5,4},{6,7},{7,6},{8,9},{9,8},{10,11... | collective-permute-start | bytes 786440 | tf_op jit(solution)/shard_map/ppermute | solution.py:1547
  306.4 23.4 %collective-permute-start.7 = (f32[512,128]{1,0:T(8,128)S(1)}, f32[512,128]{1,0:T(8,128)S(1)}, u32[]{:S(2)}, u32[]{:S(2)}) collective-permute-start(f32[512,128]{1,0:T(8,128)S(1)} %copy-done.57), channel_id=1, source_target_pairs={{0,1},{1,0},{2,3},{3,2},{4,5},{5,4},{6,7},{7,6},{8,9},{9,8},{10,11... | collective-permute-start | bytes 786440 | tf_op jit(solution)/shard_map/ppermute | solution.py:1547
  307.2 35.8 %collective-permute-start.8 = (f32[512,128]{1,0:T(8,128)S(1)}, f32[512,128]{1,0:T(8,128)S(1)}, u32[]{:S(2)}, u32[]{:S(2)}) collective-permute-start(f32[512,128]{1,0:T(8,128)S(1)} %copy-done.56), channel_id=1, source_target_pairs={{0,1},{1,0},{2,3},{3,2},{4,5},{5,4},{6,7},{7,6},{8,9},{9,8},{10,11... | collective-permute-start | bytes 786440 | tf_op jit(solution)/shard_map/ppermute | solution.py:1547
  315.4 14.5 %copy-start.7 = (f32[512,128]{1,0:T(8,128)S(1)}, f32[512,128]{1,0:T(8,128)}, u32[]{:S(2)}) copy-start(f32[512,128]{1,0:T(8,128)} %copy-done.6) | copy-start | bytes 786436
  315.4 14.5 %copy-start.20 = (f32[512,384]{1,0:T(8,128)S(1)}, f32[512,384]{1,0:T(8,128)}, u32[]{:S(2)}) copy-start(f32[512,384]{1,0:T(8,128)} %copy-done.19) | copy-start | bytes 2359300
  315.4 14.5 %copy-start.22 = (f32[512,384]{1,0:T(8,128)S(1)}, f32[512,384]{1,0:T(8,128)}, u32[]{:S(2)}) copy-start(f32[512,384]{1,0:T(8,128)} %copy-done.21) | copy-start | bytes 2359300
  315.4 14.5 %copy-start.32 = (f32[512,128]{1,0:T(8,128)S(1)}, f32[512,128]{1,0:T(8,128)}, u32[]{:S(2)}) copy-start(f32[512,128]{1,0:T(8,128)} %copy-done.31) | copy-start | bytes 786436
  315.4 14.5 %copy-start.38 = (f32[1024,128]{1,0:T(8,128)S(1)}, f32[1024,128]{1,0:T(8,128)}, u32[]{:S(2)}) copy-start(f32[1024,128]{1,0:T(8,128)} %copy-done.37) | copy-start | bytes 1572868
  315.4 14.5 %copy-start.47 = (f32[512,128]{1,0:T(8,128)S(1)}, f32[512,128]{1,0:T(8,128)}, u32[]{:S(2)}) copy-start(f32[512,128]{1,0:T(8,128)} %get-tuple-element.100.refs_4_) | copy-start | bytes 786436
  328.3 27.8 %collective-permute-start.9 = (f32[512,384]{1,0:T(8,128)S(1)}, f32[512,384]{1,0:T(8,128)S(1)}, u32[]{:S(2)}, u32[]{:S(2)}) collective-permute-start(f32[512,384]{1,0:T(8,128)S(1)} %get-tuple-element.108), channel_id=1, source_target_pairs={{0,1},{1,0},{2,3},{3,2},{4,5},{5,4},{6,7},{7,6},{8,9},{9,8},{10,11... | collective-permute-start | bytes 2359304 | tf_op jit(solution)/shard_map/ppermute | solution.py:1554
  329.9 13.1 %copy-start.16 = (f32[512,384]{1,0:T(8,128)S(1)}, f32[512,384]{1,0:T(8,128)}, u32[]{:S(2)}) copy-start(f32[512,384]{1,0:T(8,128)} %copy-done.15) | copy-start | bytes 2359300
  329.9 13.1 %copy-start.18 = (f32[512,384]{1,0:T(8,128)S(1)}, f32[512,384]{1,0:T(8,128)}, u32[]{:S(2)}) copy-start(f32[512,384]{1,0:T(8,128)} %copy-done.17) | copy-start | bytes 2359300
  577.4 14.4 %collective-permute-start.10 = (f32[192,768]{1,0:T(8,128)}, f32[192,768]{1,0:T(8,128)S(1)}, u32[]{:S(2)}, u32[]{:S(2)}) collective-permute-start(f32[192,768]{1,0:T(8,128)} %reduce-scatter.2.cloned.1.call-done), channel_id=1, source_target_pairs={{0,1},{1,0},{2,3},{3,2},{4,5},{5,4},{6,7},{7,6},{8,9},{9,8},{10,11... | collective-permute-start | bytes 1769480 | tf_op jit(solution)/shard_map/ppermute | solution.py:1561
  (39 other events, 165.4 us)
Sparse Core Ops, SparseCore 0:
  149.0 103.3 all-gather.1
  305.0 147.4 reduce-scatter.1

commit v6 on v5

--- a/solution.py
+++ b/solution.py
@@ -368,11 +368,12 @@
     rows = own.shape[0]
     length = 2 * rows
     smem = pl.BlockSpec(memory_space=pltpu.SMEM)
-    vmem = pl.BlockSpec(memory_space=pltpu.VMEM)
+    whole = lambda *shape: pl.BlockSpec(shape, lambda i: (0,) * len(shape))
     return pl.pallas_call(
         forward_kernel,
-        in_specs=[smem, smem] + [vmem] * 4,
-        out_specs=[vmem] * 3,
+        grid=(1,),
+        in_specs=[smem, smem, whole(rows, 3 * LANES), whole(rows, 3 * LANES), whole(length, LANES), whole(length // BLOCK, 1, BLOCK)],
+        out_specs=[whole(rows, LANES), whole(rows, LANES), whole(length, LANES)],
         scratch_shapes=[
             pltpu.VMEM((2, length, 2 * LANES), BF),
             pltpu.VMEM((2, length, 2 * LANES), BF),
@@ -475,11 +476,13 @@
     rows = own.shape[0]
     length = 2 * rows
     smem = pl.BlockSpec(memory_space=pltpu.SMEM)
-    vmem = pl.BlockSpec(memory_space=pltpu.VMEM)
+    whole = lambda *shape: pl.BlockSpec(shape, lambda i: (0,) * len(shape))
     return pl.pallas_call(
         backward_kernel,
-        in_specs=[smem, smem] + [vmem] * 9,
-        out_specs=[vmem] * 2,
+        grid=(1,),
+        in_specs=[smem, smem, whole(rows, 3 * LANES), whole(rows, 3 * LANES)] + [whole(rows, LANES)] * 4
+        + [whole(length, LANES), whole(length, LANES), whole(length // BLOCK, 1, BLOCK)],
+        out_specs=[whole(rows, 3 * LANES)] * 2,
         scratch_shapes=[
             pltpu.VMEM((2, length, 2 * LANES), BF),
             pltpu.VMEM((2, length, 2 * LANES), BF),
@@ -492,7 +495,7 @@
             pltpu.VMEM((length, LANES), F32),
             pltpu.VMEM((length, LANES), F32),
         ],
-        out_shape=[jax.ShapeDtypeStruct((rows, 3 * LANES), F32)] * 2,
+        out_shape=[pltpu.HBM((rows, 3 * LANES), F32)] * 2,
         cost_estimate=pl.CostEstimate(flops=13 * 10**9, bytes_accessed=60 * rows * LANES, transcendentals=length * length),
         compiler_params=pltpu.CompilerParams(vmem_limit_bytes=40 * 1024 * 1024),
         name="attend_backward",
@@ -1026,7 +1029,7 @@
 def gather_kernel(patch_ref, in_ref, qkv_ref, out_ref, vector_ref,
                   stream_ref, normed_ref, turned_ref, patch_turned_ref, in_full, qkv_full, out_full, vectors_ref,
                   sent_0, sent_1, sent_2,
-                  patch_buf, in_buf, qkv_buf, out_buf, turn_buf, acc, v_c, v_x, v_z, sent_buf,
+                  patch_buf, in_buf, qkv_buf, out_buf, turn_buf, acc, v_own, v_c, v_x, v_z, sent_buf,
                   z_sem, x_sem, y_sem, c_sem, v_sem, own_sem, patch_sem, turn_sem, full_sem, last_sem):
     fsdp = lax.axis_index("fsdp")
     row = lax.axis_index("sp")
@@ -1186,6 +1189,8 @@
             turn_buf[slot] = jnp.transpose(patch_buf[:, span((group * each + slot) * LANES, LANES)])
             turn_copy(group * each + slot, slot).start()
 
+    wide = jnp.concatenate([vector_ref[...], jnp.zeros((8, width - LANES), F32)], axis=1)
+    v_own[...] = pltpu.roll(wide, fsdp * out_ref.shape[0], 1)
     pl.semaphore_wait(barrier, 6)
     z_stage(jnp.int32(0))
     z_stage(jnp.int32(1))
@@ -1193,7 +1198,7 @@
         copy.start()
     patch_copy.start()
     v_copies = [
-        remote(vector_ref, v_c, v_sem, (0,), sibling),
+        remote(v_own, v_c, v_sem, (0,), sibling),
         remote(v_c, v_x, v_sem, (1,), beside),
     ] + [remote(v_x, v_z.at[step], v_sem, (2 + step,), along[step]) for step in range(3)]
     v_copies[0].start()
@@ -1216,7 +1221,7 @@
         def _():
             patch_copy.wait()
             v_copies[0].wait_recv()
-            v_c[...] = v_c[...] + vector_ref[...]
+            v_c[...] = v_c[...] + v_own[...]
             v_copies[1].start()
 
         @pl.when(t == 1)
@@ -1311,7 +1316,7 @@
         out_shape=[
             array(rows, width), array(rows, width), array(width, rows), array(patch_width, rows),
             array(*owners, block, width), array(*owners, piece, columns), array(*owners, piece, width),
-            array(*vectors.shape), array(rows, group), array(rows, group), array(rows, group),
+            array(8, width), array(rows, group), array(rows, group), array(rows, group),
         ],
         in_specs=[any_space] * 4 + [vmem],
         out_specs=[vmem, vmem, vmem] + [any_space] * 4 + [vmem] + [any_space] * 3,
@@ -1322,9 +1327,10 @@
             pltpu.VMEM(owners + (piece, width), F32),
             pltpu.VMEM((4, LANES, rows), F32),
             pltpu.VMEM((rows, width), F32),
-            pltpu.VMEM(vectors.shape, F32),
-            pltpu.VMEM(vectors.shape, F32),
-            pltpu.VMEM((3,) + vectors.shape, F32),
+            pltpu.VMEM((8, width), F32),
+            pltpu.VMEM((8, width), F32),
+            pltpu.VMEM((8, width), F32),
+            pltpu.VMEM((3, 8, width), F32),
             pltpu.VMEM((3, rows, group), F32),
             dma((2, units, 3)), dma((2, units)), dma((2, units)), dma((2, units, 2)), dma((2, 5)),
             dma((block // CUT_ROWS + 2,)), dma, dma((4,)), dma((units,)), dma((3,)),
@@ -1520,8 +1526,9 @@
     blocks = hidden // width
     swap = [(0, 1), (1, 0)]
 
-    vectors_own = jnp.tile(jnp.stack([norm1_gain, norm1_bias, norm2_gain, norm2_bias] + [norm1_gain] * 4), (1, owners))
-    vectors_own = jnp.where(jnp.arange(width)[None, :] // piece == index, vectors_own, 0.0)
+    vectors_own = jnp.pad(
+        jnp.stack([norm1_gain, norm1_bias, norm2_gain, norm2_bias]), ((0, 4), (0, LANES - piece))
+    )
     (stream, normed, normed_turned, patches_turned, in_full, qkv_full, out_full, vectors, *sent) = gather_stream(
         patches[0], w_in, w_qkv, w_out, vectors_own
     )

time: 610 us -> 608 us (level)
  local copies, waits for them, and re-layouts: 28.3 us -> 22.1 us
    pallas_call x6, Pallas kernels: 63.6 us -> 55.7 us  [the longest x3 31.8 us: attend_backward(): pl.pallas_call(backward_kernel, grid=(1,), in_specs=[smem, smem, whole(ro...]
    pallas_call x1, Pallas kernels: 220 us -> 227 us  [back_and_reduce(): pl.pallas_call(functools.partial(back_kernel, tuple(plan)), out_shape=[ar...]
    unnamed x120 -> x116, local copies, waits for them, and re-layouts: 24.7 us -> 19.4 us
where the time goes in v6:
time: 608 us; the launch traced here: 600 us
  Pallas kernels  483 us (79%)
  waiting for transfers between devices  54.7 us (9%)
  local copies, waits for them, and re-layouts  22.1 us (4%)
  between operations  14.8 us (2%)
  other arithmetic  13.6 us (2%)
  starting transfers between devices  11.5 us (2%)
    pallas_call x1, Pallas kernels, back_and_reduce(): pl.pallas_call(functools.partial(back_kernel, tuple(plan)), out_shape=[ar...  227 us
    pallas_call x1, Pallas kernels, gather_stream(): pl.pallas_call(gather_kernel, out_shape=[array(rows, width), array(rows,...  138 us
    pallas_call x1, Pallas kernels, middle(): pl.pallas_call(middle_kernel, grid_spec=pltpu.PrefetchScalarGridSpec(num_...  52.3 us
    ppermute x3, waiting for transfers between devices, fast_shards(): received = [lax.ppermute(part, 'sp', swap) for part in sent]  33.7 us
    pallas_call x3, Pallas kernels, attend_backward(): pl.pallas_call(backward_kernel, grid=(1,), in_specs=[smem, smem, whole(ro...  31.8 us
    pallas_call x3, Pallas kernels, attend_forward(): pl.pallas_call(forward_kernel, grid=(1,), in_specs=[smem, smem, whole(row...  23.8 us
    unnamed x116, local copies, waits for them, and re-layouts  19.4 us
  transfers between devices with their start and end apart: 13, of which 5 were waited for; matrix products, arithmetic and copies ran while one was open for 2% of the time, Pallas kernels for 49%

profile of v6, /device:TPU:0, one launch (start us, length us, event | category | flops | bytes accessed | tf_op | source)
XLA Modules:
  0.0 599.7 jit_solution(17502456754376104753)
XLA Ops:
  7.3 1.2 copy.26
  8.4 1.1 pad_maximum_fusion
  10.2 137.7 %gather_stream.1 = (f32[512,768]{1,0:T(8,128)}, f32[512,768]{1,0:T(8,128)}, f32[768,512]{1,0:T(8,128)}, f32[6144,512]{1,0:T(8,128)}, f32[4,2,2,384,768]{4,3,2,1,...) custom-call(f32[512,6144]{1,0:T(8,128)} %bitcast.63, ...), custom_call_target="tpu_custom_call" | custom-call | flops 14495514624 | bytes 90000000 | tf_op jit(solution)/shard_map/gather_stream/pallas_call | solution.py:1314
  148.9 1.4 collective-permute-start
  150.9 3.0 copy-done
  153.9 1.4 copy-done.1
  155.3 4.8 project_own.1
  160.1 8.7 %collective-permute-done.2.refs_1_ = f32[512,384]{1,0:T(8,128)S(1)} collective-permute-done((f32[512,384]{1,0:T(8,128)}, f32[512,384]{1,0:T(8,128)S(1)}, u32[]{:S(2)}, u32[]{:S(2)}) %collective-permute-start.2) | collective-permute-done | bytes 786464 | tf_op jit(solution)/shard_map/ppermute | solution.py:1539
  169.0 7.7 %attend_forward.5 = (f32[512,128]{1,0:T(8,128)S(1)}, f32[512,128]{1,0:T(8,128)S(1)}, f32[1024,128]{1,0:T(8,128)S(1)}) custom-call(s32[1]{0:T(128)} %bitcast.pos_ref, s32[1024]{0:T(1024)S(1)} %bitcast.38, f32[512,384]{1,0:T(8,128)S(1)} %get-tuple-element.74.refs_0_, f32[512,384]{1,0:T(8,128)S(1)} %collective-permute-done.2.refs_1_, ...), custom_call_target="tpu_custom_call" | custom-call | flops 6000000000 | bytes 1835008 | tf_op jit(solution)/shard_map/attend_forward/pallas_call | solution.py:372
  177.4 25.1 %collective-permute-done.1.refs_1_ = f32[512,384]{1,0:T(8,128)S(1)} collective-permute-done((f32[512,384]{1,0:T(8,128)}, f32[512,384]{1,0:T(8,128)S(1)}, u32[]{:S(2)}, u32[]{:S(2)}) %collective-permute-start.1) | collective-permute-done | bytes 786464 | tf_op jit(solution)/shard_map/ppermute | solution.py:1539
  202.5 7.7 %attend_forward.4 = (f32[512,128]{1,0:T(8,128)S(1)}, f32[512,128]{1,0:T(8,128)S(1)}, f32[1024,128]{1,0:T(8,128)S(1)}) custom-call(s32[1]{0:T(128)} %bitcast.pos_ref, s32[1024]{0:T(1024)S(1)} %bitcast.40, f32[512,384]{1,0:T(8,128)S(1)} %get-tuple-element.71.refs_0_, f32[512,384]{1,0:T(8,128)S(1)} %collective-permute-done.1.refs_1_, ...), custom_call_target="tpu_custom_call" | custom-call | flops 6000000000 | bytes 1835008 | tf_op jit(solution)/shard_map/attend_forward/pallas_call | solution.py:372
  211.7 8.4 %attend_forward.3 = (f32[512,128]{1,0:T(8,128)S(1)}, f32[512,128]{1,0:T(8,128)S(1)}, f32[1024,128]{1,0:T(8,128)S(1)}) custom-call(s32[1]{0:T(128)} %bitcast.pos_ref, s32[1024]{0:T(1024)S(1)} %bitcast.42, f32[512,384]{1,0:T(8,128)S(1)} %get-tuple-element.68.refs_0_, f32[512,384]{1,0:T(8,128)} %collective-permute-done.refs_1_, ...), custom_call_target="tpu_custom_call" | custom-call | flops 6000000000 | bytes 1835008 | tf_op jit(solution)/shard_map/attend_forward/pallas_call | solution.py:372
  221.0 1.4 collective-permute-start.3
  223.1 6.2 %collective-permute-done.3.refs_3_ = f32[512,128]{1,0:T(8,128)S(1)} collective-permute-done((f32[512,128]{1,0:T(8,128)S(1)}, f32[512,128]{1,0:T(8,128)S(1)}, u32[]{:S(2)}, u32[]{:S(2)}) %collective-permute-start.3) | collective-permute-done | bytes 262176 | tf_op jit(solution)/shard_map/ppermute | solution.py:1542
  229.4 5.5 residual_norm.1
  235.6 1.2 copy-done.12
  236.7 1.2 copy-done.13
  237.9 1.2 copy-done.14
  240.9 0.9 copy-done.27
  242.8 8.8 %all-gather.2.cloned.1.call-done = f32[6144,768]{1,0:T(8,128)} async-done(((f32[384,768]{1,0:T(8,128)}), f32[6144,768]{1,0:T(8,128)}) %all-gather.2.cloned.1.call-update) | async-done | bytes 18874384 | tf_op jit(solution)/shard_map/all_gather | solution.py:1538
  251.5 52.3 %feed_forward.1 = (f32[512,768]{1,0:T(8,128)}, f32[512,3072]{1,0:T(8,128)}, f32[16,192,768]{2,1,0:T(8,128)}, f32[512,768]{1,0:T(8,128)}, f32[512,128]{1,0:T(8,12...) custom-call(s32[1]{0:T(128)} %bitcast.pos_ref, ...), custom_call_target="tpu_custom_call" | custom-call | flops 38050725888 | bytes 60000000 | tf_op jit(solution)/shard_map/feed_forward/pallas_call | solution.py:1483
  303.9 1.5 collective-permute-start.6
  306.3 1.2 collective-permute-start.8
  307.5 5.8 collective-permute-done.6.refs_5_
  313.4 1.1 copy-done.40
  314.5 11.1 %attend_backward.3 = (f32[512,384]{1,0:T(8,128)}, f32[512,384]{1,0:T(8,128)}) custom-call(s32[1]{0:T(128)} %bitcast.pos_ref, s32[1024]{0:T(1024)S(1)} %bitcast.44, f32[512,384]{1,0:T(8,128)S(1)} %copy-done.24, f32[512,384]{1,0:T(8,128)} %collective-permute-done.refs_1_, f32[512,128]{1,0:T(8,128)S(1)} %copy-done.9, f32[512,128]{1,0:T(8,128)S(1)} %copy-done.34, ...), custom_call_target="tpu_custom_call" | custom-call | flops 12999999488 | bytes 3932160 | tf_op jit(solution)/shard_map/attend_backward/pallas_call | solution.py:480
  325.6 1.5 collective-permute-start.9
  327.2 10.3 %attend_backward.4 = (f32[512,384]{1,0:T(8,128)}, f32[512,384]{1,0:T(8,128)}) custom-call(s32[1]{0:T(128)} %bitcast.pos_ref, s32[1024]{0:T(1024)S(1)} %bitcast.46, f32[512,384]{1,0:T(8,128)S(1)} %copy-done.22, f32[512,384]{1,0:T(8,128)S(1)} %copy-done.20, f32[512,128]{1,0:T(8,128)S(1)} %copy-done.7, f32[512,128]{1,0:T(8,128)S(1)} %copy-done.32, ...), custom_call_target="tpu_custom_call" | custom-call | flops 12999999488 | bytes 3932160 | tf_op jit(solution)/shard_map/attend_backward/pallas_call | solution.py:480
  337.6 10.4 %attend_backward.5 = (f32[512,384]{1,0:T(8,128)}, f32[512,384]{1,0:T(8,128)}) custom-call(s32[1]{0:T(128)} %bitcast.pos_ref, s32[1024]{0:T(1024)S(1)} %bitcast.48, f32[512,384]{1,0:T(8,128)S(1)} %copy-done.18, f32[512,384]{1,0:T(8,128)S(1)} %copy-done.16, f32[512,128]{1,0:T(8,128)S(1)} %get-tuple-element.76.refs_2_, f32[512,128]{1,0:T(8,128)S(1)} %copy-done.30, ...), custom_call_target="tpu_custom_call" | custom-call | flops 12999999488 | bytes 3932160 | tf_op jit(solution)/shard_map/attend_backward/pallas_call | solution.py:480
  348.0 227.0 %back_and_reduce.1 = (f32[48,3072]{1,0:T(8,128)}, f32[48,768]{1,0:T(8,128)}, f32[48,2304]{1,0:T(8,128)}, f32[384,768]{1,0:T(8,128)}, f32[512,6144]{1,0:T(8,128)}...) custom-call(f32[8,2,48,512]{3,2,1,0:T(8,128)} %bitcast.50, f32[8,2,48,512]{3,2,1,0:T(8,128)} %bitcast.51, ...), custom_call_target="tpu_custom_call" | custom-call | flops 43486543872 | bytes 130000000 | tf_op jit(solution)/shard_map/back_and_reduce/pallas_call | solution.py:964
  575.8 11.0 %multiply_bitcast_fusion = f32[1,512,6144]{2,1,0:T(8,128)} fusion(f32[512,6144]{1,0:T(8,128)} %get-tuple-element.113, f32[]{:T(128)} %constant.6.clone.1), kind=kLoop, calls=%fused_computation | loop fusion | flops 3145728 | bytes 25165828 | tf_op jit(solution)/shard_map/broadcast_in_dim | solution.py:1571
  589.1 1.0 copy.31
  (131 shorter events, 15.9 us)
Async XLA Ops:
  7.2 244.3 %all-gather.2.cloned.1.call-start = ((), (), s32[]{:S(2)}) async-start(), calls=%async_computation.1 | async-start | bytes 20054016 | tf_op jit(solution)/shard_map/all_gather | solution.py:1538
  147.9 427.2 %reduce-scatter.2.cloned.1.call-start = ((), (), s32[]{:S(2)}) async-start(), calls=%async_computation.2 | async-start | bytes 10027008 | tf_op jit(solution)/shard_map/reduce_scatter | solution.py:1551
  148.2 20.6 %collective-permute-start.2 = (f32[512,384]{1,0:T(8,128)}, f32[512,384]{1,0:T(8,128)S(1)}, u32[]{:S(2)}, u32[]{:S(2)}) collective-permute-start(f32[512,384]{1,0:T(8,128)} %get-tuple-element.75), channel_id=1, source_target_pairs={{0,1},{1,0},{2,3},{3,2},{4,5},{5,4},{6,7},{7,6},{8,9},{9,8},{10,11... | collective-permute-start | bytes 2359304 | tf_op jit(solution)/shard_map/ppermute | solution.py:1539
  148.9 62.8 %collective-permute-start = (f32[512,384]{1,0:T(8,128)}, f32[512,384]{1,0:T(8,128)}, u32[]{:S(2)}, u32[]{:S(2)}) collective-permute-start(f32[512,384]{1,0:T(8,128)} %get-tuple-element.69), channel_id=1, source_target_pairs={{0,1},{1,0},{2,3},{3,2},{4,5},{5,4},{6,7},{7,6},{8,9},{9,8},{10,11... | collective-permute-start | bytes 2359304 | tf_op jit(solution)/shard_map/ppermute | solution.py:1539
  150.3 52.2 %collective-permute-start.1 = (f32[512,384]{1,0:T(8,128)}, f32[512,384]{1,0:T(8,128)S(1)}, u32[]{:S(2)}, u32[]{:S(2)}) collective-permute-start(f32[512,384]{1,0:T(8,128)} %get-tuple-element.72), channel_id=1, source_target_pairs={{0,1},{1,0},{2,3},{3,2},{4,5},{5,4},{6,7},{7,6},{8,9},{9,8},{10,11... | collective-permute-start | bytes 2359304 | tf_op jit(solution)/shard_map/ppermute | solution.py:1539
  155.3 13.5 %copy-start.11 = (s32[1,1024]{1,0:T(1,128)S(1)}, s32[1,1024]{1,0:T(1,128)}, u32[]{:S(2)}) copy-start(s32[1,1024]{1,0:T(1,128)} %param.13) | copy-start | bytes 12292
  160.1 16.6 %copy-start.17 = (f32[512,384]{1,0:T(8,128)}, f32[512,384]{1,0:T(8,128)S(1)}, u32[]{:S(2)}) copy-start(f32[512,384]{1,0:T(8,128)S(1)} %get-tuple-element.74.refs_0_) | copy-start | bytes 2359300
  160.1 42.4 %copy-start.21 = (f32[512,384]{1,0:T(8,128)}, f32[512,384]{1,0:T(8,128)S(1)}, u32[]{:S(2)}) copy-start(f32[512,384]{1,0:T(8,128)S(1)} %get-tuple-element.71.refs_0_) | copy-start | bytes 2359300
  160.1 51.6 %copy-start.23 = (f32[512,384]{1,0:T(8,128)}, f32[512,384]{1,0:T(8,128)S(1)}, u32[]{:S(2)}) copy-start(f32[512,384]{1,0:T(8,128)S(1)} %get-tuple-element.68.refs_0_) | copy-start | bytes 2359300
  169.0 42.7 %copy-start.4 = (s32[1024,128]{1,0:T(8,128)}, s32[1024,128]{1,0:T(8,128)S(1)}, u32[]{:S(2)}) copy-start(s32[1024,128]{1,0:T(8,128)S(1)} %broadcast_in_dim.15.refs_2_.refs_7_) | copy-start | bytes 1572868
  176.7 33.5 %copy-start.29 = (f32[512,128]{1,0:T(8,128)}, f32[512,128]{1,0:T(8,128)S(1)}, u32[]{:S(2)}) copy-start(f32[512,128]{1,0:T(8,128)S(1)} %get-tuple-element.79.refs_3_) | copy-start | bytes 786436
  176.7 33.5 %copy-start.35 = (f32[1024,128]{1,0:T(8,128)}, f32[1024,128]{1,0:T(8,128)S(1)}, u32[]{:S(2)}) copy-start(f32[1024,128]{1,0:T(8,128)S(1)} %get-tuple-element.106.refs_6_) | copy-start | bytes 1572868
  176.7 46.4 %collective-permute-start.5 = (f32[512,128]{1,0:T(8,128)S(1)}, f32[512,128]{1,0:T(8,128)S(1)}, u32[]{:S(2)}, u32[]{:S(2)}) collective-permute-start(f32[512,128]{1,0:T(8,128)S(1)} %get-tuple-element.79.refs_3_), channel_id=1, source_target_pairs={{0,1},{1,0},{2,3},{3,2},{4,5},{5,4},{6,7},{7,6},{8,9},{9,8},{10,11... | collective-permute-start | bytes 786440 | tf_op jit(solution)/shard_map/ppermute | solution.py:1542
  211.1 18.3 %copy-start.6 = (f32[512,128]{1,0:T(8,128)}, f32[512,128]{1,0:T(8,128)S(1)}, u32[]{:S(2)}) copy-start(f32[512,128]{1,0:T(8,128)S(1)} %get-tuple-element.73.refs_1_.refs_2_) | copy-start | bytes 786436
  211.1 12.1 %collective-permute-start.4 = (f32[512,128]{1,0:T(8,128)S(1)}, f32[512,128]{1,0:T(8,128)S(1)}, u32[]{:S(2)}, u32[]{:S(2)}) collective-permute-start(f32[512,128]{1,0:T(8,128)S(1)} %get-tuple-element.78.refs_3_), channel_id=1, source_target_pairs={{0,1},{1,0},{2,3},{3,2},{4,5},{5,4},{6,7},{7,6},{8,9},{9,8},{10,11... | collective-permute-start | bytes 786440 | tf_op jit(solution)/shard_map/ppermute | solution.py:1542
  211.7 17.7 %copy-start.2 = (f32[1,512,768]{2,1,0:T(8,128)S(1)}, f32[1,512,768]{2,1,0:T(8,128)}, u32[]{:S(2)}) copy-start(f32[1,512,768]{2,1,0:T(8,128)} %param.23) | copy-start | bytes 4718596
  211.7 17.7 %copy-start.3 = (f32[512,768]{1,0:T(8,128)S(1)}, f32[512,768]{1,0:T(8,128)}, u32[]{:S(2)}) copy-start(f32[512,768]{1,0:T(8,128)} %get-tuple-element.80.refs_6_.refs_13_) | copy-start | bytes 4718596
  211.7 17.7 %copy-start.10 = (f32[8,768]{1,0:T(8,128)S(1)}, f32[8,768]{1,0:T(8,128)}, u32[]{:S(2)}) copy-start(f32[8,768]{1,0:T(8,128)} %get-tuple-element.82.refs_9_.refs_7_.refs_15_) | copy-start | bytes 73732
  221.0 8.4 %collective-permute-start.3 = (f32[512,128]{1,0:T(8,128)S(1)}, f32[512,128]{1,0:T(8,128)S(1)}, u32[]{:S(2)}, u32[]{:S(2)}) collective-permute-start(f32[512,128]{1,0:T(8,128)S(1)} %get-tuple-element.77.refs_3_), channel_id=1, source_target_pairs={{0,1},{1,0},{2,3},{3,2},{4,5},{5,4},{6,7},{7,6},{8,9},{9,8},{10,11... | collective-permute-start | bytes 786440 | tf_op jit(solution)/shard_map/ppermute | solution.py:1542
  303.9 9.4 %collective-permute-start.6 = (f32[512,128]{1,0:T(8,128)}, f32[512,128]{1,0:T(8,128)S(1)}, u32[]{:S(2)}, u32[]{:S(2)}) collective-permute-start(f32[512,128]{1,0:T(8,128)} %get-tuple-element.97), channel_id=1, source_target_pairs={{0,1},{1,0},{2,3},{3,2},{4,5},{5,4},{6,7},{7,6},{8,9},{9,8},{10,11... | collective-permute-start | bytes 786440 | tf_op jit(solution)/shard_map/ppermute | solution.py:1554
  305.5 21.6 %collective-permute-start.7 = (f32[512,128]{1,0:T(8,128)S(1)}, f32[512,128]{1,0:T(8,128)S(1)}, u32[]{:S(2)}, u32[]{:S(2)}) collective-permute-start(f32[512,128]{1,0:T(8,128)S(1)} %copy-done.55), channel_id=1, source_target_pairs={{0,1},{1,0},{2,3},{3,2},{4,5},{5,4},{6,7},{7,6},{8,9},{9,8},{10,11... | collective-permute-start | bytes 786440 | tf_op jit(solution)/shard_map/ppermute | solution.py:1554
  306.3 31.3 %collective-permute-start.8 = (f32[512,128]{1,0:T(8,128)S(1)}, f32[512,128]{1,0:T(8,128)S(1)}, u32[]{:S(2)}, u32[]{:S(2)}) collective-permute-start(f32[512,128]{1,0:T(8,128)S(1)} %copy-done.54), channel_id=1, source_target_pairs={{0,1},{1,0},{2,3},{3,2},{4,5},{5,4},{6,7},{7,6},{8,9},{9,8},{10,11... | collective-permute-start | bytes 786440 | tf_op jit(solution)/shard_map/ppermute | solution.py:1554
  314.5 12.6 %copy-start.7 = (f32[512,128]{1,0:T(8,128)S(1)}, f32[512,128]{1,0:T(8,128)}, u32[]{:S(2)}) copy-start(f32[512,128]{1,0:T(8,128)} %copy-done.6) | copy-start | bytes 786436
  314.5 12.6 %copy-start.20 = (f32[512,384]{1,0:T(8,128)S(1)}, f32[512,384]{1,0:T(8,128)}, u32[]{:S(2)}) copy-start(f32[512,384]{1,0:T(8,128)} %copy-done.19) | copy-start | bytes 2359300
  314.5 12.6 %copy-start.22 = (f32[512,384]{1,0:T(8,128)S(1)}, f32[512,384]{1,0:T(8,128)}, u32[]{:S(2)}) copy-start(f32[512,384]{1,0:T(8,128)} %copy-done.21) | copy-start | bytes 2359300
  314.5 12.7 %copy-start.32 = (f32[512,128]{1,0:T(8,128)S(1)}, f32[512,128]{1,0:T(8,128)}, u32[]{:S(2)}) copy-start(f32[512,128]{1,0:T(8,128)} %copy-done.31) | copy-start | bytes 786436
  314.5 12.7 %copy-start.38 = (f32[1024,128]{1,0:T(8,128)S(1)}, f32[1024,128]{1,0:T(8,128)}, u32[]{:S(2)}) copy-start(f32[1024,128]{1,0:T(8,128)} %copy-done.37) | copy-start | bytes 1572868
  314.5 12.7 %copy-start.42 = (f32[512,128]{1,0:T(8,128)S(1)}, f32[512,128]{1,0:T(8,128)}, u32[]{:S(2)}) copy-start(f32[512,128]{1,0:T(8,128)} %get-tuple-element.100.refs_4_) | copy-start | bytes 786436
  325.6 22.4 %collective-permute-start.9 = (f32[512,384]{1,0:T(8,128)}, f32[512,384]{1,0:T(8,128)}, u32[]{:S(2)}, u32[]{:S(2)}) collective-permute-start(f32[512,384]{1,0:T(8,128)} %get-tuple-element.108), channel_id=1, source_target_pairs={{0,1},{1,0},{2,3},{3,2},{4,5},{5,4},{6,7},{7,6},{8,9},{9,8},{10,11... | collective-permute-start | bytes 2359304 | tf_op jit(solution)/shard_map/ppermute | solution.py:1561
  327.2 10.4 %copy-start.16 = (f32[512,384]{1,0:T(8,128)S(1)}, f32[512,384]{1,0:T(8,128)}, u32[]{:S(2)}) copy-start(f32[512,384]{1,0:T(8,128)} %copy-done.15) | copy-start | bytes 2359300
  575.1 13.1 %collective-permute-start.10 = (f32[192,768]{1,0:T(8,128)}, f32[192,768]{1,0:T(8,128)S(1)}, u32[]{:S(2)}, u32[]{:S(2)}) collective-permute-start(f32[192,768]{1,0:T(8,128)} %reduce-scatter.2.cloned.1.call-done), channel_id=1, source_target_pairs={{0,1},{1,0},{2,3},{3,2},{4,5},{5,4},{6,7},{7,6},{8,9},{9,8},{10,11... | collective-permute-start | bytes 1769480 | tf_op jit(solution)/shard_map/ppermute | solution.py:1568
  575.8 12.4 %copy-start.45 = (f32[192,768]{1,0:T(8,128)S(1)}, f32[192,768]{1,0:T(8,128)}, u32[]{:S(2)}) copy-start(f32[192,768]{1,0:T(8,128)} %reduce-scatter.2.cloned.1.call-done) | copy-start | bytes 1769476
  (37 other events, 152.2 us)
Sparse Core Ops, SparseCore 0:
  148.0 103.4 all-gather.1
  304.1 146.9 reduce-scatter.1
